TPU v7x, 32 devices: a whole 2x2x4 slice. The times are simulated.
32 devices in a mesh: src: 8 (over z, y), rcv: 2 (over x), freq: 2 (over core).
Axes of the slice: x: 2, y: 2, z: 4, core: 2. Of those that a mesh axis runs over, the one named last changes fastest.
Arguments:
- recorded: float32 [2, 2, 4096, 4096], P('freq', None, 'src', 'rcv'), parts along dimension 0, as said below
Outputs:
- multiples: float32 [2, 2, 4096, 4096], P('freq', None, 'src', 'rcv'), parts along dimension 0
There are 2 independent parts, one for each index of `freq`. A program takes and returns all parts, laid end to end along the dimension named above; each array names one. Nothing has to cross between parts.
Inputs may be any that keep to these rules, and one draw needn't show every extreme that they name: By reciprocity each frequency bin's data is symmetric: recorded[f, c, s, r] equals recorded[f, c, r, s].
All inputs are finite; a program needn't handle non-finite values.
Results may differ from a plain program's by a relative error of at most 0.00007.
Values sent between devices are 32-bit elements; how exact they have to be, the bound alone decides.
No kernel may reach another device: no remote copies, remote signals or barrier semaphores. Data moves between devices by JAX's collectives and lax.ppermute only.
A program may use at most 192 MiB of HBM per device.

v0:
```python
import jax
import jax.numpy as jnp
from jax import lax
from jax.sharding import PartitionSpec as P


def complex_product(left, right, form):
    highest = lax.Precision.HIGHEST

    def multiply(first, second):
        return jnp.einsum(form, first, second, precision=highest)

    real_part = multiply(left[:, 0], right[:, 0]) - multiply(left[:, 1], right[:, 1])
    imag_part = multiply(left[:, 0], right[:, 1]) + multiply(left[:, 1], right[:, 0])
    return jnp.stack([real_part, imag_part], axis=1)


def local(recorded):
    rows_full = lax.all_gather(recorded, "rcv", axis=3, tiled=True)
    return complex_product(
        rows_full, lax.all_gather(recorded, "src", axis=2, tiled=True), "fik,fkj->fij"
    )


def solution(mesh):
    return jax.shard_map(
        local,
        mesh=mesh,
        in_specs=(P("freq", None, "src", "rcv"),),
        out_specs=P("freq", None, "src", "rcv"),
        check_vma=False,
    )
```

profile of v0, /device:TPU:6, one launch (start us, length us, event | category | flops | bytes accessed | tf_op | source)
XLA Modules:
  0.0 1733.5 jit_solution(8596552578259312416)
XLA Ops:
  6.5 0.0 all-gather.3.cloned.1.call-start
  6.5 0.7 all-gather.3.cloned.1.call-update
  7.3 0.0 all-gather.5.cloned.1.call-start
  7.3 0.7 all-gather.5.cloned.1.call-update
  8.0 200.1 %all-gather.3.cloned.1.call-done = f32[1,2,512,4096]{3,2,1,0:T(8,128)} async-done(((f32[1,2,512,2048]{3,2,1,0:T(8,128)}), f32[1,2,512,4096]{3,2,1,0:T(8,128)}) %all-gather.3.cloned.1.call-update) | async-done | bytes 16777232 | tf_op jit(solution)/shard_map/all_gather | solution.py:19
  208.1 1268.5 %all-gather.5.cloned.1.call-done = f32[1,2,4096,2048]{3,2,1,0:T(8,128)} async-done(((f32[1,2,512,2048]{3,2,1,0:T(8,128)}), f32[1,2,4096,2048]{3,2,1,0:T(8,128)}) %all-gather.5.cloned.1.call-update) | async-done | bytes 67108880 | tf_op jit(solution)/shard_map/all_gather | solution.py:21
  1476.6 0.0 copy-start
  1476.6 59.6 %fusion = f32[512,2048]{1,0:T(8,128)S(1)} fusion(f32[1,2,4096,2048]{3,2,1,0:T(8,128)} %all-gather.5.cloned.1.call-done, f32[1,2,512,4096]{3,2,1,0:T(8,128)} %all-gather.3.cloned.1.call-done), kind=kOutput, calls=%fused_computation.2 | convolution fusion | flops 51539607552 | bytes 46137344 | tf_op jit(solution)/shard_map/fik,fkj->fij/dot_general | solution.py:11
  1536.2 0.0 copy-done
  1536.2 57.0 %fusion.1 = f32[512,2048]{1,0:T(8,128)} fusion(f32[1,2,4096,2048]{3,2,1,0:T(8,128)} %all-gather.5.cloned.1.call-done, f32[1,2,512,4096]{3,2,1,0:T(8,128)S(1)} %copy-done), kind=kOutput, calls=%fused_computation.3 | convolution fusion | flops 51539607552 | bytes 46137344 | tf_op jit(solution)/shard_map/fik,fkj->fij/dot_general | solution.py:11
  1593.2 60.4 %add_bitcast_fusion = f32[1,1,512,2048]{3,2,1,0:T(8,128)S(1)} fusion(f32[512,2048]{1,0:T(8,128)S(1)} %fusion, f32[1,2,4096,2048]{3,2,1,0:T(8,128)} %all-gather.5.cloned.1.call-done, f32[1,2,512,4096]{3,2,1,0:T(8,128)} %all-gather.3.cloned.1.call-done), kind=kOutput, calls=%fused_computation.9 | convolution fusion | flops 51540656128 | bytes 50331648 | tf_op jit(solution)/shard_map/fik,fkj->fij/dot_general | solution.py:11
  1653.6 68.2 %subtract_bitcast_fusion = f32[1,1,512,2048]{3,2,1,0:T(8,128)S(1)} fusion(f32[512,2048]{1,0:T(8,128)} %fusion.1, f32[1,2,4096,2048]{3,2,1,0:T(8,128)} %all-gather.5.cloned.1.call-done, f32[1,2,512,4096]{3,2,1,0:T(8,128)} %all-gather.3.cloned.1.call-done), kind=kOutput, calls=%fused_computation.10 | convolution fusion | flops 51540656128 | bytes 50331648 | tf_op jit(solution)/shard_map/fik,fkj->fij/dot_general | solution.py:11
  1721.8 4.4 pad_maximum_fusion
Async XLA Ops:
  6.5 201.5 %all-gather.3.cloned.1.call-start = ((), (), s32[]{:S(2)}) async-start(), calls=%async_computation | async-start | bytes 25165824 | tf_op jit(solution)/shard_map/all_gather | solution.py:19
  7.3 1469.3 %all-gather.5.cloned.1.call-start = ((), (), s32[]{:S(2)}) async-start(), calls=%async_computation.1 | async-start | bytes 75497472 | tf_op jit(solution)/shard_map/all_gather | solution.py:21
  1476.6 59.6 %copy-start = (f32[1,2,512,4096]{3,2,1,0:T(8,128)S(1)}, f32[1,2,512,4096]{3,2,1,0:T(8,128)}, u32[]{:S(2)}) copy-start(f32[1,2,512,4096]{3,2,1,0:T(8,128)} %all-gather.3.cloned.1.call-done) | copy-start | bytes 50331652
Sparse Core Ops, SparseCore 0:
  8.9 199.1 all-gather.2
  209.6 1266.9 all-gather.4
where the time goes:
time: 1740 us; the launch traced here: 1730 us
  waiting for transfers between devices  1470 us (84%)
  matrix products  245 us (14%)
    all_gather x1, waiting for transfers between devices, local(): lax.all_gather(recorded, 'src', axis=2, tiled=True)  1270 us
    dot_general x4, matrix products, multiply(): return jnp.einsum(form, first, second, precision=highest)  245 us
    all_gather x1, waiting for transfers between devices, local(): rows_full = lax.all_gather(recorded, 'rcv', axis=3, tiled=True)  200 us
  transfers between devices with their start and end apart: 2, of which 2 were waited for; matrix products, arithmetic and copies ran while one was open for 0% of the time, Pallas kernels for 0%

commit v1 on v0

v1 whole, which is shorter than its diff:
```python
import functools
import random

import jax
import jax.numpy as jnp
import numpy as np
from jax import lax
from jax.experimental import pallas as pl
from jax.experimental.pallas import tpu as pltpu
from jax.sharding import PartitionSpec as P

AXES = ("src", "rcv")


def split_axis(n):
    return (n,) if n <= 4 else (4, n // 4)


class Grid:
    def __init__(self, src, rcv):
        self.src, self.rcv, self.width = src, rcv, src // rcv
        dims = split_axis(src) + split_axis(rcv)
        self.count = src * rcv
        place = np.array(np.unravel_index(np.arange(self.count), dims)).T
        self.dist = np.abs(place[:, None] - place[None]).sum(-1)
        self.ways = []
        for axis, size in enumerate(dims):
            for sign in (1, -1) if size > 2 else (0,):
                pairs = []
                for u in range(self.count):
                    to = place[u].copy()
                    to[axis] = 1 - to[axis] if sign == 0 else to[axis] + sign
                    if 0 <= to[axis] < size:
                        pairs.append((u, int(np.ravel_multi_index(tuple(to), dims))))
                if pairs:
                    self.ways.append(pairs)
        self.tiles = [(p, q) for p in range(src) for q in range(p, src)]
        self.number = {}
        for i, (p, q) in enumerate(self.tiles):
            self.number[p, q] = self.number[q, p] = i

    def columns(self, x):
        return range(x * self.width, (x + 1) * self.width)


def plan_moves(grid, seed):
    rnd = random.Random(seed)
    items, n = 2 * len(grid.tiles), grid.count
    has = np.full((n, items), 10**6)
    need = np.zeros((n, items), bool)
    row = np.zeros((n, items), bool)
    flip = np.zeros((n, items), bool)
    for d in range(n):
        s, x = divmod(d, grid.rcv)
        for c in range(2):
            for q in range(grid.src):
                need[d, 2 * grid.number[s, q] + c] = True
                row[d, 2 * grid.number[s, q] + c] = True
                for j in grid.columns(x):
                    need[d, 2 * grid.number[q, j] + c] = True
            for q in grid.columns(x):
                has[d, 2 * grid.number[s, q] + c] = 0
                flip[d, 2 * grid.number[s, q] + c] = s > q
    links = [(way, u, v) for way, pairs in enumerate(grid.ways) for u, v in pairs]
    degree = np.zeros(n)
    for _, _, v in links:
        degree[v] += 1
    near = np.stack([grid.dist[has[:, i] == 0].min(0) for i in range(items)])
    moves, step = [], 0
    while True:
        missing = need & (has > 10**5)
        if not missing.any():
            return moves, has, flip
        load = missing.sum(1) / degree
        weight = missing.sum(1) / np.maximum(need.sum(1), 1)
        rnd.shuffle(links)
        links.sort(key=lambda link: -load[link[2]])
        open_ = has > 10**5
        into = [[] for _ in range(n)]
        for _, u, v in links:
            into[v].append(u)
        ready = has <= step
        now = []
        for way, u, v in links:
            cand = np.nonzero(ready[u] & open_[v])[0]
            if not len(cand):
                continue
            helped = (missing[:, cand].T & (grid.dist[v][None] < near[cand])).astype(float)
            helped[:, v] = 0
            value = 3.0 * missing[v, cand] + helped @ weight
            useful = value > 0
            if not useful.any():
                continue
            others = sum(ready[w, cand].astype(float) for w in into[v])
            value = value + 0.5 * np.array([rnd.random() for _ in cand]) - 0.7 * (others - 1)
            value = value + 0.6 * (row[v, cand] & missing[v, cand])
            value[~useful] = -100
            item = int(cand[np.argmax(value)])
            open_[v, item] = False
            missing[v, item] = False
            near[item] = np.minimum(near[item], grid.dist[v])
            now.append((way, u, v, item))
        for _, u, v, item in now:
            has[v, item] = step + 2
            flip[v, item] = flip[u, item]
        moves.append(now)
        step += 1


@functools.lru_cache(None)
def plan(src, rcv):
    grid = Grid(src, rcv)
    best = None
    for seed in range(24 if grid.count <= 16 else 1):
        got = plan_moves(grid, seed)
        if best is None or len(got[0]) < len(best[0]):
            best = got
    moves, has, flip = best
    n, ways, steps = grid.count, len(grid.ways), len(moves)
    slot = np.full((n, 2 * len(grid.tiles)), -1)
    used = np.zeros(n, int)
    for d in range(n):
        s, x = divmod(d, rcv)
        for q in grid.columns(x):
            for c in range(2):
                slot[d, 2 * grid.number[s, q] + c] = used[d]
                used[d] += 1
    send = np.full((steps + 2, ways, n), -1)
    take = np.full((steps + 2, ways, n), -1)
    perms = [[[] for _ in range(ways)] for _ in range(steps)]
    for step, now in enumerate(moves):
        for way, u, v, item in now:
            slot[v, item] = used[v]
            used[v] += 1
            take[step + 2, way, v] = slot[v, item]
            perms[step][way].append((u, v))
    for step, now in enumerate(moves):
        taken = [way for way in range(ways) if step >= 2 and perms[step - 2][way]]
        for way, u, v, item in now:
            new = [i for i, w in enumerate(taken) if take[step, w, u] == slot[u, item]]
            send[step, way, u] = used.max() + new[0] if new else slot[u, item]
    calls = sorted({*range(4, steps, 2), *range(max(steps - 3, 0), steps + 2)})
    cap = 10
    lists = [[[] for _ in range(n)] for _ in calls]
    for d in range(n):
        s, x = divmod(d, rcv)
        todo = []
        for k in range(src):
            left = [2 * grid.number[s, k] + c for c in range(2)]
            for j, q in enumerate(grid.columns(x)):
                for c in range(2):
                    right = 2 * grid.number[k, q] + c
                    ready = max(has[d, left[0]], has[d, left[1]], has[d, right])
                    todo.append((ready, k, j, c, left, right, q))
        todo.sort()
        for at, step in enumerate(calls):
            fit = [one for one in todo if one[0] <= step]
            if step < steps + 1:
                fit = fit[:cap]
            todo = [one for one in todo if one not in fit]
            fit.sort(key=lambda one: one[1])
            old = None
            for ready, k, j, c, left, right, q in fit:
                lt = [int((s > k) != flip[d, i]) for i in left]
                rt = int((k > q) != flip[d, right])
                lists[at][d].append(
                    (slot[d, left[0]], slot[d, left[1]], lt[0], lt[1], int(k != old), slot[d, right], rt, j, c)
                )
                old = k
        assert not todo
    longest = [max(len(one) for one in per) for per in lists]
    table = []
    starts = {}
    for step in range(steps + 2):
        starts["route", step] = len(table)
        for way in range(ways):
            table.append(take[step, way])
        for way in range(ways):
            table.append(send[step, way])
    for at, step in enumerate(calls):
        starts["ops", step] = len(table)
        table.append(np.array([len(lists[at][d]) for d in range(n)]))
        for i in range(longest[at]):
            for f in range(9):
                table.append(np.array([lists[at][d][i][f] if i < len(lists[at][d]) else 0 for d in range(n)]))
    return perms, calls, longest, starts, np.array(table, np.int32).T.copy(), int(used.max()), ways


ANY = pl.BlockSpec(memory_space=pl.ANY)


def first_kernel(tab, own, buf, hold, sem):
    tile = buf.shape[-1]
    width = own.shape[-1] // tile
    pairs = [(q, c) for q in range(width) for c in range(2)]
    loads = [
        pltpu.make_async_copy(own.at[0, c, :, pl.ds(q * tile, tile)], hold.at[i], sem.at[i])
        for i, (q, c) in enumerate(pairs)
    ]
    stores = [pltpu.make_async_copy(hold.at[i], buf.at[i], sem.at[i]) for i in range(len(pairs))]
    for load in loads:
        load.start()
    for load, store in zip(loads, stores):
        load.wait()
        store.start()
    for store in stores:
        store.wait()


def route_kernel(start, ways, taken, sent, slots, tab, *refs):
    got = refs[2 : 2 + len(taken)]
    buf = refs[2 + len(taken)]
    outs = refs[4 + len(taken) : 4 + len(taken) + len(sent)]
    hold_in, hold_out, sem_in, sem_out = refs[-4:]

    def load_in(i):
        return pltpu.make_async_copy(got[i], hold_in.at[i], sem_in.at[i])

    def load_out(i, slot):
        return pltpu.make_async_copy(buf.at[slot], hold_out.at[i], sem_out.at[i])

    def store_in(i, slot):
        return pltpu.make_async_copy(hold_in.at[i], buf.at[slot], sem_in.at[i])

    def store_out(i):
        return pltpu.make_async_copy(hold_out.at[i], outs[i], sem_out.at[i])

    def pass_on(i, at):
        return pltpu.make_async_copy(hold_in.at[at], outs[i], sem_out.at[i])

    to = [tab[start + way] for way in taken]
    of = [tab[start + ways + way] for way in sent]
    for i, slot in enumerate(of):
        pl.when((slot >= 0) & (slot < slots))(lambda: load_out(i, slot).start())
    for i, slot in enumerate(to):
        pl.when(slot >= 0)(lambda: load_in(i).start())
    for i, slot in enumerate(of):
        @pl.when((slot >= 0) & (slot < slots))
        def _():
            load_out(i, slot).wait()
            store_out(i).start()
    for i, slot in enumerate(to):
        @pl.when(slot >= 0)
        def _():
            load_in(i).wait()
            store_in(i, slot).start()
    if taken:
        for i, slot in enumerate(of):
            pl.when(slot >= slots)(lambda: pass_on(i, slot - slots).start())
        for i, slot in enumerate(of):
            pl.when(slot >= slots)(lambda: pass_on(i, slot - slots).wait())
    for i, slot in enumerate(of):
        pl.when((slot >= 0) & (slot < slots))(lambda: store_out(i).wait())
    for i, slot in enumerate(to):
        pl.when(slot >= 0)(lambda: store_in(i, slot).wait())


def split(value):
    high = value.astype(jnp.bfloat16)
    return high, (value - high.astype(jnp.float32)).astype(jnp.bfloat16)


def multiply_kernel(start, first, tab, buf, *refs):
    if first:
        out, *scratch = refs
        acc_in = None
    else:
        acc_in, out, *scratch = refs
    acc, left, right, lcat, rcat, nt, sem_acc, sem_l, sem_r = scratch
    tile = buf.shape[-1]
    width = acc.shape[1]
    rows = min(256, tile)
    count = tab[start]

    def field(i, f):
        return tab[start + 1 + 9 * i + f]

    def acc_copies(ref, back):
        for c in range(2):
            for j in range(width):
                there, here = ref.at[0, c, :, pl.ds(j * tile, tile)], acc.at[c, j]
                pair = (here, there) if back else (there, here)
                yield pltpu.make_async_copy(*pair, sem_acc.at[c * width + j])

    def fetch_left(i, c):
        return pltpu.make_async_copy(buf.at[field(i, c)], left.at[c], sem_l.at[c])

    def fetch_right(i):
        return pltpu.make_async_copy(buf.at[field(i, 5)], right.at[lax.rem(i, 2)], sem_r.at[lax.rem(i, 2)])

    def fetch(i):
        fetch_right(i).start()

        @pl.when(field(i, 4) == 1)
        def _():
            fetch_left(i, 0).start()
            fetch_left(i, 1).start()

    @pl.when(count > 0)
    def _():
        fetch(0)

    if first:
        acc[...] = jnp.zeros_like(acc)
    else:
        for copy in acc_copies(acc_in, False):
            copy.start()
        for copy in acc_copies(acc_in, False):
            copy.wait()

    def op(i, carry):
        now = lax.rem(i, 2)
        fetch_right(i).wait()

        @pl.when(field(i, 4) == 1)
        def _():
            fetch_left(i, 0).wait()
            fetch_left(i, 1).wait()
            for c in range(2):
                @pl.when(field(i, 2 + c) == 1)
                def _():
                    left[c] = left[c].T

            def cut(r, carry):
                at = pl.ds(pl.multiple_of(r * rows, rows), rows)
                for c in range(2):
                    high, low = split(left[c, at, :])
                    lcat[c, at, 0:tile] = high
                    lcat[c, at, tile : 2 * tile] = high
                    lcat[c, at, 2 * tile :] = low
                return carry

            lax.fori_loop(0, tile // rows, cut, 0)

        @pl.when(i + 1 < count)
        def _():
            fetch(i + 1)

        j, c, turned = field(i, 7), field(i, 8), field(i, 6)

        def cut(r, carry):
            at = pl.ds(pl.multiple_of(r * rows, rows), rows)
            high, low = split(right[now, at, :])
            rcat[0, at, :] = high
            rcat[1, at, :] = low
            rcat[2, at, :] = high
            return carry

        lax.fori_loop(0, tile // rows, cut, 0)

        def product(turn):
            def part(r, carry):
                cl, half = r // (tile // rows), lax.rem(r, tile // rows)
                at = pl.ds(pl.multiple_of(half * rows, rows), rows)
                contract = ((1,), (1,)) if turn else ((1,), (0,))
                if turn:
                    total = sum(
                        lax.dot_general(
                            lcat[cl, at, m * tile : (m + 1) * tile],
                            rcat[m],
                            (contract, ((), ())),
                            preferred_element_type=jnp.float32,
                        )
                        for m in range(3)
                    )
                else:
                    total = jnp.dot(
                        lcat[cl, at, :],
                        rcat[...].reshape(3 * tile, tile),
                        preferred_element_type=jnp.float32,
                    )
                both = c * cl
                to = c + cl - 2 * both
                sign = (1 - 2 * both).astype(jnp.float32)
                acc[to, j, at, :] += sign * total
                return carry

            lax.fori_loop(0, 2 * (tile // rows), part, 0)

        @pl.when(turned == 0)
        def _():
            product(False)

        @pl.when(turned == 1)
        def _():
            product(True)

        return carry

    lax.fori_loop(0, count, op, 0)
    for copy in acc_copies(out, True):
        copy.start()
    for copy in acc_copies(out, True):
        copy.wait()


def local(src, rcv, recorded):
    perms, calls, longest, starts, table, slots, ways = plan(src, rcv)
    steps = len(perms)
    tile = recorded.shape[2]
    me = lax.axis_index("src") * rcv + lax.axis_index("rcv")
    tab = lax.dynamic_index_in_dim(jnp.asarray(table), me, 0, keepdims=False)
    chunk = jax.ShapeDtypeStruct((tile, tile), jnp.float32)
    buf_shape = jax.ShapeDtypeStruct((slots, tile, tile), jnp.float32)
    width = recorded.shape[3] // tile

    def call(kernel, ins, outs, scratch, aliases, cost, limit=None):
        return pl.pallas_call(
            kernel,
            out_shape=outs,
            grid_spec=pltpu.PrefetchScalarGridSpec(
                num_scalar_prefetch=1,
                grid=(),
                in_specs=[ANY] * len(ins),
                out_specs=[ANY] * len(outs),
                scratch_shapes=scratch,
            ),
            input_output_aliases=aliases,
            cost_estimate=pl.CostEstimate(flops=cost[0], bytes_accessed=cost[1], transcendentals=0),
            compiler_params=pltpu.CompilerParams(vmem_limit_bytes=limit),
        )(tab, *ins)

    size = tile * tile * 4
    (buf,) = call(
        first_kernel, [recorded], [buf_shape],
        [pltpu.VMEM((2 * width, tile, tile), jnp.float32), pltpu.SemaphoreType.DMA((2 * width,))],
        {}, (0, 4 * width * size), 48 << 20,
    )
    acc = None
    flight = {}
    for step in range(steps + 2):
        got = flight.pop(step - 2, {})
        taken = sorted(got)
        sent = [way for way in range(ways) if step < steps and perms[step][way]]
        ins = [buf, recorded if acc is None else acc] + [got[way] for way in taken]
        outs = [buf_shape, jax.ShapeDtypeStruct(recorded.shape, jnp.float32)] + [chunk] * len(sent)
        aliases = {1: 0} if acc is None else {1: 0, 2: 1}
        if acc is None:
            ins.pop(1)
            outs.pop(1)
            kernel = functools.partial(first_route, starts["route", step], ways, taken, sent, slots)
        else:
            kernel = functools.partial(route_kernel, starts["route", step], ways, taken, sent, slots)
        done = call(
            kernel,
            ins,
            outs,
            [
                pltpu.VMEM((max(len(taken), 1), tile, tile), jnp.float32),
                pltpu.VMEM((max(len(sent), 1), tile, tile), jnp.float32),
                pltpu.SemaphoreType.DMA((max(len(taken), 1),)),
                pltpu.SemaphoreType.DMA((max(len(sent), 1),)),
            ],
            aliases,
            (0, 2 * (len(taken) + len(sent)) * size),
            24 << 20,
        )
        if acc is None:
            buf, *out = done
        else:
            buf, acc, *out = done
        flight[step] = {
            way: lax.ppermute(value, AXES, perms[step][way]) for way, value in zip(sent, out)
        }
        if step in calls:
            ops = longest[calls.index(step)]
            first = acc is None
            scratch = [
                pltpu.VMEM((2, width, tile, tile), jnp.float32),
                pltpu.VMEM((2, tile, tile), jnp.float32),
                pltpu.VMEM((2, tile, tile), jnp.float32),
                pltpu.VMEM((2, tile, 3 * tile), jnp.bfloat16),
                pltpu.VMEM((3, tile, tile), jnp.bfloat16),
                pltpu.SMEM((1,), jnp.int32),
                pltpu.SemaphoreType.DMA((2 * width,)),
                pltpu.SemaphoreType.DMA((2,)),
                pltpu.SemaphoreType.DMA((2,)),
            ]
            (acc,) = call(
                functools.partial(multiply_kernel, starts["ops", step], first),
                [buf] if first else [buf, acc],
                [jax.ShapeDtypeStruct(recorded.shape, jnp.float32)],
                scratch,
                {} if first else {2: 0},
                (ops * 12 * tile**3, ops * 3 * size + 4 * width * size),
                48 << 20,
            )
    return acc


def first_route(start, ways, taken, sent, slots, tab, *refs):
    buf, rest = refs[0], refs[1:]
    got, rest = rest[: len(taken)], rest[len(taken) :]
    route_kernel(start, ways, taken, sent, slots, tab, buf, None, *got, rest[0], None, *rest[1:])


def solution(mesh):
    src, rcv = mesh.shape["src"], mesh.shape["rcv"]
    return jax.shard_map(
        functools.partial(local, src, rcv),
        mesh=mesh,
        in_specs=(P("freq", None, "src", "rcv"),),
        out_specs=P("freq", None, "src", "rcv"),
        check_vma=False,
    )
```

time: 1740 us -> 621 us (0.36)
  waiting for transfers between devices: 1470 us -> 85.9 us
  Pallas kernels: 0 us -> 349 us
  matrix products: 245 us -> 0 us
  starting transfers between devices: 0.04 us -> 176 us
    all_gather x2 -> x0, waiting for transfers between devices: 1470 us -> none  [the longest x1 1270 us: local(): lax.all_gather(recorded, 'src', axis=2, tiled=True)]
    pallas_call x0 -> x32, Pallas kernels: none -> 349 us  [call(): pl.pallas_call(kernel, out_shape=outs, grid_spec=pltpu.PrefetchScalarGrid...]
    dot_general x4 -> x0, matrix products: 245 us -> none  [multiply(): return jnp.einsum(form, first, second, precision=highest)]
    ppermute x0 -> x71, starting transfers between devices: none -> 176 us  [local(): lax.ppermute(value, AXES, perms[step][way])]
    ppermute x0 -> x71, waiting for transfers between devices: none -> 85.9 us  [local(): lax.ppermute(value, AXES, perms[step][way])]
  transfers between devices with their start and end apart: 2 -> 71, of which waited for: 2 -> 20; matrix products, arithmetic and copies ran while one was open for 0% -> 0% of each run, Pallas kernels for 0% -> 53%
where the time goes in v1:
time: 621 us; the launch traced here: 613 us
  Pallas kernels  349 us (56%)
  starting transfers between devices  176 us (28%)
  waiting for transfers between devices  85.9 us (14%)
    pallas_call x32, Pallas kernels, call(): pl.pallas_call(kernel, out_shape=outs, grid_spec=pltpu.PrefetchScalarGrid...  349 us
    ppermute x71, starting transfers between devices, local(): lax.ppermute(value, AXES, perms[step][way])  176 us
    ppermute x71, waiting for transfers between devices, local(): lax.ppermute(value, AXES, perms[step][way])  85.9 us
  transfers between devices with their start and end apart: 71, of which 20 were waited for; matrix products, arithmetic and copies ran while one was open for 0% of the time, Pallas kernels for 53%

profile of v1, /device:TPU:6, one launch (start us, length us, event | category | flops | bytes accessed | tf_op | source)
XLA Modules:
  0.0 612.9 jit_solution(3754718781078110628)
XLA Ops:
  0.8 7.1 %shard_map.28.refs_0_ = f32[60,512,512]{2,1,0:T(8,128)} custom-call(s32[936]{0:T(1024)S(1)} %bitcast.1, f32[1,2,512,2048]{3,2,1,0:T(8,128)} %own.1), custom_call_target="tpu_custom_call" | custom-call | bytes 16777216 | tf_op jit(solution)/shard_map/pallas_call | solution.py:408
  7.9 2.6 shard_map.29
  10.5 3.9 collective-permute-start
  16.7 2.6 shard_map.30
  19.3 5.1 collective-permute-start.4
  24.5 13.4 %collective-permute-done.refs_1_ = f32[512,512]{1,0:T(8,128)S(1)} collective-permute-done((f32[512,512]{1,0:T(8,128)S(1)}, f32[512,512]{1,0:T(8,128)S(1)}, u32[]{:S(2)}, u32[]{:S(2)}) %collective-permute-start) | collective-permute-done | bytes 1048608 | tf_op jit(solution)/shard_map/ppermute | solution.py:463
  41.9 4.3 shard_map.31
  46.2 4.4 collective-permute-start.8
  50.6 9.8 %collective-permute-done.4.refs_1_ = f32[512,512]{1,0:T(8,128)S(1)} collective-permute-done((f32[512,512]{1,0:T(8,128)S(1)}, f32[512,512]{1,0:T(8,128)S(1)}, u32[]{:S(2)}, u32[]{:S(2)}) %collective-permute-start.4) | collective-permute-done | bytes 1048608 | tf_op jit(solution)/shard_map/ppermute | solution.py:463
  63.9 2.1 collective-permute-done.6.refs_3_
  66.7 4.3 shard_map.32
  71.0 3.5 collective-permute-start.12
  74.5 8.3 %collective-permute-done.8.refs_1_ = f32[512,512]{1,0:T(8,128)S(1)} collective-permute-done((f32[512,512]{1,0:T(8,128)S(1)}, f32[512,512]{1,0:T(8,128)S(1)}, u32[]{:S(2)}, u32[]{:S(2)}) %collective-permute-start.8) | collective-permute-done | bytes 1048608 | tf_op jit(solution)/shard_map/ppermute | solution.py:463
  86.4 2.1 collective-permute-done.10.refs_3_
  89.2 4.2 shard_map.33
  93.4 2.9 collective-permute-start.16
  96.4 8.9 %collective-permute-done.12.refs_2_ = f32[512,512]{1,0:T(8,128)S(1)} collective-permute-done((f32[512,512]{1,0:T(8,128)S(1)}, f32[512,512]{1,0:T(8,128)S(1)}, u32[]{:S(2)}, u32[]{:S(2)}) %collective-permute-start.12) | collective-permute-done | bytes 1048608 | tf_op jit(solution)/shard_map/ppermute | solution.py:463
  111.6 4.5 shard_map.34.refs_1_
  116.2 4.0 shard_map.35
  120.2 27.5 %collective-permute-start.20 = (f32[512,512]{1,0:T(8,128)S(1)}, f32[512,512]{1,0:T(8,128)S(1)}, u32[]{:S(2)}, u32[]{:S(2)}) collective-permute-start(f32[512,512]{1,0:T(8,128)S(1)} %get-tuple-element.140), channel_id=1, source_target_pairs={{16,24},{20,28},{18,26},{22,30},{2,10},{8,16},{6,14},{12,20},{14,2... | collective-permute-start | bytes 3145736 | tf_op jit(solution)/shard_map/ppermute | solution.py:463
  149.1 7.5 %collective-permute-start.23 = (f32[512,512]{1,0:T(8,128)S(1)}, f32[512,512]{1,0:T(8,128)S(1)}, u32[]{:S(2)}, u32[]{:S(2)}) collective-permute-start(f32[512,512]{1,0:T(8,128)S(1)} %get-tuple-element.143), channel_id=1, source_target_pairs={{0,2},{30,28},{4,6},{26,24},{28,30},{24,26},{2,0},{6,4},{12,14},{2... | collective-permute-start | bytes 3145736 | tf_op jit(solution)/shard_map/ppermute | solution.py:463
  156.5 4.0 shard_map.36
  160.5 5.3 collective-permute-start.24
  165.8 5.3 collective-permute-done.20.refs_2_
  172.5 4.6 collective-permute-done.21.refs_3_
  177.1 2.2 collective-permute-start.26
  179.3 2.3 collective-permute-start.27
  181.6 21.9 %shard_map.37.refs_1_ = f32[1,2,512,2048]{3,2,1,0:T(8,128)} custom-call(s32[936]{0:T(1024)S(1)} %bitcast.10, f32[60,512,512]{2,1,0:T(8,128)} %get-tuple-element.138.buf.refs_0_, f32[1,2,512,2048]{3,2,1,0:T(8,128)} %get-tuple-element.139.refs_0_), custom_call_target="tpu_custom_call", output_to_operand_aliasing={{}: (2, {})} | custom-call | flops 16106127360 | bytes 48234496 | tf_op jit(solution)/shard_map/pallas_call | solution.py:408
  203.5 4.3 shard_map.38
  207.8 17.4 %collective-permute-start.28 = (f32[512,512]{1,0:T(8,128)S(1)}, f32[512,512]{1,0:T(8,128)S(1)}, u32[]{:S(2)}, u32[]{:S(2)}) collective-permute-start(f32[512,512]{1,0:T(8,128)S(1)} %get-tuple-element.152), channel_id=1, source_target_pairs={{20,28},{16,24},{18,26},{22,30},{6,14},{8,16},{2,10},{12,20},{4,12... | collective-permute-start | bytes 3145736 | tf_op jit(solution)/shard_map/ppermute | solution.py:463
  229.3 4.3 shard_map.39
  233.7 5.5 collective-permute-start.32
  239.2 9.6 %collective-permute-done.28.refs_2_ = f32[512,512]{1,0:T(8,128)S(1)} collective-permute-done((f32[512,512]{1,0:T(8,128)S(1)}, f32[512,512]{1,0:T(8,128)S(1)}, u32[]{:S(2)}, u32[]{:S(2)}) %collective-permute-start.28) | collective-permute-done | bytes 1048608 | tf_op jit(solution)/shard_map/ppermute | solution.py:463
  251.8 4.0 collective-permute-start.34
  255.7 36.1 %shard_map.40.refs_1_ = f32[1,2,512,2048]{3,2,1,0:T(8,128)} custom-call(s32[936]{0:T(1024)S(1)} %bitcast.13, f32[60,512,512]{2,1,0:T(8,128)} %get-tuple-element.150.buf.refs_0_, f32[1,2,512,2048]{3,2,1,0:T(8,128)} %get-tuple-element.151.refs_0_), custom_call_target="tpu_custom_call", output_to_operand_aliasing={{}: (2, {})} | custom-call | flops 16106127360 | bytes 48234496 | tf_op jit(solution)/shard_map/pallas_call | solution.py:408
  291.9 4.4 shard_map.41
  296.3 4.7 collective-permute-start.36
  303.8 4.0 shard_map.42
  307.8 5.3 collective-permute-start.40
  314.5 3.8 collective-permute-done.37.refs_3_
  320.9 35.1 %shard_map.43.refs_1_ = f32[1,2,512,2048]{3,2,1,0:T(8,128)} custom-call(s32[936]{0:T(1024)S(1)} %bitcast.16, f32[60,512,512]{2,1,0:T(8,128)} %get-tuple-element.162.buf.refs_0_, f32[1,2,512,2048]{3,2,1,0:T(8,128)} %get-tuple-element.163.refs_0_), custom_call_target="tpu_custom_call", output_to_operand_aliasing={{}: (2, {})} | custom-call | flops 16106127360 | bytes 48234496 | tf_op jit(solution)/shard_map/pallas_call | solution.py:408
  356.0 4.0 shard_map.44
  360.0 4.9 collective-permute-start.44
  370.2 3.7 shard_map.45
  374.6 2.5 collective-permute-done.44.refs_2_
  378.4 3.2 collective-permute-done.45.refs_3_
  381.6 2.2 collective-permute-start.50
  383.8 2.3 collective-permute-start.51
  386.1 37.1 %shard_map.46.refs_1_ = f32[1,2,512,2048]{3,2,1,0:T(8,128)} custom-call(s32[936]{0:T(1024)S(1)} %bitcast.19, f32[60,512,512]{2,1,0:T(8,128)} %get-tuple-element.174.buf.refs_0_, f32[1,2,512,2048]{3,2,1,0:T(8,128)} %get-tuple-element.175.refs_0_), custom_call_target="tpu_custom_call", output_to_operand_aliasing={{}: (2, {})} | custom-call | flops 16106127360 | bytes 48234496 | tf_op jit(solution)/shard_map/pallas_call | solution.py:408
  423.2 4.0 shard_map.47
  431.2 4.2 collective-permute-start.55
  435.5 3.9 shard_map.48
  441.5 36.1 %shard_map.49.refs_1_ = f32[1,2,512,2048]{3,2,1,0:T(8,128)} custom-call(s32[936]{0:T(1024)S(1)} %bitcast.22, f32[60,512,512]{2,1,0:T(8,128)} %get-tuple-element.186.buf.refs_0_, f32[1,2,512,2048]{3,2,1,0:T(8,128)} %get-tuple-element.187.refs_0_), custom_call_target="tpu_custom_call", output_to_operand_aliasing={{}: (2, {})} | custom-call | flops 16106127360 | bytes 48234496 | tf_op jit(solution)/shard_map/pallas_call | solution.py:408
  479.5 5.0 collective-permute-start.59
  484.5 3.6 shard_map.50
  492.1 22.8 %shard_map.51.refs_1_ = f32[1,2,512,2048]{3,2,1,0:T(8,128)} custom-call(s32[936]{0:T(1024)S(1)} %bitcast.24, f32[60,512,512]{2,1,0:T(8,128)} %get-tuple-element.192.buf.refs_0_, f32[1,2,512,2048]{3,2,1,0:T(8,128)} %get-tuple-element.193.refs_0_), custom_call_target="tpu_custom_call", output_to_operand_aliasing={{}: (2, {})} | custom-call | flops 16106127360 | bytes 48234496 | tf_op jit(solution)/shard_map/pallas_call | solution.py:408
  516.3 3.7 shard_map.52
  522.0 4.3 collective-permute-start.66
  527.6 23.7 %shard_map.53.refs_1_ = f32[1,2,512,2048]{3,2,1,0:T(8,128)} custom-call(s32[936]{0:T(1024)S(1)} %bitcast.26, f32[60,512,512]{2,1,0:T(8,128)} %get-tuple-element.198.buf.refs_0_, f32[1,2,512,2048]{3,2,1,0:T(8,128)} %get-tuple-element.199.refs_0_), custom_call_target="tpu_custom_call", output_to_operand_aliasing={{}: (2, {})} | custom-call | flops 8053063680 | bytes 32505856 | tf_op jit(solution)/shard_map/pallas_call | solution.py:408
  551.3 2.6 shard_map.54
  556.7 20.0 %shard_map.55.refs_1_ = f32[1,2,512,2048]{3,2,1,0:T(8,128)} custom-call(s32[936]{0:T(1024)S(1)} %bitcast.28, f32[60,512,512]{2,1,0:T(8,128)} %get-tuple-element.204.buf.refs_0_, f32[1,2,512,2048]{3,2,1,0:T(8,128)} %get-tuple-element.205.refs_0_), custom_call_target="tpu_custom_call", output_to_operand_aliasing={{}: (2, {})} | custom-call | flops 8053063680 | bytes 32505856 | tf_op jit(solution)/shard_map/pallas_call | solution.py:408
  576.7 2.5 shard_map.56
  579.2 20.4 %shard_map.57.refs_1_ = f32[1,2,512,2048]{3,2,1,0:T(8,128)} custom-call(s32[936]{0:T(1024)S(1)} %bitcast.30, f32[60,512,512]{2,1,0:T(8,128)} %get-tuple-element.210.buf.refs_0_, f32[1,2,512,2048]{3,2,1,0:T(8,128)} %get-tuple-element.211.refs_0_), custom_call_target="tpu_custom_call", output_to_operand_aliasing={{}: (2, {})} | custom-call | flops 6442450944 | bytes 29360128 | tf_op jit(solution)/shard_map/pallas_call | solution.py:408
  601.4 11.3 %shard_map.59 = f32[1,2,512,2048]{3,2,1,0:T(8,128)} custom-call(s32[936]{0:T(1024)S(1)} %bitcast.32, f32[60,512,512]{2,1,0:T(8,128)} %get-tuple-element.215.buf, f32[1,2,512,2048]{3,2,1,0:T(8,128)} %get-tuple-element.216.refs_0_), custom_call_target="tpu_custom_call", output_to_operand_aliasing={{}: (2, {})} | custom-call | flops 1610612736 | bytes 19922944 | tf_op jit(solution)/shard_map/pallas_call | solution.py:408
  (111 shorter events, 66.6 us)
Async XLA Ops:
  10.5 27.4 %collective-permute-start = (f32[512,512]{1,0:T(8,128)S(1)}, f32[512,512]{1,0:T(8,128)S(1)}, u32[]{:S(2)}, u32[]{:S(2)}) collective-permute-start(f32[512,512]{1,0:T(8,128)S(1)} %get-tuple-element.113), channel_id=1, source_target_pairs={{20,28},{16,24},{22,30},{18,26},{2,10},{6,14},{8,16},{12,20},{10,1... | collective-permute-start | bytes 3145736 | tf_op jit(solution)/shard_map/ppermute | solution.py:463
  14.4 26.5 %collective-permute-start.1 = (f32[512,512]{1,0:T(8,128)S(1)}, f32[512,512]{1,0:T(8,128)S(1)}, u32[]{:S(2)}, u32[]{:S(2)}) collective-permute-start(f32[512,512]{1,0:T(8,128)S(1)} %get-tuple-element.114), channel_id=1, source_target_pairs={{14,6},{10,2},{8,0},{12,4},{24,16},{18,10},{28,20},{22,14},{30,22}... | collective-permute-start | bytes 3145736 | tf_op jit(solution)/shard_map/ppermute | solution.py:463
  15.7 25.7 %collective-permute-start.2 = (f32[512,512]{1,0:T(8,128)S(1)}, f32[512,512]{1,0:T(8,128)S(1)}, u32[]{:S(2)}, u32[]{:S(2)}) collective-permute-start(f32[512,512]{1,0:T(8,128)S(1)} %get-tuple-element.115), channel_id=1, source_target_pairs={{24,28},{28,24},{6,2},{2,6},{30,26},{26,30},{4,0},{0,4},{10,14},{2... | collective-permute-start | bytes 3145736 | tf_op jit(solution)/shard_map/ppermute | solution.py:463
  16.3 25.6 %collective-permute-start.3 = (f32[512,512]{1,0:T(8,128)S(1)}, f32[512,512]{1,0:T(8,128)S(1)}, u32[]{:S(2)}, u32[]{:S(2)}) collective-permute-start(f32[512,512]{1,0:T(8,128)S(1)} %get-tuple-element.116), channel_id=1, source_target_pairs={{26,24},{30,28},{4,6},{0,2},{24,26},{2,0},{6,4},{28,30},{8,10},{22... | collective-permute-start | bytes 3145736 | tf_op jit(solution)/shard_map/ppermute | solution.py:463
  19.3 41.0 %collective-permute-start.4 = (f32[512,512]{1,0:T(8,128)S(1)}, f32[512,512]{1,0:T(8,128)S(1)}, u32[]{:S(2)}, u32[]{:S(2)}) collective-permute-start(f32[512,512]{1,0:T(8,128)S(1)} %get-tuple-element.118), channel_id=1, source_target_pairs={{20,28},{16,24},{22,30},{18,26},{2,10},{12,20},{8,16},{6,14},{14,2... | collective-permute-start | bytes 3145736 | tf_op jit(solution)/shard_map/ppermute | solution.py:463
  37.9 25.5 %collective-permute-start.5 = (f32[512,512]{1,0:T(8,128)S(1)}, f32[512,512]{1,0:T(8,128)S(1)}, u32[]{:S(2)}, u32[]{:S(2)}) collective-permute-start(f32[512,512]{1,0:T(8,128)S(1)} %get-tuple-element.119), channel_id=1, source_target_pairs={{10,2},{14,6},{12,4},{8,0},{22,14},{18,10},{24,16},{28,20},{30,22}... | collective-permute-start | bytes 3145736 | tf_op jit(solution)/shard_map/ppermute | solution.py:463
  40.9 25.1 %collective-permute-start.6 = (f32[512,512]{1,0:T(8,128)S(1)}, f32[512,512]{1,0:T(8,128)S(1)}, u32[]{:S(2)}, u32[]{:S(2)}) collective-permute-start(f32[512,512]{1,0:T(8,128)S(1)} %get-tuple-element.120), channel_id=1, source_target_pairs={{2,6},{28,24},{6,2},{24,28},{4,0},{26,30},{0,4},{30,26},{14,10},{1... | collective-permute-start | bytes 3145736 | tf_op jit(solution)/shard_map/ppermute | solution.py:463
  41.4 25.3 %collective-permute-start.7 = (f32[512,512]{1,0:T(8,128)S(1)}, f32[512,512]{1,0:T(8,128)S(1)}, u32[]{:S(2)}, u32[]{:S(2)}) collective-permute-start(f32[512,512]{1,0:T(8,128)S(1)} %get-tuple-element.121), channel_id=1, source_target_pairs={{0,2},{26,24},{30,28},{4,6},{24,26},{6,4},{2,0},{28,30},{18,16},{8... | collective-permute-start | bytes 3145736 | tf_op jit(solution)/shard_map/ppermute | solution.py:463
  46.2 36.7 %collective-permute-start.8 = (f32[512,512]{1,0:T(8,128)S(1)}, f32[512,512]{1,0:T(8,128)S(1)}, u32[]{:S(2)}, u32[]{:S(2)}) collective-permute-start(f32[512,512]{1,0:T(8,128)S(1)} %get-tuple-element.123), channel_id=1, source_target_pairs={{20,28},{16,24},{18,26},{22,30},{8,16},{12,20},{6,14},{2,10},{10,1... | collective-permute-start | bytes 3145736 | tf_op jit(solution)/shard_map/ppermute | solution.py:463
  60.4 25.5 %collective-permute-start.9 = (f32[512,512]{1,0:T(8,128)S(1)}, f32[512,512]{1,0:T(8,128)S(1)}, u32[]{:S(2)}, u32[]{:S(2)}) collective-permute-start(f32[512,512]{1,0:T(8,128)S(1)} %get-tuple-element.124), channel_id=1, source_target_pairs={{14,6},{10,2},{8,0},{12,4},{24,16},{22,14},{28,20},{18,10},{26,18}... | collective-permute-start | bytes 3145736 | tf_op jit(solution)/shard_map/ppermute | solution.py:463
  63.4 25.1 %collective-permute-start.10 = (f32[512,512]{1,0:T(8,128)S(1)}, f32[512,512]{1,0:T(8,128)S(1)}, u32[]{:S(2)}, u32[]{:S(2)}) collective-permute-start(f32[512,512]{1,0:T(8,128)S(1)} %get-tuple-element.125), channel_id=1, source_target_pairs={{28,24},{2,6},{6,2},{24,28},{4,0},{30,26},{0,4},{26,30},{16,20},{1... | collective-permute-start | bytes 3145736 | tf_op jit(solution)/shard_map/ppermute | solution.py:463
  66.0 23.1 %collective-permute-start.11 = (f32[512,512]{1,0:T(8,128)S(1)}, f32[512,512]{1,0:T(8,128)S(1)}, u32[]{:S(2)}, u32[]{:S(2)}) collective-permute-start(f32[512,512]{1,0:T(8,128)S(1)} %get-tuple-element.126), channel_id=1, source_target_pairs={{26,24},{4,6},{30,28},{0,2},{28,30},{6,4},{2,0},{24,26},{8,10},{22... | collective-permute-start | bytes 3145736 | tf_op jit(solution)/shard_map/ppermute | solution.py:463
  71.0 34.3 %collective-permute-start.12 = (f32[512,512]{1,0:T(8,128)S(1)}, f32[512,512]{1,0:T(8,128)S(1)}, u32[]{:S(2)}, u32[]{:S(2)}) collective-permute-start(f32[512,512]{1,0:T(8,128)S(1)} %get-tuple-element.128), channel_id=1, source_target_pairs={{16,24},{20,28},{18,26},{22,30},{6,14},{8,16},{2,10},{12,20},{0,8}... | collective-permute-start | bytes 3145736 | tf_op jit(solution)/shard_map/ppermute | solution.py:463
  82.8 25.5 %collective-permute-start.13 = (f32[512,512]{1,0:T(8,128)S(1)}, f32[512,512]{1,0:T(8,128)S(1)}, u32[]{:S(2)}, u32[]{:S(2)}) collective-permute-start(f32[512,512]{1,0:T(8,128)S(1)} %get-tuple-element.129), channel_id=1, source_target_pairs={{14,6},{10,2},{8,0},{12,4},{24,16},{22,14},{18,10},{28,20},{16,8},... | collective-permute-start | bytes 3145736 | tf_op jit(solution)/shard_map/ppermute | solution.py:463
  85.9 25.1 %collective-permute-start.14 = (f32[512,512]{1,0:T(8,128)S(1)}, f32[512,512]{1,0:T(8,128)S(1)}, u32[]{:S(2)}, u32[]{:S(2)}) collective-permute-start(f32[512,512]{1,0:T(8,128)S(1)} %get-tuple-element.130), channel_id=1, source_target_pairs={{2,6},{6,2},{28,24},{24,28},{0,4},{26,30},{30,26},{4,0},{16,20},{1... | collective-permute-start | bytes 3145736 | tf_op jit(solution)/shard_map/ppermute | solution.py:463
  88.5 27.7 %collective-permute-start.15 = (f32[512,512]{1,0:T(8,128)S(1)}, f32[512,512]{1,0:T(8,128)S(1)}, u32[]{:S(2)}, u32[]{:S(2)}) collective-permute-start(f32[512,512]{1,0:T(8,128)S(1)} %get-tuple-element.131), channel_id=1, source_target_pairs={{30,28},{26,24},{0,2},{4,6},{6,4},{2,0},{24,26},{28,30},{18,16},{8... | collective-permute-start | bytes 3145736 | tf_op jit(solution)/shard_map/ppermute | solution.py:463
  93.4 54.2 %collective-permute-start.16 = (f32[512,512]{1,0:T(8,128)S(1)}, f32[512,512]{1,0:T(8,128)S(1)}, u32[]{:S(2)}, u32[]{:S(2)}) collective-permute-start(f32[512,512]{1,0:T(8,128)S(1)} %get-tuple-element.134), channel_id=1, source_target_pairs={{16,24},{20,28},{22,30},{18,26},{8,16},{2,10},{12,20},{6,14},{4,12... | collective-permute-start | bytes 3145736 | tf_op jit(solution)/shard_map/ppermute | solution.py:463
  105.3 43.7 %collective-permute-start.17 = (f32[512,512]{1,0:T(8,128)S(1)}, f32[512,512]{1,0:T(8,128)S(1)}, u32[]{:S(2)}, u32[]{:S(2)}) collective-permute-start(f32[512,512]{1,0:T(8,128)S(1)} %get-tuple-element.135), channel_id=1, source_target_pairs={{14,6},{10,2},{12,4},{8,0},{18,10},{24,16},{22,14},{28,20},{16,8},... | collective-permute-start | bytes 3145736 | tf_op jit(solution)/shard_map/ppermute | solution.py:463
  108.3 40.7 %collective-permute-start.18 = (f32[512,512]{1,0:T(8,128)S(1)}, f32[512,512]{1,0:T(8,128)S(1)}, u32[]{:S(2)}, u32[]{:S(2)}) collective-permute-start(f32[512,512]{1,0:T(8,128)S(1)} %get-tuple-element.136), channel_id=1, source_target_pairs={{28,24},{6,2},{2,6},{24,28},{0,4},{26,30},{4,0},{30,26},{16,20},{1... | collective-permute-start | bytes 3145736 | tf_op jit(solution)/shard_map/ppermute | solution.py:463
  111.0 45.6 %collective-permute-start.19 = (f32[512,512]{1,0:T(8,128)S(1)}, f32[512,512]{1,0:T(8,128)S(1)}, u32[]{:S(2)}, u32[]{:S(2)}) collective-permute-start(f32[512,512]{1,0:T(8,128)S(1)} %get-tuple-element.137), channel_id=1, source_target_pairs={{26,24},{30,28},{4,6},{0,2},{24,26},{6,4},{2,0},{28,30},{12,14},{2... | collective-permute-start | bytes 3145736 | tf_op jit(solution)/shard_map/ppermute | solution.py:463
  120.2 51.0 %collective-permute-start.20 = (f32[512,512]{1,0:T(8,128)S(1)}, f32[512,512]{1,0:T(8,128)S(1)}, u32[]{:S(2)}, u32[]{:S(2)}) collective-permute-start(f32[512,512]{1,0:T(8,128)S(1)} %get-tuple-element.140), channel_id=1, source_target_pairs={{16,24},{20,28},{18,26},{22,30},{2,10},{8,16},{6,14},{12,20},{14,2... | collective-permute-start | bytes 3145736 | tf_op jit(solution)/shard_map/ppermute | solution.py:463
  147.7 29.4 %collective-permute-start.21 = (f32[512,512]{1,0:T(8,128)S(1)}, f32[512,512]{1,0:T(8,128)S(1)}, u32[]{:S(2)}, u32[]{:S(2)}) collective-permute-start(f32[512,512]{1,0:T(8,128)S(1)} %get-tuple-element.141), channel_id=1, source_target_pairs={{14,6},{10,2},{12,4},{8,0},{28,20},{22,14},{24,16},{18,10},{16,8},... | collective-permute-start | bytes 3145736 | tf_op jit(solution)/shard_map/ppermute | solution.py:463
  149.0 30.3 %collective-permute-start.22 = (f32[512,512]{1,0:T(8,128)S(1)}, f32[512,512]{1,0:T(8,128)S(1)}, u32[]{:S(2)}, u32[]{:S(2)}) collective-permute-start(f32[512,512]{1,0:T(8,128)S(1)} %get-tuple-element.142), channel_id=1, source_target_pairs={{28,24},{24,28},{6,2},{2,6},{4,0},{26,30},{0,4},{30,26},{14,10},{2... | collective-permute-start | bytes 3145736 | tf_op jit(solution)/shard_map/ppermute | solution.py:463
  149.1 54.4 %collective-permute-start.23 = (f32[512,512]{1,0:T(8,128)S(1)}, f32[512,512]{1,0:T(8,128)S(1)}, u32[]{:S(2)}, u32[]{:S(2)}) collective-permute-start(f32[512,512]{1,0:T(8,128)S(1)} %get-tuple-element.143), channel_id=1, source_target_pairs={{0,2},{30,28},{4,6},{26,24},{28,30},{24,26},{2,0},{6,4},{12,14},{2... | collective-permute-start | bytes 3145736 | tf_op jit(solution)/shard_map/ppermute | solution.py:463
  160.5 64.8 %collective-permute-start.24 = (f32[512,512]{1,0:T(8,128)S(1)}, f32[512,512]{1,0:T(8,128)S(1)}, u32[]{:S(2)}, u32[]{:S(2)}) collective-permute-start(f32[512,512]{1,0:T(8,128)S(1)} %get-tuple-element.146), channel_id=1, source_target_pairs={{20,28},{16,24},{18,26},{22,30},{2,10},{12,20},{6,14},{8,16},{4,12... | collective-permute-start | bytes 3145736 | tf_op jit(solution)/shard_map/ppermute | solution.py:463
  171.2 55.4 %collective-permute-start.25 = (f32[512,512]{1,0:T(8,128)S(1)}, f32[512,512]{1,0:T(8,128)S(1)}, u32[]{:S(2)}, u32[]{:S(2)}) collective-permute-start(f32[512,512]{1,0:T(8,128)S(1)} %get-tuple-element.147), channel_id=1, source_target_pairs={{10,2},{14,6},{8,0},{12,4},{22,14},{28,20},{24,16},{18,10},{20,12}... | collective-permute-start | bytes 3145736 | tf_op jit(solution)/shard_map/ppermute | solution.py:463
  177.1 51.5 %collective-permute-start.26 = (f32[512,512]{1,0:T(8,128)S(1)}, f32[512,512]{1,0:T(8,128)S(1)}, u32[]{:S(2)}, u32[]{:S(2)}) collective-permute-start(f32[512,512]{1,0:T(8,128)S(1)} %get-tuple-element.148), channel_id=1, source_target_pairs={{24,28},{28,24},{6,2},{2,6},{0,4},{30,26},{26,30},{4,0},{10,14},{1... | collective-permute-start | bytes 3145736 | tf_op jit(solution)/shard_map/ppermute | solution.py:463
  179.3 50.0 %collective-permute-start.27 = (f32[512,512]{1,0:T(8,128)S(1)}, f32[512,512]{1,0:T(8,128)S(1)}, u32[]{:S(2)}, u32[]{:S(2)}) collective-permute-start(f32[512,512]{1,0:T(8,128)S(1)} %get-tuple-element.149), channel_id=1, source_target_pairs={{30,28},{0,2},{4,6},{26,24},{24,26},{6,4},{2,0},{28,30},{8,10},{12... | collective-permute-start | bytes 3145736 | tf_op jit(solution)/shard_map/ppermute | solution.py:463
  207.8 41.0 %collective-permute-start.28 = (f32[512,512]{1,0:T(8,128)S(1)}, f32[512,512]{1,0:T(8,128)S(1)}, u32[]{:S(2)}, u32[]{:S(2)}) collective-permute-start(f32[512,512]{1,0:T(8,128)S(1)} %get-tuple-element.152), channel_id=1, source_target_pairs={{20,28},{16,24},{18,26},{22,30},{6,14},{8,16},{2,10},{12,20},{4,12... | collective-permute-start | bytes 3145736 | tf_op jit(solution)/shard_map/ppermute | solution.py:463
  225.3 26.5 %collective-permute-start.29 = (f32[512,512]{1,0:T(8,128)S(1)}, f32[512,512]{1,0:T(8,128)S(1)}, u32[]{:S(2)}, u32[]{:S(2)}) collective-permute-start(f32[512,512]{1,0:T(8,128)S(1)} %get-tuple-element.153), channel_id=1, source_target_pairs={{14,6},{10,2},{12,4},{8,0},{24,16},{22,14},{28,20},{18,10},{20,12}... | collective-permute-start | bytes 3145736 | tf_op jit(solution)/shard_map/ppermute | solution.py:463
  226.6 29.1 %collective-permute-start.30 = (f32[512,512]{1,0:T(8,128)S(1)}, f32[512,512]{1,0:T(8,128)S(1)}, u32[]{:S(2)}, u32[]{:S(2)}) collective-permute-start(f32[512,512]{1,0:T(8,128)S(1)} %get-tuple-element.154), channel_id=1, source_target_pairs={{6,2},{24,28},{28,24},{2,6},{4,0},{30,26},{0,4},{26,30},{16,20},{1... | collective-permute-start | bytes 3145736 | tf_op jit(solution)/shard_map/ppermute | solution.py:463
  228.6 63.3 %collective-permute-start.31 = (f32[512,512]{1,0:T(8,128)S(1)}, f32[512,512]{1,0:T(8,128)S(1)}, u32[]{:S(2)}, u32[]{:S(2)}) collective-permute-start(f32[512,512]{1,0:T(8,128)S(1)} %get-tuple-element.155), channel_id=1, source_target_pairs={{0,2},{30,28},{4,6},{26,24},{28,30},{2,0},{24,26},{6,4},{12,14},{8... | collective-permute-start | bytes 3145736 | tf_op jit(solution)/shard_map/ppermute | solution.py:463
  233.7 67.3 %collective-permute-start.32 = (f32[512,512]{1,0:T(8,128)S(1)}, f32[512,512]{1,0:T(8,128)S(1)}, u32[]{:S(2)}, u32[]{:S(2)}) collective-permute-start(f32[512,512]{1,0:T(8,128)S(1)} %get-tuple-element.158), channel_id=1, source_target_pairs={{20,28},{16,24},{18,26},{22,30},{6,14},{2,10},{12,20},{8,16},{4,12... | collective-permute-start | bytes 3145736 | tf_op jit(solution)/shard_map/ppermute | solution.py:463
  248.8 53.5 %collective-permute-start.33 = (f32[512,512]{1,0:T(8,128)S(1)}, f32[512,512]{1,0:T(8,128)S(1)}, u32[]{:S(2)}, u32[]{:S(2)}) collective-permute-start(f32[512,512]{1,0:T(8,128)S(1)} %get-tuple-element.159), channel_id=1, source_target_pairs={{14,6},{10,2},{8,0},{12,4},{28,20},{22,14},{24,16},{18,10},{30,22}... | collective-permute-start | bytes 3145736 | tf_op jit(solution)/shard_map/ppermute | solution.py:463
  251.8 50.6 %collective-permute-start.34 = (f32[512,512]{1,0:T(8,128)S(1)}, f32[512,512]{1,0:T(8,128)S(1)}, u32[]{:S(2)}, u32[]{:S(2)}) collective-permute-start(f32[512,512]{1,0:T(8,128)S(1)} %get-tuple-element.160), channel_id=1, source_target_pairs={{28,24},{24,28},{6,2},{2,6},{4,0},{30,26},{0,4},{26,30},{16,20},{1... | collective-permute-start | bytes 3145736 | tf_op jit(solution)/shard_map/ppermute | solution.py:463
  255.7 48.0 %collective-permute-start.35 = (f32[512,512]{1,0:T(8,128)S(1)}, f32[512,512]{1,0:T(8,128)S(1)}, u32[]{:S(2)}, u32[]{:S(2)}) collective-permute-start(f32[512,512]{1,0:T(8,128)S(1)} %get-tuple-element.161), channel_id=1, source_target_pairs={{30,28},{4,6},{26,24},{0,2},{2,0},{28,30},{6,4},{24,26},{12,14},{1... | collective-permute-start | bytes 3145736 | tf_op jit(solution)/shard_map/ppermute | solution.py:463
  302.4 53.6 %collective-permute-start.39 = (f32[512,512]{1,0:T(8,128)S(1)}, f32[512,512]{1,0:T(8,128)S(1)}, u32[]{:S(2)}, u32[]{:S(2)}) collective-permute-start(f32[512,512]{1,0:T(8,128)S(1)} %get-tuple-element.167), channel_id=1, source_target_pairs={{4,6},{26,24},{30,28},{0,2},{6,4},{24,26},{2,0},{28,30},{18,16},{1... | collective-permute-start | bytes 3145736 | tf_op jit(solution)/shard_map/ppermute | solution.py:463
  307.8 57.2 %collective-permute-start.40 = (f32[512,512]{1,0:T(8,128)S(1)}, f32[512,512]{1,0:T(8,128)S(1)}, u32[]{:S(2)}, u32[]{:S(2)}) collective-permute-start(f32[512,512]{1,0:T(8,128)S(1)} %get-tuple-element.170), channel_id=1, source_target_pairs={{16,24},{20,28},{22,30},{18,26},{6,14},{12,20},{2,10},{8,16},{14,2... | collective-permute-start | bytes 3145736 | tf_op jit(solution)/shard_map/ppermute | solution.py:463
  313.2 53.0 %collective-permute-start.41 = (f32[512,512]{1,0:T(8,128)S(1)}, f32[512,512]{1,0:T(8,128)S(1)}, u32[]{:S(2)}, u32[]{:S(2)}) collective-permute-start(f32[512,512]{1,0:T(8,128)S(1)} %get-tuple-element.171), channel_id=1, source_target_pairs={{10,2},{14,6},{8,0},{12,4},{24,16},{28,20},{22,14},{18,10},{16,8},... | collective-permute-start | bytes 3145736 | tf_op jit(solution)/shard_map/ppermute | solution.py:463
  318.3 50.0 %collective-permute-start.42 = (f32[512,512]{1,0:T(8,128)S(1)}, f32[512,512]{1,0:T(8,128)S(1)}, u32[]{:S(2)}, u32[]{:S(2)}) collective-permute-start(f32[512,512]{1,0:T(8,128)S(1)} %get-tuple-element.172), channel_id=1, source_target_pairs={{24,28},{2,6},{6,2},{28,24},{26,30},{0,4},{30,26},{4,0},{16,20},{1... | collective-permute-start | bytes 3145736 | tf_op jit(solution)/shard_map/ppermute | solution.py:463
  319.9 50.4 %collective-permute-start.43 = (f32[512,512]{1,0:T(8,128)S(1)}, f32[512,512]{1,0:T(8,128)S(1)}, u32[]{:S(2)}, u32[]{:S(2)}) collective-permute-start(f32[512,512]{1,0:T(8,128)S(1)} %get-tuple-element.173), channel_id=1, source_target_pairs={{30,28},{26,24},{0,2},{4,6},{2,0},{28,30},{6,4},{24,26},{22,20},{1... | collective-permute-start | bytes 3145736 | tf_op jit(solution)/shard_map/ppermute | solution.py:463
  368.3 54.9 %collective-permute-start.47 = (f32[512,512]{1,0:T(8,128)S(1)}, f32[512,512]{1,0:T(8,128)S(1)}, u32[]{:S(2)}, u32[]{:S(2)}) collective-permute-start(f32[512,512]{1,0:T(8,128)S(1)} %get-tuple-element.179), channel_id=1, source_target_pairs={{30,28},{4,6},{26,24},{0,2},{24,26},{2,0},{6,4},{28,30},{18,16},{2... | collective-permute-start | bytes 3145736 | tf_op jit(solution)/shard_map/ppermute | solution.py:463
  373.9 54.1 %collective-permute-start.48 = (f32[512,512]{1,0:T(8,128)}, f32[512,512]{1,0:T(8,128)S(1)}, u32[]{:S(2)}, u32[]{:S(2)}) collective-permute-start(f32[512,512]{1,0:T(8,128)} %get-tuple-element.182), channel_id=1, source_target_pairs={{20,28},{16,24},{18,26},{22,30},{2,10},{12,20},{8,16},{21,29},{17,... | collective-permute-start | bytes 3145736 | tf_op jit(solution)/shard_map/ppermute | solution.py:463
  377.2 52.1 %collective-permute-start.49 = (f32[512,512]{1,0:T(8,128)S(1)}, f32[512,512]{1,0:T(8,128)S(1)}, u32[]{:S(2)}, u32[]{:S(2)}) collective-permute-start(f32[512,512]{1,0:T(8,128)S(1)} %get-tuple-element.183), channel_id=1, source_target_pairs={{10,2},{14,6},{12,4},{8,0},{28,20},{18,10},{24,16},{22,14},{11,3},... | collective-permute-start | bytes 3145736 | tf_op jit(solution)/shard_map/ppermute | solution.py:463
  381.6 49.6 %collective-permute-start.50 = (f32[512,512]{1,0:T(8,128)S(1)}, f32[512,512]{1,0:T(8,128)S(1)}, u32[]{:S(2)}, u32[]{:S(2)}) collective-permute-start(f32[512,512]{1,0:T(8,128)S(1)} %get-tuple-element.184), channel_id=1, source_target_pairs={{24,28},{28,24},{2,6},{6,2},{30,26},{26,30},{0,4},{4,0},{16,20},{2... | collective-permute-start | bytes 3145736 | tf_op jit(solution)/shard_map/ppermute | solution.py:463
  383.8 51.6 %collective-permute-start.51 = (f32[512,512]{1,0:T(8,128)S(1)}, f32[512,512]{1,0:T(8,128)S(1)}, u32[]{:S(2)}, u32[]{:S(2)}) collective-permute-start(f32[512,512]{1,0:T(8,128)S(1)} %get-tuple-element.185), channel_id=1, source_target_pairs={{26,24},{4,6},{0,2},{30,28},{6,4},{2,0},{28,30},{24,26},{12,14},{8... | collective-permute-start | bytes 3145736 | tf_op jit(solution)/shard_map/ppermute | solution.py:463
  428.0 49.5 %collective-permute-start.53 = (f32[512,512]{1,0:T(8,128)S(1)}, f32[512,512]{1,0:T(8,128)S(1)}, u32[]{:S(2)}, u32[]{:S(2)}) collective-permute-start(f32[512,512]{1,0:T(8,128)S(1)} %get-tuple-element.189), channel_id=1, source_target_pairs={{10,2},{14,6},{12,4},{8,0},{22,14},{11,3},{15,7},{13,5},{9,1},{23,... | collective-permute-start | bytes 3145736 | tf_op jit(solution)/shard_map/ppermute | solution.py:463
  429.3 50.2 %collective-permute-start.54 = (f32[512,512]{1,0:T(8,128)S(1)}, f32[512,512]{1,0:T(8,128)S(1)}, u32[]{:S(2)}, u32[]{:S(2)}) collective-permute-start(f32[512,512]{1,0:T(8,128)S(1)} %get-tuple-element.190), channel_id=1, source_target_pairs={{6,2},{28,24},{2,6},{24,28},{26,30},{30,26},{0,4},{4,0},{7,3},{29,... | collective-permute-start | bytes 3145736 | tf_op jit(solution)/shard_map/ppermute | solution.py:463
  431.2 53.3 %collective-permute-start.55 = (f32[512,512]{1,0:T(8,128)S(1)}, f32[512,512]{1,0:T(8,128)S(1)}, u32[]{:S(2)}, u32[]{:S(2)}) collective-permute-start(f32[512,512]{1,0:T(8,128)S(1)} %get-tuple-element.191), channel_id=1, source_target_pairs={{4,6},{26,24},{30,28},{0,2},{24,26},{6,4},{2,0},{28,30},{5,7},{27,... | collective-permute-start | bytes 3145736 | tf_op jit(solution)/shard_map/ppermute | solution.py:463
  439.4 49.5 %collective-permute-start.56 = (f32[512,512]{1,0:T(8,128)}, f32[512,512]{1,0:T(8,128)S(1)}, u32[]{:S(2)}, u32[]{:S(2)}) collective-permute-start(f32[512,512]{1,0:T(8,128)} %get-tuple-element.194), channel_id=1, source_target_pairs={{16,24},{20,28},{18,26},{22,30},{17,25},{21,29},{19,27},{23,31}} | collective-permute-start | bytes 3145736 | tf_op jit(solution)/shard_map/ppermute | solution.py:463
  440.2 50.0 %collective-permute-start.57 = (f32[512,512]{1,0:T(8,128)S(1)}, f32[512,512]{1,0:T(8,128)S(1)}, u32[]{:S(2)}, u32[]{:S(2)}) collective-permute-start(f32[512,512]{1,0:T(8,128)S(1)} %get-tuple-element.195), channel_id=1, source_target_pairs={{14,6},{10,2},{12,4},{8,0},{15,7},{11,3},{13,5},{9,1}} | collective-permute-start | bytes 3145736 | tf_op jit(solution)/shard_map/ppermute | solution.py:463
  477.5 37.4 %collective-permute-start.58 = (f32[512,512]{1,0:T(8,128)S(1)}, f32[512,512]{1,0:T(8,128)S(1)}, u32[]{:S(2)}, u32[]{:S(2)}) collective-permute-start(f32[512,512]{1,0:T(8,128)S(1)} %get-tuple-element.196), channel_id=1, source_target_pairs={{6,2},{28,24},{2,6},{24,28},{4,0},{7,3},{29,25},{3,7},{25,29},{5,1}} | collective-permute-start | bytes 3145736 | tf_op jit(solution)/shard_map/ppermute | solution.py:463
  479.5 36.8 %collective-permute-start.59 = (f32[512,512]{1,0:T(8,128)S(1)}, f32[512,512]{1,0:T(8,128)S(1)}, u32[]{:S(2)}, u32[]{:S(2)}) collective-permute-start(f32[512,512]{1,0:T(8,128)S(1)} %get-tuple-element.197), channel_id=1, source_target_pairs={{30,28},{26,24},{0,2},{4,6},{24,26},{6,4},{28,30},{31,29},{27,25},... | collective-permute-start | bytes 3145736 | tf_op jit(solution)/shard_map/ppermute | solution.py:463
  488.1 32.5 %collective-permute-start.60 = (f32[512,512]{1,0:T(8,128)}, f32[512,512]{1,0:T(8,128)S(1)}, u32[]{:S(2)}, u32[]{:S(2)}) collective-permute-start(f32[512,512]{1,0:T(8,128)} %get-tuple-element.200), channel_id=1, source_target_pairs={{20,28},{16,24},{21,29},{17,25}} | collective-permute-start | bytes 3145736 | tf_op jit(solution)/shard_map/ppermute | solution.py:463
  488.9 33.1 %collective-permute-start.61 = (f32[512,512]{1,0:T(8,128)S(1)}, f32[512,512]{1,0:T(8,128)S(1)}, u32[]{:S(2)}, u32[]{:S(2)}) collective-permute-start(f32[512,512]{1,0:T(8,128)S(1)} %get-tuple-element.201), channel_id=1, source_target_pairs={{10,2},{14,6},{11,3},{15,7}} | collective-permute-start | bytes 3145736 | tf_op jit(solution)/shard_map/ppermute | solution.py:463
  490.2 36.1 %collective-permute-start.62 = (f32[512,512]{1,0:T(8,128)S(1)}, f32[512,512]{1,0:T(8,128)S(1)}, u32[]{:S(2)}, u32[]{:S(2)}) collective-permute-start(f32[512,512]{1,0:T(8,128)S(1)} %get-tuple-element.202), channel_id=1, source_target_pairs={{2,6},{6,2},{28,24},{24,28},{3,7},{7,3},{29,25},{25,29}} | collective-permute-start | bytes 3145736 | tf_op jit(solution)/shard_map/ppermute | solution.py:463
  515.0 36.4 %collective-permute-start.63 = (f32[512,512]{1,0:T(8,128)S(1)}, f32[512,512]{1,0:T(8,128)S(1)}, u32[]{:S(2)}, u32[]{:S(2)}) collective-permute-start(f32[512,512]{1,0:T(8,128)S(1)} %get-tuple-element.203), channel_id=1, source_target_pairs={{4,6},{26,24},{0,2},{30,28},{5,7},{27,25},{1,3},{31,29}} | collective-permute-start | bytes 3145736 | tf_op jit(solution)/shard_map/ppermute | solution.py:463
  519.9 34.7 %collective-permute-start.64 = (f32[512,512]{1,0:T(8,128)S(1)}, f32[512,512]{1,0:T(8,128)S(1)}, u32[]{:S(2)}, u32[]{:S(2)}) collective-permute-start(f32[512,512]{1,0:T(8,128)S(1)} %get-tuple-element.206), channel_id=1, source_target_pairs={{20,28},{16,24},{21,29},{17,25}} | collective-permute-start | bytes 3145736 | tf_op jit(solution)/shard_map/ppermute | solution.py:463
  520.7 35.3 %collective-permute-start.65 = (f32[512,512]{1,0:T(8,128)S(1)}, f32[512,512]{1,0:T(8,128)S(1)}, u32[]{:S(2)}, u32[]{:S(2)}) collective-permute-start(f32[512,512]{1,0:T(8,128)S(1)} %get-tuple-element.207), channel_id=1, source_target_pairs={{14,6},{10,2},{15,7},{11,3}} | collective-permute-start | bytes 3145736 | tf_op jit(solution)/shard_map/ppermute | solution.py:463
  522.0 54.7 %collective-permute-start.66 = (f32[512,512]{1,0:T(8,128)S(1)}, f32[512,512]{1,0:T(8,128)S(1)}, u32[]{:S(2)}, u32[]{:S(2)}) collective-permute-start(f32[512,512]{1,0:T(8,128)S(1)} %get-tuple-element.208), channel_id=1, source_target_pairs={{24,28},{6,2},{28,24},{2,6},{25,29},{7,3},{29,25},{3,7}} | collective-permute-start | bytes 3145736 | tf_op jit(solution)/shard_map/ppermute | solution.py:463
  526.3 50.4 %collective-permute-start.67 = (f32[512,512]{1,0:T(8,128)S(1)}, f32[512,512]{1,0:T(8,128)S(1)}, u32[]{:S(2)}, u32[]{:S(2)}) collective-permute-start(f32[512,512]{1,0:T(8,128)S(1)} %get-tuple-element.209), channel_id=1, source_target_pairs={{4,6},{30,28},{0,2},{26,24},{5,7},{31,29},{1,3},{27,25}} | collective-permute-start | bytes 3145736 | tf_op jit(solution)/shard_map/ppermute | solution.py:463
  553.9 45.7 %collective-permute-start.68 = (f32[512,512]{1,0:T(8,128)S(1)}, f32[512,512]{1,0:T(8,128)S(1)}, u32[]{:S(2)}, u32[]{:S(2)}) collective-permute-start(f32[512,512]{1,0:T(8,128)S(1)} %get-tuple-element.212), channel_id=1, source_target_pairs={{10,2},{11,3}} | collective-permute-start | bytes 3145736 | tf_op jit(solution)/shard_map/ppermute | solution.py:463
  554.7 45.0 %collective-permute-start.69 = (f32[512,512]{1,0:T(8,128)S(1)}, f32[512,512]{1,0:T(8,128)S(1)}, u32[]{:S(2)}, u32[]{:S(2)}) collective-permute-start(f32[512,512]{1,0:T(8,128)S(1)} %get-tuple-element.213), channel_id=1, source_target_pairs={{2,6},{3,7}} | collective-permute-start | bytes 3145736 | tf_op jit(solution)/shard_map/ppermute | solution.py:463
  556.0 43.7 %collective-permute-start.70 = (f32[512,512]{1,0:T(8,128)S(1)}, f32[512,512]{1,0:T(8,128)S(1)}, u32[]{:S(2)}, u32[]{:S(2)}) collective-permute-start(f32[512,512]{1,0:T(8,128)S(1)} %get-tuple-element.214), channel_id=1, source_target_pairs={{30,28},{26,24},{31,29},{27,25}} | collective-permute-start | bytes 3145736 | tf_op jit(solution)/shard_map/ppermute | solution.py:463
  (7 other events, 116.2 us)

commit v2 on v0

v2 whole, which is shorter than its diff:
```python
import functools
import random

import jax
import jax.numpy as jnp
import numpy as np
from jax import lax
from jax.experimental import pallas as pl
from jax.experimental.pallas import tpu as pltpu
from jax.sharding import PartitionSpec as P

AXES = ("src", "rcv")
FIELDS = 6
CAP = 6


def split_axis(n):
    return (n,) if n <= 4 else (4, n // 4)


class Grid:
    def __init__(self, src, rcv):
        self.src, self.rcv, self.width = src, rcv, src // rcv
        dims = split_axis(src) + split_axis(rcv)
        self.count = src * rcv
        place = np.array(np.unravel_index(np.arange(self.count), dims)).T
        self.dist = np.abs(place[:, None] - place[None]).sum(-1)
        self.ways = []
        for axis, size in enumerate(dims):
            for sign in (1, -1) if size > 2 else (0,):
                pairs = []
                for u in range(self.count):
                    to = place[u].copy()
                    to[axis] = 1 - to[axis] if sign == 0 else to[axis] + sign
                    if 0 <= to[axis] < size:
                        pairs.append((u, int(np.ravel_multi_index(tuple(to), dims))))
                if pairs:
                    self.ways.append(pairs)
        self.tiles = [(p, q) for p in range(src) for q in range(p, src)]
        self.number = {}
        for i, (p, q) in enumerate(self.tiles):
            self.number[p, q] = self.number[q, p] = i

    def columns(self, x):
        return range(x * self.width, (x + 1) * self.width)


def plan_moves(grid, seed):
    rnd = random.Random(seed)
    items, n = len(grid.tiles), grid.count
    has = np.full((n, items), 10**6)
    need = np.zeros((n, items), bool)
    row = np.zeros((n, items), bool)
    flip = np.zeros((n, items), bool)
    for d in range(n):
        s, x = divmod(d, grid.rcv)
        for q in range(grid.src):
            need[d, grid.number[s, q]] = True
            row[d, grid.number[s, q]] = True
            for j in grid.columns(x):
                need[d, grid.number[q, j]] = True
        for q in grid.columns(x):
            has[d, grid.number[s, q]] = 0
            flip[d, grid.number[s, q]] = s > q
    links = [(way, u, v) for way, pairs in enumerate(grid.ways) for u, v in pairs]
    degree = np.zeros(n)
    for _, _, v in links:
        degree[v] += 1
    near = np.stack([grid.dist[has[:, i] == 0].min(0) for i in range(items)])
    moves, step = [], 0
    while True:
        missing = need & (has > 10**5)
        if not missing.any():
            return moves, has, flip
        load = missing.sum(1) / degree
        weight = missing.sum(1) / np.maximum(need.sum(1), 1)
        rnd.shuffle(links)
        links.sort(key=lambda link: -load[link[2]])
        open_ = has > 10**5
        into = [[] for _ in range(n)]
        for _, u, v in links:
            into[v].append(u)
        ready = has <= step
        now = []
        for way, u, v in links:
            cand = np.nonzero(ready[u] & open_[v])[0]
            if not len(cand):
                continue
            helped = (missing[:, cand].T & (grid.dist[v][None] < near[cand])).astype(float)
            helped[:, v] = 0
            value = 3.0 * missing[v, cand] + helped @ weight
            useful = value > 0
            if not useful.any():
                continue
            others = sum(ready[w, cand].astype(float) for w in into[v])
            value = value + 0.5 * np.array([rnd.random() for _ in cand]) - 0.7 * (others - 1)
            value = value + 3.0 * (row[v, cand] & missing[v, cand])
            value[~useful] = -100
            item = int(cand[np.argmax(value)])
            open_[v, item] = False
            missing[v, item] = False
            near[item] = np.minimum(near[item], grid.dist[v])
            now.append((way, u, v, item))
        for _, u, v, item in now:
            has[v, item] = step + 2
            flip[v, item] = flip[u, item]
        moves.append(now)
        step += 1


def plan_products(grid, moves, has, flip):
    steps, n = len(moves), grid.count
    calls = [*range(3, steps + 2)]
    lists = [[[] for _ in range(n)] for _ in calls]
    for d in range(n):
        s, x = divmod(d, grid.rcv)
        todo = []
        for k in range(grid.src):
            left = grid.number[s, k]
            for j, q in enumerate(grid.columns(x)):
                right = grid.number[k, q]
                todo.append((max(has[d, left], has[d, right]), k, j, left, right, q))
        todo.sort()
        for at, step in enumerate(calls):
            fit = [one for one in todo if one[0] <= step]
            if step < steps + 1:
                alike = {j: sum(one[2] == j for one in fit) for j in range(grid.width)}
                fit.sort(key=lambda one: (-alike[one[2]], one[2], one[0]))
                fit = fit[:CAP]
            fit.sort(key=lambda one: (one[2], one[0]))
            todo = [one for one in todo if one not in fit]
            lists[at][d] = [one[1:] for one in fit]
        assert not todo
    return calls, lists


@functools.lru_cache(None)
def plan(src, rcv):
    grid = Grid(src, rcv)
    best = None
    for seed in range(240 if grid.count <= 16 else 1):
        got = plan_moves(grid, seed)
        calls, work = plan_products(grid, *got)
        late = [max(len(per) for per in lists) for lists in work[-3:]]
        cost = 46 * len(got[0]) + 4 * (late[2] + max(late[1] - 5, 0) + max(late[0] - 5, 0))
        if best is None or cost < best[0]:
            best = cost, got, calls, work
    (moves, has, flip), calls, work = best[1:]
    n, ways, steps = grid.count, len(grid.ways), len(moves)
    slot = np.full((n, len(grid.tiles)), -1)
    used = np.zeros(n, int)
    for d in range(n):
        s, x = divmod(d, rcv)
        for q in grid.columns(x):
            slot[d, grid.number[s, q]] = used[d]
            used[d] += 1
    keep = np.zeros((n, len(grid.tiles)), bool)
    for step, now in enumerate(moves):
        for way, u, v, item in now:
            keep[u, item] |= has[u, item] < step
    send = np.full((steps + 2, ways, n), -1)
    take = np.full((steps + 2, ways, n), -1)
    turn = np.zeros((steps + 2, ways, n), int)
    use = np.zeros((n, len(grid.tiles)), bool)
    rows = np.zeros((n, len(grid.tiles)), int)
    for d in range(n):
        s, x = divmod(d, rcv)
        for i in range(len(grid.tiles)):
            p, q = grid.tiles[i]
            rows[d, i] = s if s in (p, q) else p if q in grid.columns(x) else q
            use[d, i] = s in (p, q) or p in grid.columns(x) or q in grid.columns(x)
    place = slot.copy()
    other = np.full((n, len(grid.tiles)), -1)
    placed = used.copy()
    both = np.zeros((n, len(grid.tiles)), bool)
    for d in range(n):
        for i in range(len(grid.tiles)):
            p, q = grid.tiles[i]
            s, at = d // rcv, grid.columns(d % rcv)
            both[d, i] = p != q and (p in at and q in at or s in (p, q) and s in at)
            if place[d, i] >= 0 and both[d, i]:
                other[d, i] = placed[d]
                placed[d] += 1
    perms = [[[] for _ in range(ways)] for _ in range(steps)]
    for step, now in enumerate(moves):
        for way, u, v, item in now:
            if keep[v, item]:
                slot[v, item] = used[v]
                used[v] += 1
            take[step + 2, way, v] = item
            if use[v, item]:
                place[v, item] = placed[v]
                placed[v] += 1
                if both[v, item]:
                    other[v, item] = placed[v]
                    placed[v] += 1
                p, q = grid.tiles[item]
                turn[step + 2, way, v] = int(p != q and (rows[v, item] == q) != flip[v, item])
            perms[step][way].append((u, v))
    for step, now in enumerate(moves):
        taken = [way for way in range(ways) if step >= 2 and perms[step - 2][way]]
        for way, u, v, item in now:
            new = [i for i, w in enumerate(taken) if take[step, w, u] == item]
            send[step, way, u] = used.max() + new[0] if new else slot[u, item]
    kept = np.full((steps + 2, ways, n), -1)
    store = np.full((steps + 2, ways, n), -1)
    again = np.full((steps + 2, ways, n), -1)
    for step, now in enumerate(moves):
        for way, u, v, item in now:
            kept[step + 2, way, v] = slot[v, item]
            store[step + 2, way, v] = place[v, item]
            again[step + 2, way, v] = other[v, item]
    lists = [[[] for _ in range(n)] for _ in calls]
    fresh = [set() for _ in range(n)]
    for at, per in enumerate(work):
        for d in range(n):
            s = d // rcv
            for i, (k, j, left, right, q) in enumerate(per[d]):
                begin = i == 0 or per[d][i - 1][1] != j
                end = i + 1 == len(per[d]) or per[d][i + 1][1] != j
                over = other[d, right] if k != q and rows[d, right] != k else place[d, right]
                assert over >= 0
                mode = 0 if not begin else 1 if j in fresh[d] else 2
                fresh[d].add(j)
                group = len({one[1] for one in per[d][: i + 1]}) - 1
                lists[at][d].append((place[d, left], over, j, mode, int(end), group))
    longest = [max(len(one) for one in per) for per in lists]
    table = []
    starts = {"own": 0}
    for q in range(grid.width):
        table.append(np.array([other[d, grid.number[d // rcv, d % rcv * grid.width + q]] for d in range(n)]))
    for step in range(steps + 2):
        starts["route", step] = len(table)
        for what in (take, send, kept, store, turn, again):
            for way in range(ways):
                table.append(what[step, way])
    for at, step in enumerate(calls):
        starts["ops", step] = len(table)
        table.append(np.array([len(lists[at][d]) for d in range(n)]))
        table.append(np.array([lists[at][d][-1][5] + 1 if lists[at][d] else 0 for d in range(n)]))
        for i in range(longest[at]):
            for f in range(FIELDS):
                table.append(np.array([lists[at][d][i][f] if i < len(lists[at][d]) else 0 for d in range(n)]))
    return perms, calls, longest, starts, np.array(table, np.int32).T.copy(), int(used.max()), int(placed.max()), ways


ANY = pl.BlockSpec(memory_space=pl.ANY)


def split(value):
    high = value.astype(jnp.bfloat16)
    return high, (value - high.astype(jnp.float32)).astype(jnp.bfloat16)


def cut(ref, at, out, to, turn):
    tile = ref.shape[-1]
    rows = min(128, tile)
    count = tile // rows

    def block(r):
        return pl.ds(pl.multiple_of(r * rows, rows), rows)

    def straight(i, carry):
        c, r = i // count, lax.rem(i, count)
        out[to, c, 0, block(r), :], out[to, c, 1, block(r), :] = split(ref[at, c, block(r), :])
        return carry

    def across(i, carry):
        c, r = i // count, lax.rem(i, count)
        out[to, c, 0, block(r), :], out[to, c, 1, block(r), :] = split(ref[at, c, :, block(r)].T)
        return carry

    @pl.when(turn == 0)
    def _():
        lax.fori_loop(0, 2 * count, straight, 0)

    @pl.when(turn != 0)
    def _():
        lax.fori_loop(0, 2 * count, across, 0)


def first_kernel(tab, own, buf, cuts, hold, ready, sem, sem_cut):
    tile = buf.shape[-1]
    width = own.shape[-1] // tile

    def load(i):
        for c in range(2):
            yield pltpu.make_async_copy(own.at[0, c, :, pl.ds(i * tile, tile)], hold.at[i, c], sem.at[i, c])

    def store(i):
        return pltpu.make_async_copy(hold.at[i], buf.at[i], sem.at[i, 0])

    def write(i):
        return pltpu.make_async_copy(ready.at[i], cuts.at[i], sem_cut.at[i])

    def again(i):
        return pltpu.make_async_copy(ready.at[width + i], cuts.at[tab[i]], sem_cut.at[width + i])

    for i in range(width):
        for copy in load(i):
            copy.start()
    for i in range(width):
        for copy in load(i):
            copy.wait()
        store(i).start()

    def part(i, carry):
        cut(hold, i, ready, i, 0)
        write(i).start()

        @pl.when(tab[i] >= 0)
        def _():
            cut(hold, i, ready, width + i, 1)
            again(i).start()

        return carry

    lax.fori_loop(0, width, part, 0)
    for i in range(width):
        store(i).wait()
        write(i).wait()
        pl.when(tab[i] >= 0)(lambda: again(i).wait())


def route_kernel(start, ways, taken, sent, slots, tab, *refs):
    got = refs[3 : 3 + len(taken)]
    buf, cuts = refs[3 + len(taken) : 5 + len(taken)]
    outs = refs[6 + len(taken) : 6 + len(taken) + len(sent)]
    hold_in, hold_out, ready, sem_in, sem_out, sem_cut = refs[-6:]

    def load_in(i):
        return pltpu.make_async_copy(got[i], hold_in.at[i], sem_in.at[i])

    def load_out(i, slot):
        return pltpu.make_async_copy(buf.at[slot], hold_out.at[i], sem_out.at[i])

    def store_in(i, slot):
        return pltpu.make_async_copy(hold_in.at[i], buf.at[slot], sem_in.at[i])

    def store_out(i):
        return pltpu.make_async_copy(hold_out.at[i], outs[i], sem_out.at[i])

    def pass_on(i, at):
        return pltpu.make_async_copy(hold_in.at[at], outs[i], sem_out.at[i])

    def write(i, slot):
        return pltpu.make_async_copy(ready.at[i], cuts.at[slot], sem_cut.at[i])

    def again(i):
        at = len(taken) + i
        return pltpu.make_async_copy(ready.at[at], cuts.at[entry(5, taken[i])], sem_cut.at[at])

    def entry(kind, way):
        return tab[start + kind * ways + way]

    to = [entry(0, way) for way in taken]
    of = [entry(1, way) for way in sent]
    keep = [entry(2, way) for way in taken]
    place = [entry(3, way) for way in taken]
    for i, slot in enumerate(of):
        pl.when((slot >= 0) & (slot < slots))(lambda: load_out(i, slot).start())
    for i, slot in enumerate(to):
        pl.when(slot >= 0)(lambda: load_in(i).start())
    for i, slot in enumerate(of):
        @pl.when((slot >= 0) & (slot < slots))
        def _():
            load_out(i, slot).wait()
            store_out(i).start()
    for i, slot in enumerate(to):
        pl.when(slot >= 0)(lambda: load_in(i).wait())
        pl.when(keep[i] >= 0)(lambda: store_in(i, keep[i]).start())
    if taken:
        for i, slot in enumerate(of):
            pl.when(slot >= slots)(lambda: pass_on(i, slot - slots).start())
        for i, way in enumerate(taken):
            @pl.when(place[i] >= 0)
            def _():
                cut(hold_in, i, ready, i, entry(4, way))
                write(i, place[i]).start()

                @pl.when(entry(5, way) >= 0)
                def _():
                    cut(hold_in, i, ready, len(taken) + i, 1 - entry(4, way))
                    again(i).start()
        for i, slot in enumerate(of):
            pl.when(slot >= slots)(lambda: pass_on(i, slot - slots).wait())
    for i, slot in enumerate(of):
        pl.when((slot >= 0) & (slot < slots))(lambda: store_out(i).wait())
    for i in range(len(taken)):
        pl.when(keep[i] >= 0)(lambda: store_in(i, keep[i]).wait())
        pl.when(place[i] >= 0)(lambda: write(i, place[i]).wait())
        pl.when(entry(5, taken[i]) >= 0)(lambda: again(i).wait())


def multiply_kernel(start, first, tab, cuts, *refs):
    if first:
        out, *scratch = refs
        before = None
    else:
        before, out, *scratch = refs
    total, left, right, sem_get, sem_put, sem_l, sem_r = scratch
    tile = cuts.shape[-1]
    count = tab[start]

    def field(i, f):
        return tab[start + 2 + FIELDS * i + f]

    def columns(ref, c, j):
        return ref.at[0, c, :, pl.ds(pl.multiple_of(j * tile, tile), tile)]

    def fetch(i):
        now = lax.rem(i, 2)
        yield pltpu.make_async_copy(cuts.at[field(i, 0)], left.at[now], sem_l.at[now])
        yield pltpu.make_async_copy(cuts.at[field(i, 1)], right.at[now], sem_r.at[now])

    def get(i):
        at = lax.rem(field(i, 5), 2)
        for c in range(2):
            yield pltpu.make_async_copy(columns(before, c, field(i, 2)), total.at[at, c], sem_get.at[2 * at + c])

    def put(group, j):
        at = lax.rem(group, 2)
        for c in range(2):
            yield pltpu.make_async_copy(total.at[at, c], columns(out, c, j), sem_put.at[2 * at + c])

    def begin(i):
        for copy in fetch(i):
            copy.start()

        @pl.when((field(i, 3) > 0) & (field(i, 5) > 1))
        def _():
            for copy in put(field(i, 5), 0):
                copy.wait()

        if not first:
            @pl.when(field(i, 3) == 1)
            def _():
                for copy in get(i):
                    copy.start()

    @pl.when(count > 0)
    def _():
        begin(0)

    def op(i, carry):
        now = lax.rem(i, 2)
        at = lax.rem(field(i, 5), 2)
        if not first:
            @pl.when(field(i, 3) == 1)
            def _():
                for copy in get(i):
                    copy.wait()

        @pl.when(field(i, 3) == 2)
        def _():
            total[at] = jnp.zeros((2, tile, tile), jnp.float32)

        for copy in fetch(i):
            copy.wait()

        @pl.when(i + 1 < count)
        def _():
            begin(i + 1)

        def product(step, carry):
            cl, c = step // 2, lax.rem(step, 2)
            to = cl + c - 2 * cl * c
            sign = (1 - 2 * cl * c).astype(jnp.float32)
            one = jnp.concatenate([left[now, cl, 0], left[now, cl, 0], left[now, cl, 1]], axis=1)
            two = jnp.concatenate([right[now, c, 0], right[now, c, 1], right[now, c, 0]], axis=0)
            total[at, to] += sign * jnp.dot(one, two, preferred_element_type=jnp.float32)
            return carry

        lax.fori_loop(0, 4, product, 0)

        @pl.when(field(i, 4) == 1)
        def _():
            for copy in put(field(i, 5), field(i, 2)):
                copy.start()

        return carry

    lax.fori_loop(0, count, op, 0)
    for back in (2, 1):
        @pl.when(tab[start + 1] >= back)
        def _():
            for copy in put(tab[start + 1] - back, 0):
                copy.wait()


def local(src, rcv, recorded):
    perms, calls, longest, starts, table, slots, places, ways = plan(src, rcv)
    steps = len(perms)
    tile = recorded.shape[2]
    me = lax.axis_index("src") * rcv + lax.axis_index("rcv")
    tab = lax.dynamic_index_in_dim(jnp.asarray(table), me, 0, keepdims=False)
    chunk = jax.ShapeDtypeStruct((2, tile, tile), jnp.float32)
    buf_shape = jax.ShapeDtypeStruct((slots, 2, tile, tile), jnp.float32)
    cut_shape = jax.ShapeDtypeStruct((places, 2, 2, tile, tile), jnp.bfloat16)
    acc_shape = jax.ShapeDtypeStruct(recorded.shape, jnp.float32)
    width = recorded.shape[3] // tile

    def call(kernel, ins, outs, scratch, aliases, cost, limit=None):
        return pl.pallas_call(
            kernel,
            out_shape=outs,
            grid_spec=pltpu.PrefetchScalarGridSpec(
                num_scalar_prefetch=1,
                grid=(),
                in_specs=[ANY] * len(ins),
                out_specs=[ANY] * len(outs),
                scratch_shapes=scratch,
            ),
            input_output_aliases=aliases,
            cost_estimate=pl.CostEstimate(flops=cost[0], bytes_accessed=cost[1], transcendentals=0),
            compiler_params=pltpu.CompilerParams(vmem_limit_bytes=limit),
        )(tab, *ins)

    size = tile * tile * 8
    buf, cuts = call(
        first_kernel,
        [recorded],
        [buf_shape, cut_shape],
        [
            pltpu.VMEM((width, 2, tile, tile), jnp.float32),
            pltpu.VMEM((2 * width, 2, 2, tile, tile), jnp.bfloat16),
            pltpu.SemaphoreType.DMA((width, 2)),
            pltpu.SemaphoreType.DMA((2 * width,)),
        ],
        {},
        (0, 3 * width * size),
        48 << 20,
    )
    acc = None
    flight = {}
    for step in range(steps + 2):
        got = flight.pop(step - 2, {})
        taken = sorted(got)
        sent = [way for way in range(ways) if step < steps and perms[step][way]]
        state = [buf, cuts] if acc is None else [buf, cuts, acc]
        m = len(state)
        kernel = functools.partial(
            route_kernel if m == 3 else first_route, starts["route", step], ways, taken, sent, slots
        )
        done = call(
            kernel,
            state + [got[way] for way in taken],
            [buf_shape, cut_shape, acc_shape][:m] + [chunk] * len(sent),
            [
                pltpu.VMEM((max(len(taken), 1), 2, tile, tile), jnp.float32),
                pltpu.VMEM((max(len(sent), 1), 2, tile, tile), jnp.float32),
                pltpu.VMEM((max(2 * len(taken), 1), 2, 2, tile, tile), jnp.bfloat16),
                pltpu.SemaphoreType.DMA((max(len(taken), 1),)),
                pltpu.SemaphoreType.DMA((max(len(sent), 1),)),
                pltpu.SemaphoreType.DMA((max(2 * len(taken), 1),)),
            ],
            {1 + i: i for i in range(m)},
            (0, (3 * len(taken) + 2 * len(sent)) * size),
            50 << 20,
        )
        buf, cuts = done[:2]
        if m == 3:
            acc = done[2]
        flight[step] = {
            way: lax.ppermute(value, AXES, perms[step][way]) for way, value in zip(sent, done[m:])
        }
        if step in calls and longest[calls.index(step)]:
            ops = longest[calls.index(step)]
            first = acc is None
            (acc,) = call(
                functools.partial(multiply_kernel, starts["ops", step], first),
                [cuts] if first else [cuts, acc],
                [acc_shape],
                [
                    pltpu.VMEM((2, 2, tile, tile), jnp.float32),
                    pltpu.VMEM((2, 2, 2, tile, tile), jnp.bfloat16),
                    pltpu.VMEM((2, 2, 2, tile, tile), jnp.bfloat16),
                    pltpu.SemaphoreType.DMA((4,)),
                    pltpu.SemaphoreType.DMA((4,)),
                    pltpu.SemaphoreType.DMA((2,)),
                    pltpu.SemaphoreType.DMA((2,)),
                ],
                {} if first else {2: 0},
                (ops * 24 * tile**3, ops * 3 * size),
                32 << 20,
            )
    return acc


def first_route(start, ways, taken, sent, slots, tab, *refs):
    n = 2 + len(taken)
    route_kernel(start, ways, taken, sent, slots, tab, *refs[:2], None, *refs[2 : n + 2], None, *refs[n + 2 :])


def solution(mesh):
    src, rcv = mesh.shape["src"], mesh.shape["rcv"]
    return jax.shard_map(
        functools.partial(local, src, rcv),
        mesh=mesh,
        in_specs=(P("freq", None, "src", "rcv"),),
        out_specs=P("freq", None, "src", "rcv"),
        check_vma=False,
    )
```

time: 1740 us -> 523 us (0.30)
  waiting for transfers between devices: 1470 us -> 141 us
  Pallas kernels: 0 us -> 274 us
  matrix products: 245 us -> 0 us
  starting transfers between devices: 0.04 us -> 102 us
    all_gather x2 -> x0, waiting for transfers between devices: 1470 us -> none  [the longest x1 1270 us: local(): lax.all_gather(recorded, 'src', axis=2, tiled=True)]
    pallas_call x0 -> x20, Pallas kernels: none -> 274 us  [call(): pl.pallas_call(kernel, out_shape=outs, grid_spec=pltpu.PrefetchScalarGrid...]
    dot_general x4 -> x0, matrix products: 245 us -> none  [multiply(): return jnp.einsum(form, first, second, precision=highest)]
    ppermute x0 -> x36, waiting for transfers between devices: none -> 141 us  [local(): lax.ppermute(value, AXES, perms[step][way])]
    ppermute x0 -> x36, starting transfers between devices: none -> 102 us  [local(): lax.ppermute(value, AXES, perms[step][way])]
  transfers between devices with their start and end apart: 2 -> 36, of which waited for: 2 -> 14; matrix products, arithmetic and copies ran while one was open for 0% -> 0% of each run, Pallas kernels for 0% -> 45%
where the time goes in v2:
time: 523 us; the launch traced here: 522 us
  Pallas kernels  274 us (52%)
  waiting for transfers between devices  141 us (27%)
  starting transfers between devices  102 us (20%)
    pallas_call x20, Pallas kernels, call(): pl.pallas_call(kernel, out_shape=outs, grid_spec=pltpu.PrefetchScalarGrid...  274 us
    ppermute x36, waiting for transfers between devices, local(): lax.ppermute(value, AXES, perms[step][way])  141 us
    ppermute x36, starting transfers between devices, local(): lax.ppermute(value, AXES, perms[step][way])  102 us
  transfers between devices with their start and end apart: 36, of which 14 were waited for; matrix products, arithmetic and copies ran while one was open for 0% of the time, Pallas kernels for 45%

profile of v2, /device:TPU:6, one launch (start us, length us, event | category | flops | bytes accessed | tf_op | source)
XLA Modules:
  0.0 521.8 jit_solution(5645143485630579521)
XLA Ops:
  0.7 10.3 %shard_map.28 = (f32[13,2,512,512]{3,2,1,0:T(8,128)}, bf16[36,2,2,512,512]{4,3,2,1,0:T(8,128)(2,1)}) custom-call(s32[536]{0:T(1024)S(1)} %dynamic-slice_reduce_fusion.tab, f32[1,2,512,2048]{3,2,1,0:T(8,128)} %own.1), custom_call_target="tpu_custom_call" | custom-call | bytes 25165824 | tf_op jit(solution)/shard_map/pallas_call | solution.py:504
  11.1 4.8 shard_map.29
  15.9 5.5 %collective-permute-start = (f32[2,512,512]{2,1,0:T(8,128)S(1)}, f32[2,512,512]{2,1,0:T(8,128)S(1)}, u32[]{:S(2)}, u32[]{:S(2)}) collective-permute-start(f32[2,512,512]{2,1,0:T(8,128)S(1)} %get-tuple-element.77), channel_id=1, source_target_pairs={{20,28},{16,24},{18,26},{22,30},{2,10},{12,20},{8,16},{6,14},{14,2... | collective-permute-start | bytes 6291464 | tf_op jit(solution)/shard_map/ppermute | solution.py:565
  21.4 1.3 collective-permute-start.1
  22.9 3.2 collective-permute-start.3
  26.1 5.4 %shard_map.30 = (f32[13,2,512,512]{3,2,1,0:T(8,128)}, bf16[36,2,2,512,512]{4,3,2,1,0:T(8,128)(2,1)}, f32[2,512,512]{2,1,0:T(8,128)S(1)}, f32[2,512,512]{2,1,0:T(...) custom-call(s32[536]{0:T(1024)S(1)} %dynamic-slice_reduce_fusion.tab, ...), custom_call_target="tpu_custom_call", output_to_operand_aliasing={{0}: (1, {}), {1}: (2, {})} | custom-call | bytes 16777216 | tf_op jit(solution)/shard_map/pallas_call | solution.py:504
  31.5 5.7 %collective-permute-start.4 = (f32[2,512,512]{2,1,0:T(8,128)S(1)}, f32[2,512,512]{2,1,0:T(8,128)S(1)}, u32[]{:S(2)}, u32[]{:S(2)}) collective-permute-start(f32[2,512,512]{2,1,0:T(8,128)S(1)} %get-tuple-element.83), channel_id=1, source_target_pairs={{20,28},{16,24},{18,26},{22,30},{2,10},{12,20},{6,14},{8,16},{14,2... | collective-permute-start | bytes 6291464 | tf_op jit(solution)/shard_map/ppermute | solution.py:565
  37.3 30.0 %collective-permute-done.refs_2_ = f32[2,512,512]{2,1,0:T(8,128)S(1)} collective-permute-done((f32[2,512,512]{2,1,0:T(8,128)S(1)}, f32[2,512,512]{2,1,0:T(8,128)S(1)}, u32[]{:S(2)}, u32[]{:S(2)}) %collective-permute-start) | collective-permute-done | bytes 2097184 | tf_op jit(solution)/shard_map/ppermute | solution.py:565
  67.3 1.3 collective-permute-start.5
  68.6 4.8 collective-permute-done.1.refs_3_
  74.0 0.8 copy-done.16
  74.7 10.9 %shard_map.31 = (f32[13,2,512,512]{3,2,1,0:T(8,128)}, bf16[36,2,2,512,512]{4,3,2,1,0:T(8,128)(2,1)}, f32[2,512,512]{2,1,0:T(8,128)S(1)}, f32[2,512,512]{2,1,0:T(...) custom-call(s32[536]{0:T(1024)S(1)} %dynamic-slice_reduce_fusion.tab, ...), custom_call_target="tpu_custom_call", output_to_operand_aliasing={{0}: (1, {}), {1}: (2, {})} | custom-call | bytes 41943040 | tf_op jit(solution)/shard_map/pallas_call | solution.py:504
  85.6 4.5 collective-permute-start.8
  90.1 22.1 %collective-permute-done.4.refs_2_ = f32[2,512,512]{2,1,0:T(8,128)S(1)} collective-permute-done((f32[2,512,512]{2,1,0:T(8,128)S(1)}, f32[2,512,512]{2,1,0:T(8,128)S(1)}, u32[]{:S(2)}, u32[]{:S(2)}) %collective-permute-start.4) | collective-permute-done | bytes 2097184 | tf_op jit(solution)/shard_map/ppermute | solution.py:565
  112.2 1.3 collective-permute-start.9
  113.5 4.8 collective-permute-done.5.refs_3_
  118.3 2.3 collective-permute-done.6.refs_4_
  120.6 0.9 collective-permute-start.11
  121.9 8.8 %shard_map.32 = (f32[13,2,512,512]{3,2,1,0:T(8,128)}, bf16[36,2,2,512,512]{4,3,2,1,0:T(8,128)(2,1)}, f32[2,512,512]{2,1,0:T(8,128)S(1)}, f32[2,512,512]{2,1,0:T(...) custom-call(s32[536]{0:T(1024)S(1)} %dynamic-slice_reduce_fusion.tab, ...), custom_call_target="tpu_custom_call", output_to_operand_aliasing={{0}: (1, {}), {1}: (2, {})} | custom-call | bytes 41943040 | tf_op jit(solution)/shard_map/pallas_call | solution.py:504
  130.7 5.3 %collective-permute-start.12 = (f32[2,512,512]{2,1,0:T(8,128)S(1)}, f32[2,512,512]{2,1,0:T(8,128)S(1)}, u32[]{:S(2)}, u32[]{:S(2)}) collective-permute-start(f32[2,512,512]{2,1,0:T(8,128)S(1)} %get-tuple-element.96), channel_id=1, source_target_pairs={{16,24},{20,28},{18,26},{22,30},{12,20},{8,16},{6,14},{2,10},{4,12... | collective-permute-start | bytes 6291464 | tf_op jit(solution)/shard_map/ppermute | solution.py:565
  136.0 21.2 %collective-permute-done.8.refs_3_ = f32[2,512,512]{2,1,0:T(8,128)S(1)} collective-permute-done((f32[2,512,512]{2,1,0:T(8,128)S(1)}, f32[2,512,512]{2,1,0:T(8,128)S(1)}, u32[]{:S(2)}, u32[]{:S(2)}) %collective-permute-start.8) | collective-permute-done | bytes 2097184 | tf_op jit(solution)/shard_map/ppermute | solution.py:565
  157.2 1.3 collective-permute-start.13
  158.4 4.8 collective-permute-done.9.refs_4_
  163.3 2.4 collective-permute-done.10.refs_5_
  165.6 0.9 collective-permute-start.15
  166.6 29.5 %shard_map.33.refs_2_ = f32[1,2,512,2048]{3,2,1,0:T(8,128)} custom-call(s32[536]{0:T(1024)S(1)} %dynamic-slice_reduce_fusion.tab, bf16[36,2,2,512,512]{4,3,2,1,0:T(8,128)(2,1)} %get-tuple-element.88.cuts.refs_1_), custom_call_target="tpu_custom_call" | custom-call | flops 19327352832 | bytes 37748736 | tf_op jit(solution)/shard_map/pallas_call | solution.py:504
  196.1 9.4 %shard_map.34 = (f32[13,2,512,512]{3,2,1,0:T(8,128)}, bf16[36,2,2,512,512]{4,3,2,1,0:T(8,128)(2,1)}, f32[1,2,512,2048]{3,2,1,0:T(8,128)}, f32[2,512,512]{2,1,0:T...) custom-call(s32[536]{0:T(1024)S(1)} %dynamic-slice_reduce_fusion.tab, ...), custom_call_target="tpu_custom_call", output_to_operand_aliasing={{0}: (1, {}), {1}: (2, {}), {2}: (3, {})} | custom-call | bytes 41943040 | tf_op jit(solution)/shard_map/pallas_call | solution.py:504
  205.5 2.0 collective-permute-start.16
  207.5 16.7 %shard_map.35.refs_2_ = f32[1,2,512,2048]{3,2,1,0:T(8,128)} custom-call(s32[536]{0:T(1024)S(1)} %dynamic-slice_reduce_fusion.tab, bf16[36,2,2,512,512]{4,3,2,1,0:T(8,128)(2,1)} %get-tuple-element.94.cuts.refs_1_, f32[1,2,512,2048]{3,2,1,0:T(8,128)} %get-tuple-element.95.refs_0_), custom_call_target="tpu_custom_call", output_to_operand_aliasing={{}: (2, {})} | custom-call | flops 19327352832 | bytes 37748736 | tf_op jit(solution)/shard_map/pallas_call | solution.py:504
  224.3 1.3 collective-permute-start.17
  225.7 16.3 %collective-permute-start.19 = (f32[2,512,512]{2,1,0:T(8,128)}, f32[2,512,512]{2,1,0:T(8,128)}, u32[]{:S(2)}, u32[]{:S(2)}) collective-permute-start(f32[2,512,512]{2,1,0:T(8,128)} %get-tuple-element.106), channel_id=1, source_target_pairs={{4,6},{0,2},{30,28},{26,24},{24,26},{28,30},{6,4},{2,0},{8,10},{12... | collective-permute-start | bytes 6291464 | tf_op jit(solution)/shard_map/ppermute | solution.py:565
  242.0 9.4 %shard_map.36 = (f32[13,2,512,512]{3,2,1,0:T(8,128)}, bf16[36,2,2,512,512]{4,3,2,1,0:T(8,128)(2,1)}, f32[1,2,512,2048]{3,2,1,0:T(8,128)}, f32[2,512,512]{2,1,0:T...) custom-call(s32[536]{0:T(1024)S(1)} %dynamic-slice_reduce_fusion.tab, ...), custom_call_target="tpu_custom_call", output_to_operand_aliasing={{0}: (1, {}), {1}: (2, {}), {2}: (3, {})} | custom-call | bytes 41943040 | tf_op jit(solution)/shard_map/pallas_call | solution.py:504
  251.4 5.9 %collective-permute-start.20 = (f32[2,512,512]{2,1,0:T(8,128)S(1)}, f32[2,512,512]{2,1,0:T(8,128)S(1)}, u32[]{:S(2)}, u32[]{:S(2)}) collective-permute-start(f32[2,512,512]{2,1,0:T(8,128)S(1)} %get-tuple-element.110), channel_id=1, source_target_pairs={{16,24},{20,28},{18,26},{22,30},{2,10},{6,14},{8,16},{12,20},{0,8}... | collective-permute-start | bytes 6291464 | tf_op jit(solution)/shard_map/ppermute | solution.py:565
  257.3 1.3 collective-permute-start.21
  258.6 23.2 %shard_map.37.refs_2_ = f32[1,2,512,2048]{3,2,1,0:T(8,128)} custom-call(s32[536]{0:T(1024)S(1)} %dynamic-slice_reduce_fusion.tab, bf16[36,2,2,512,512]{4,3,2,1,0:T(8,128)(2,1)} %get-tuple-element.101.cuts.refs_1_, f32[1,2,512,2048]{3,2,1,0:T(8,128)} %get-tuple-element.102.refs_0_), custom_call_target="tpu_custom_call", output_to_operand_aliasing={{}: (2, {})} | custom-call | flops 19327352832 | bytes 37748736 | tf_op jit(solution)/shard_map/pallas_call | solution.py:504
  281.8 6.2 %collective-permute-done.17.refs_4_ = f32[2,512,512]{2,1,0:T(8,128)} collective-permute-done((f32[2,512,512]{2,1,0:T(8,128)}, f32[2,512,512]{2,1,0:T(8,128)}, u32[]{:S(2)}, u32[]{:S(2)}) %collective-permute-start.17) | collective-permute-done | bytes 2097184 | tf_op jit(solution)/shard_map/ppermute | solution.py:565
  288.0 5.1 collective-permute-start.22
  293.1 3.1 collective-permute-start.23
  296.3 8.7 %shard_map.38 = (f32[13,2,512,512]{3,2,1,0:T(8,128)}, bf16[36,2,2,512,512]{4,3,2,1,0:T(8,128)(2,1)}, f32[1,2,512,2048]{3,2,1,0:T(8,128)}, f32[2,512,512]{2,1,0:T...) custom-call(s32[536]{0:T(1024)S(1)} %dynamic-slice_reduce_fusion.tab, ...), custom_call_target="tpu_custom_call", output_to_operand_aliasing={{0}: (1, {}), {1}: (2, {}), {2}: (3, {})} | custom-call | bytes 41943040 | tf_op jit(solution)/shard_map/pallas_call | solution.py:504
  305.0 0.8 collective-permute-start.24
  305.8 1.3 collective-permute-start.25
  307.1 25.7 %collective-permute-done.21.refs_4_ = f32[2,512,512]{2,1,0:T(8,128)S(1)} collective-permute-done((f32[2,512,512]{2,1,0:T(8,128)}, f32[2,512,512]{2,1,0:T(8,128)S(1)}, u32[]{:S(2)}, u32[]{:S(2)}) %collective-permute-start.21) | collective-permute-done | bytes 2097184 | tf_op jit(solution)/shard_map/ppermute | solution.py:565
  332.8 3.5 collective-permute-start.26
  336.3 16.7 %shard_map.39.refs_2_ = f32[1,2,512,2048]{3,2,1,0:T(8,128)} custom-call(s32[536]{0:T(1024)S(1)} %dynamic-slice_reduce_fusion.tab, bf16[36,2,2,512,512]{4,3,2,1,0:T(8,128)(2,1)} %get-tuple-element.108.cuts.refs_1_, f32[1,2,512,2048]{3,2,1,0:T(8,128)} %get-tuple-element.109.refs_0_), custom_call_target="tpu_custom_call", output_to_operand_aliasing={{}: (2, {})} | custom-call | flops 19327352832 | bytes 37748736 | tf_op jit(solution)/shard_map/pallas_call | solution.py:504
  353.1 15.6 %collective-permute-start.27 = (f32[2,512,512]{2,1,0:T(8,128)}, f32[2,512,512]{2,1,0:T(8,128)}, u32[]{:S(2)}, u32[]{:S(2)}) collective-permute-start(f32[2,512,512]{2,1,0:T(8,128)} %get-tuple-element.120), channel_id=1, source_target_pairs={{30,28},{0,2},{4,6},{26,24},{2,0},{6,4},{28,30},{24,26},{8,10},{31... | collective-permute-start | bytes 6291464 | tf_op jit(solution)/shard_map/ppermute | solution.py:565
  368.7 9.2 %shard_map.40 = (f32[13,2,512,512]{3,2,1,0:T(8,128)}, bf16[36,2,2,512,512]{4,3,2,1,0:T(8,128)(2,1)}, f32[1,2,512,2048]{3,2,1,0:T(8,128)}, f32[2,512,512]{2,1,0:T...) custom-call(s32[536]{0:T(1024)S(1)} %dynamic-slice_reduce_fusion.tab, ...), custom_call_target="tpu_custom_call", output_to_operand_aliasing={{0}: (1, {}), {1}: (2, {}), {2}: (3, {})} | custom-call | bytes 41943040 | tf_op jit(solution)/shard_map/pallas_call | solution.py:504
  377.9 0.8 collective-permute-start.28
  378.7 1.3 collective-permute-start.29
  380.0 2.7 collective-permute-start.30
  383.2 1.3 collective-permute-start.31
  384.5 26.0 %shard_map.41.refs_2_ = f32[1,2,512,2048]{3,2,1,0:T(8,128)} custom-call(s32[536]{0:T(1024)S(1)} %dynamic-slice_reduce_fusion.tab, bf16[36,2,2,512,512]{4,3,2,1,0:T(8,128)(2,1)} %get-tuple-element.115.cuts.refs_1_, f32[1,2,512,2048]{3,2,1,0:T(8,128)} %get-tuple-element.116.refs_0_), custom_call_target="tpu_custom_call", output_to_operand_aliasing={{}: (2, {})} | custom-call | flops 19327352832 | bytes 37748736 | tf_op jit(solution)/shard_map/pallas_call | solution.py:504
  410.5 5.1 collective-permute-done.27.refs_6_
  415.5 7.9 %shard_map.42 = (f32[13,2,512,512]{3,2,1,0:T(8,128)}, bf16[36,2,2,512,512]{4,3,2,1,0:T(8,128)(2,1)}, f32[1,2,512,2048]{3,2,1,0:T(8,128)}, f32[2,512,512]{2,1,0:T...) custom-call(s32[536]{0:T(1024)S(1)} %dynamic-slice_reduce_fusion.tab, ...), custom_call_target="tpu_custom_call", output_to_operand_aliasing={{0}: (1, {}), {1}: (2, {}), {2}: (3, {})} | custom-call | bytes 41943040 | tf_op jit(solution)/shard_map/pallas_call | solution.py:504
  423.4 0.8 collective-permute-start.32
  424.3 1.3 collective-permute-start.33
  425.6 4.2 collective-permute-start.34
  429.8 1.3 collective-permute-start.35
  431.1 18.0 %shard_map.43.refs_2_ = f32[1,2,512,2048]{3,2,1,0:T(8,128)} custom-call(s32[536]{0:T(1024)S(1)} %dynamic-slice_reduce_fusion.tab, bf16[36,2,2,512,512]{4,3,2,1,0:T(8,128)(2,1)} %get-tuple-element.122.cuts.refs_1_, f32[1,2,512,2048]{3,2,1,0:T(8,128)} %get-tuple-element.123.refs_0_), custom_call_target="tpu_custom_call", output_to_operand_aliasing={{}: (2, {})} | custom-call | flops 12884901888 | bytes 25165824 | tf_op jit(solution)/shard_map/pallas_call | solution.py:504
  449.1 11.4 %collective-permute-done.31.refs_6_ = f32[2,512,512]{2,1,0:T(8,128)} collective-permute-done((f32[2,512,512]{2,1,0:T(8,128)}, f32[2,512,512]{2,1,0:T(8,128)}, u32[]{:S(2)}, u32[]{:S(2)}) %collective-permute-start.31) | collective-permute-done | bytes 2097184 | tf_op jit(solution)/shard_map/ppermute | solution.py:565
  460.5 9.4 %shard_map.44 = (f32[13,2,512,512]{3,2,1,0:T(8,128)}, bf16[36,2,2,512,512]{4,3,2,1,0:T(8,128)(2,1)}, f32[1,2,512,2048]{3,2,1,0:T(8,128)}) custom-call(s32[536]{0:T(1024)S(1)} %dynamic-slice_reduce_fusion.tab, f32[13,2,512,512]{3,2,1,0:T(8,128)} %get-tuple-element.121.refs_0_, ...), custom_call_target="tpu_custom_call", output_to_operand_aliasing={{0}: (1, {}), {1}: (2, {}), {2}: (3, {})} | custom-call | bytes 25165824 | tf_op jit(solution)/shard_map/pallas_call | solution.py:504
  469.9 24.7 %shard_map.45.refs_2_ = f32[1,2,512,2048]{3,2,1,0:T(8,128)} custom-call(s32[536]{0:T(1024)S(1)} %dynamic-slice_reduce_fusion.tab, bf16[36,2,2,512,512]{4,3,2,1,0:T(8,128)(2,1)} %get-tuple-element.129.cuts.refs_1_, f32[1,2,512,2048]{3,2,1,0:T(8,128)} %get-tuple-element.130.refs_0_), custom_call_target="tpu_custom_call", output_to_operand_aliasing={{}: (2, {})} | custom-call | flops 16106127360 | bytes 31457280 | tf_op jit(solution)/shard_map/pallas_call | solution.py:504
  494.8 1.2 copy-done.10
  496.6 7.0 %shard_map.46 = (f32[13,2,512,512]{3,2,1,0:T(8,128)}, bf16[36,2,2,512,512]{4,3,2,1,0:T(8,128)(2,1)}, f32[1,2,512,2048]{3,2,1,0:T(8,128)}) custom-call(s32[536]{0:T(1024)S(1)} %dynamic-slice_reduce_fusion.tab, f32[13,2,512,512]{3,2,1,0:T(8,128)} %get-tuple-element.128.refs_0_, ...), custom_call_target="tpu_custom_call", output_to_operand_aliasing={{0}: (1, {}), {1}: (2, {}), {2}: (3, {})} | custom-call | bytes 25165824 | tf_op jit(solution)/shard_map/pallas_call | solution.py:504
  503.6 18.0 %shard_map.47 = f32[1,2,512,2048]{3,2,1,0:T(8,128)} custom-call(s32[536]{0:T(1024)S(1)} %dynamic-slice_reduce_fusion.tab, bf16[36,2,2,512,512]{4,3,2,1,0:T(8,128)(2,1)} %get-tuple-element.135.cuts, f32[1,2,512,2048]{3,2,1,0:T(8,128)} %get-tuple-element.136.refs_0_), custom_call_target="tpu_custom_call", output_to_operand_aliasing={{}: (2, {})} | custom-call | flops 9663676416 | bytes 18874368 | tf_op jit(solution)/shard_map/pallas_call | solution.py:504
  (63 shorter events, 3.2 us)
Async XLA Ops:
  15.9 51.4 %collective-permute-start = (f32[2,512,512]{2,1,0:T(8,128)S(1)}, f32[2,512,512]{2,1,0:T(8,128)S(1)}, u32[]{:S(2)}, u32[]{:S(2)}) collective-permute-start(f32[2,512,512]{2,1,0:T(8,128)S(1)} %get-tuple-element.77), channel_id=1, source_target_pairs={{20,28},{16,24},{18,26},{22,30},{2,10},{12,20},{8,16},{6,14},{14,2... | collective-permute-start | bytes 6291464 | tf_op jit(solution)/shard_map/ppermute | solution.py:565
  21.4 52.0 %collective-permute-start.1 = (f32[2,512,512]{2,1,0:T(8,128)}, f32[2,512,512]{2,1,0:T(8,128)S(1)}, u32[]{:S(2)}, u32[]{:S(2)}) collective-permute-start(f32[2,512,512]{2,1,0:T(8,128)} %get-tuple-element.78), channel_id=1, source_target_pairs={{10,2},{14,6},{12,4},{8,0},{24,16},{18,10},{22,14},{28,20},{16,8},... | collective-permute-start | bytes 6291464 | tf_op jit(solution)/shard_map/ppermute | solution.py:565
  22.7 50.7 %collective-permute-start.2 = (f32[2,512,512]{2,1,0:T(8,128)}, f32[2,512,512]{2,1,0:T(8,128)}, u32[]{:S(2)}, u32[]{:S(2)}) collective-permute-start(f32[2,512,512]{2,1,0:T(8,128)} %get-tuple-element.79), channel_id=1, source_target_pairs={{6,2},{28,24},{2,6},{24,28},{30,26},{0,4},{26,30},{4,0},{16,20},{2... | collective-permute-start | bytes 6291464 | tf_op jit(solution)/shard_map/ppermute | solution.py:565
  22.9 51.1 %collective-permute-start.3 = (f32[2,512,512]{2,1,0:T(8,128)}, f32[2,512,512]{2,1,0:T(8,128)}, u32[]{:S(2)}, u32[]{:S(2)}) collective-permute-start(f32[2,512,512]{2,1,0:T(8,128)} %get-tuple-element.80), channel_id=1, source_target_pairs={{0,2},{4,6},{30,28},{26,24},{28,30},{2,0},{24,26},{6,4},{8,10},{18... | collective-permute-start | bytes 6291464 | tf_op jit(solution)/shard_map/ppermute | solution.py:565
  31.5 80.7 %collective-permute-start.4 = (f32[2,512,512]{2,1,0:T(8,128)S(1)}, f32[2,512,512]{2,1,0:T(8,128)S(1)}, u32[]{:S(2)}, u32[]{:S(2)}) collective-permute-start(f32[2,512,512]{2,1,0:T(8,128)S(1)} %get-tuple-element.83), channel_id=1, source_target_pairs={{20,28},{16,24},{18,26},{22,30},{2,10},{12,20},{6,14},{8,16},{14,2... | collective-permute-start | bytes 6291464 | tf_op jit(solution)/shard_map/ppermute | solution.py:565
  67.3 7.4 %copy-start.15 = (f32[2,512,512]{2,1,0:T(8,128)}, f32[2,512,512]{2,1,0:T(8,128)S(1)}, u32[]{:S(2)}) copy-start(f32[2,512,512]{2,1,0:T(8,128)S(1)} %collective-permute-done.refs_2_) | copy-start | bytes 6291460
  67.3 51.0 %collective-permute-start.5 = (f32[2,512,512]{2,1,0:T(8,128)}, f32[2,512,512]{2,1,0:T(8,128)S(1)}, u32[]{:S(2)}, u32[]{:S(2)}) collective-permute-start(f32[2,512,512]{2,1,0:T(8,128)} %get-tuple-element.84), channel_id=1, source_target_pairs={{14,6},{10,2},{8,0},{12,4},{28,20},{24,16},{22,14},{18,10},{16,8},... | collective-permute-start | bytes 6291464 | tf_op jit(solution)/shard_map/ppermute | solution.py:565
  73.4 1.3 copy-start.16
  73.4 47.2 %collective-permute-start.6 = (f32[2,512,512]{2,1,0:T(8,128)}, f32[2,512,512]{2,1,0:T(8,128)S(1)}, u32[]{:S(2)}, u32[]{:S(2)}) collective-permute-start(f32[2,512,512]{2,1,0:T(8,128)} %get-tuple-element.85), channel_id=1, source_target_pairs={{24,28},{2,6},{28,24},{6,2},{26,30},{0,4},{30,26},{4,0},{10,14},{1... | collective-permute-start | bytes 6291464 | tf_op jit(solution)/shard_map/ppermute | solution.py:565
  73.4 48.1 %collective-permute-start.7 = (f32[2,512,512]{2,1,0:T(8,128)}, f32[2,512,512]{2,1,0:T(8,128)}, u32[]{:S(2)}, u32[]{:S(2)}) collective-permute-start(f32[2,512,512]{2,1,0:T(8,128)} %get-tuple-element.86), channel_id=1, source_target_pairs={{26,24},{30,28},{4,6},{0,2},{24,26},{2,0},{28,30},{6,4},{12,14},{8... | collective-permute-start | bytes 6291464 | tf_op jit(solution)/shard_map/ppermute | solution.py:565
  85.6 71.5 %collective-permute-start.8 = (f32[2,512,512]{2,1,0:T(8,128)S(1)}, f32[2,512,512]{2,1,0:T(8,128)S(1)}, u32[]{:S(2)}, u32[]{:S(2)}) collective-permute-start(f32[2,512,512]{2,1,0:T(8,128)S(1)} %get-tuple-element.89), channel_id=1, source_target_pairs={{16,24},{20,28},{18,26},{22,30},{2,10},{12,20},{8,16},{6,14},{10,1... | collective-permute-start | bytes 6291464 | tf_op jit(solution)/shard_map/ppermute | solution.py:565
  112.2 9.7 %copy-start.12 = (f32[2,512,512]{2,1,0:T(8,128)}, f32[2,512,512]{2,1,0:T(8,128)S(1)}, u32[]{:S(2)}) copy-start(f32[2,512,512]{2,1,0:T(8,128)S(1)} %collective-permute-done.4.refs_2_) | copy-start | bytes 6291460
  112.2 51.0 %collective-permute-start.9 = (f32[2,512,512]{2,1,0:T(8,128)}, f32[2,512,512]{2,1,0:T(8,128)S(1)}, u32[]{:S(2)}, u32[]{:S(2)}) collective-permute-start(f32[2,512,512]{2,1,0:T(8,128)} %get-tuple-element.90), channel_id=1, source_target_pairs={{14,6},{10,2},{8,0},{12,4},{22,14},{28,20},{18,10},{24,16},{20,12}... | collective-permute-start | bytes 6291464 | tf_op jit(solution)/shard_map/ppermute | solution.py:565
  118.3 3.6 copy-start.13
  118.3 47.3 %collective-permute-start.10 = (f32[2,512,512]{2,1,0:T(8,128)}, f32[2,512,512]{2,1,0:T(8,128)}, u32[]{:S(2)}, u32[]{:S(2)}) collective-permute-start(f32[2,512,512]{2,1,0:T(8,128)} %get-tuple-element.91), channel_id=1, source_target_pairs={{6,2},{28,24},{2,6},{24,28},{26,30},{4,0},{30,26},{0,4},{10,14},{1... | collective-permute-start | bytes 6291464 | tf_op jit(solution)/shard_map/ppermute | solution.py:565
  120.6 1.3 copy-start.14
  120.6 75.5 %collective-permute-start.11 = (f32[2,512,512]{2,1,0:T(8,128)}, f32[2,512,512]{2,1,0:T(8,128)}, u32[]{:S(2)}, u32[]{:S(2)}) collective-permute-start(f32[2,512,512]{2,1,0:T(8,128)} %get-tuple-element.92), channel_id=1, source_target_pairs={{4,6},{26,24},{30,28},{0,2},{6,4},{2,0},{28,30},{24,26},{22,20},{1... | collective-permute-start | bytes 6291464 | tf_op jit(solution)/shard_map/ppermute | solution.py:565
  130.7 93.5 %collective-permute-start.12 = (f32[2,512,512]{2,1,0:T(8,128)S(1)}, f32[2,512,512]{2,1,0:T(8,128)S(1)}, u32[]{:S(2)}, u32[]{:S(2)}) collective-permute-start(f32[2,512,512]{2,1,0:T(8,128)S(1)} %get-tuple-element.96), channel_id=1, source_target_pairs={{16,24},{20,28},{18,26},{22,30},{12,20},{8,16},{6,14},{2,10},{4,12... | collective-permute-start | bytes 6291464 | tf_op jit(solution)/shard_map/ppermute | solution.py:565
  157.2 39.0 %copy-start.4 = (f32[2,512,512]{2,1,0:T(8,128)}, f32[2,512,512]{2,1,0:T(8,128)S(1)}, u32[]{:S(2)}) copy-start(f32[2,512,512]{2,1,0:T(8,128)S(1)} %collective-permute-done.8.refs_3_) | copy-start | bytes 6291460
  157.2 68.4 %collective-permute-start.13 = (f32[2,512,512]{2,1,0:T(8,128)}, f32[2,512,512]{2,1,0:T(8,128)S(1)}, u32[]{:S(2)}, u32[]{:S(2)}) collective-permute-start(f32[2,512,512]{2,1,0:T(8,128)} %get-tuple-element.97), channel_id=1, source_target_pairs={{10,2},{14,6},{12,4},{8,0},{18,10},{22,14},{24,16},{28,20},{16,8},... | collective-permute-start | bytes 6291464 | tf_op jit(solution)/shard_map/ppermute | solution.py:565
  163.3 32.9 %copy-start.9 = (f32[2,512,512]{2,1,0:T(8,128)}, f32[2,512,512]{2,1,0:T(8,128)S(1)}, u32[]{:S(2)}) copy-start(f32[2,512,512]{2,1,0:T(8,128)S(1)} %collective-permute-done.9.refs_4_) | copy-start | bytes 6291460
  163.3 62.4 %collective-permute-start.14 = (f32[2,512,512]{2,1,0:T(8,128)}, f32[2,512,512]{2,1,0:T(8,128)}, u32[]{:S(2)}, u32[]{:S(2)}) collective-permute-start(f32[2,512,512]{2,1,0:T(8,128)} %get-tuple-element.98), channel_id=1, source_target_pairs={{28,24},{2,6},{24,28},{6,2},{26,30},{4,0},{0,4},{30,26},{20,16},{1... | collective-permute-start | bytes 6291464 | tf_op jit(solution)/shard_map/ppermute | solution.py:565
  165.6 76.3 %collective-permute-start.15 = (f32[2,512,512]{2,1,0:T(8,128)}, f32[2,512,512]{2,1,0:T(8,128)}, u32[]{:S(2)}, u32[]{:S(2)}) collective-permute-start(f32[2,512,512]{2,1,0:T(8,128)} %get-tuple-element.99), channel_id=1, source_target_pairs={{4,6},{30,28},{0,2},{26,24},{6,4},{28,30},{2,0},{24,26},{22,20},{8... | collective-permute-start | bytes 6291464 | tf_op jit(solution)/shard_map/ppermute | solution.py:565
  205.5 51.7 %collective-permute-start.16 = (f32[2,512,512]{2,1,0:T(8,128)S(1)}, f32[2,512,512]{2,1,0:T(8,128)S(1)}, u32[]{:S(2)}, u32[]{:S(2)}) collective-permute-start(f32[2,512,512]{2,1,0:T(8,128)S(1)} %get-tuple-element.103), channel_id=1, source_target_pairs={{20,28},{16,24},{18,26},{22,30},{6,14},{2,10},{8,16},{12,20},{4,12... | collective-permute-start | bytes 6291464 | tf_op jit(solution)/shard_map/ppermute | solution.py:565
  224.3 17.7 %copy-start.3 = (f32[2,512,512]{2,1,0:T(8,128)}, f32[2,512,512]{2,1,0:T(8,128)S(1)}, u32[]{:S(2)}) copy-start(f32[2,512,512]{2,1,0:T(8,128)S(1)} %collective-permute-done.12.refs_3_) | copy-start | bytes 6291460
  224.3 63.7 %collective-permute-start.17 = (f32[2,512,512]{2,1,0:T(8,128)}, f32[2,512,512]{2,1,0:T(8,128)}, u32[]{:S(2)}, u32[]{:S(2)}) collective-permute-start(f32[2,512,512]{2,1,0:T(8,128)} %get-tuple-element.104), channel_id=1, source_target_pairs={{14,6},{10,2},{12,4},{8,0},{18,10},{24,16},{22,14},{28,20},{20,12}... | collective-permute-start | bytes 6291464 | tf_op jit(solution)/shard_map/ppermute | solution.py:565
  225.6 16.4 %copy-start.7 = (f32[2,512,512]{2,1,0:T(8,128)}, f32[2,512,512]{2,1,0:T(8,128)S(1)}, u32[]{:S(2)}) copy-start(f32[2,512,512]{2,1,0:T(8,128)S(1)} %collective-permute-done.13.refs_4_) | copy-start | bytes 6291460
  225.6 67.5 %collective-permute-start.18 = (f32[2,512,512]{2,1,0:T(8,128)}, f32[2,512,512]{2,1,0:T(8,128)}, u32[]{:S(2)}, u32[]{:S(2)}) collective-permute-start(f32[2,512,512]{2,1,0:T(8,128)} %get-tuple-element.105), channel_id=1, source_target_pairs={{28,24},{24,28},{6,2},{2,6},{0,4},{26,30},{30,26},{4,0},{16,20},{1... | collective-permute-start | bytes 6291464 | tf_op jit(solution)/shard_map/ppermute | solution.py:565
  225.7 70.6 %collective-permute-start.19 = (f32[2,512,512]{2,1,0:T(8,128)}, f32[2,512,512]{2,1,0:T(8,128)}, u32[]{:S(2)}, u32[]{:S(2)}) collective-permute-start(f32[2,512,512]{2,1,0:T(8,128)} %get-tuple-element.106), channel_id=1, source_target_pairs={{4,6},{0,2},{30,28},{26,24},{24,26},{28,30},{6,4},{2,0},{8,10},{12... | collective-permute-start | bytes 6291464 | tf_op jit(solution)/shard_map/ppermute | solution.py:565
  251.4 54.4 %collective-permute-start.20 = (f32[2,512,512]{2,1,0:T(8,128)S(1)}, f32[2,512,512]{2,1,0:T(8,128)S(1)}, u32[]{:S(2)}, u32[]{:S(2)}) collective-permute-start(f32[2,512,512]{2,1,0:T(8,128)S(1)} %get-tuple-element.110), channel_id=1, source_target_pairs={{16,24},{20,28},{18,26},{22,30},{2,10},{6,14},{8,16},{12,20},{0,8}... | collective-permute-start | bytes 6291464 | tf_op jit(solution)/shard_map/ppermute | solution.py:565
  257.3 24.5 %copy-start = (f32[2,512,512]{2,1,0:T(8,128)}, f32[2,512,512]{2,1,0:T(8,128)S(1)}, u32[]{:S(2)}) copy-start(f32[2,512,512]{2,1,0:T(8,128)S(1)} %collective-permute-done.16.refs_3_) | copy-start | bytes 6291460
  257.3 75.5 %collective-permute-start.21 = (f32[2,512,512]{2,1,0:T(8,128)}, f32[2,512,512]{2,1,0:T(8,128)S(1)}, u32[]{:S(2)}, u32[]{:S(2)}) collective-permute-start(f32[2,512,512]{2,1,0:T(8,128)} %get-tuple-element.111), channel_id=1, source_target_pairs={{10,2},{14,6},{8,0},{12,4},{24,16},{18,10},{22,14},{28,20},{26,18}... | collective-permute-start | bytes 6291464 | tf_op jit(solution)/shard_map/ppermute | solution.py:565
  288.0 65.1 %collective-permute-start.22 = (f32[2,512,512]{2,1,0:T(8,128)}, f32[2,512,512]{2,1,0:T(8,128)}, u32[]{:S(2)}, u32[]{:S(2)}) collective-permute-start(f32[2,512,512]{2,1,0:T(8,128)} %get-tuple-element.112), channel_id=1, source_target_pairs={{28,24},{6,2},{24,28},{2,6},{4,0},{30,26},{26,30},{0,4},{16,20},{2... | collective-permute-start | bytes 6291464 | tf_op jit(solution)/shard_map/ppermute | solution.py:565
  293.1 75.6 %collective-permute-start.23 = (f32[2,512,512]{2,1,0:T(8,128)}, f32[2,512,512]{2,1,0:T(8,128)}, u32[]{:S(2)}, u32[]{:S(2)}) collective-permute-start(f32[2,512,512]{2,1,0:T(8,128)} %get-tuple-element.113), channel_id=1, source_target_pairs={{30,28},{4,6},{26,24},{0,2},{28,30},{24,26},{2,0},{6,4},{8,10},{22... | collective-permute-start | bytes 6291464 | tf_op jit(solution)/shard_map/ppermute | solution.py:565
  305.0 73.7 %collective-permute-start.24 = (f32[2,512,512]{2,1,0:T(8,128)S(1)}, f32[2,512,512]{2,1,0:T(8,128)S(1)}, u32[]{:S(2)}, u32[]{:S(2)}) collective-permute-start(f32[2,512,512]{2,1,0:T(8,128)S(1)} %get-tuple-element.117), channel_id=1, source_target_pairs={{20,28},{16,24},{22,30},{18,26},{8,16},{12,20},{21,29},{17,25},{23... | collective-permute-start | bytes 6291464 | tf_op jit(solution)/shard_map/ppermute | solution.py:565
  305.8 47.2 %copy-start.1 = (f32[2,512,512]{2,1,0:T(8,128)}, f32[2,512,512]{2,1,0:T(8,128)S(1)}, u32[]{:S(2)}) copy-start(f32[2,512,512]{2,1,0:T(8,128)S(1)} %collective-permute-done.20.refs_3_) | copy-start | bytes 6291460
  305.8 74.2 %collective-permute-start.25 = (f32[2,512,512]{2,1,0:T(8,128)}, f32[2,512,512]{2,1,0:T(8,128)S(1)}, u32[]{:S(2)}, u32[]{:S(2)}) collective-permute-start(f32[2,512,512]{2,1,0:T(8,128)} %get-tuple-element.118), channel_id=1, source_target_pairs={{14,6},{10,2},{12,4},{8,0},{18,10},{22,14},{15,7},{11,3},{13,5},{9... | collective-permute-start | bytes 6291464 | tf_op jit(solution)/shard_map/ppermute | solution.py:565
  332.8 20.3 %copy-start.5 = (f32[2,512,512]{2,1,0:T(8,128)}, f32[2,512,512]{2,1,0:T(8,128)S(1)}, u32[]{:S(2)}) copy-start(f32[2,512,512]{2,1,0:T(8,128)S(1)} %collective-permute-done.21.refs_4_) | copy-start | bytes 6291460
  332.8 50.4 %collective-permute-start.26 = (f32[2,512,512]{2,1,0:T(8,128)}, f32[2,512,512]{2,1,0:T(8,128)}, u32[]{:S(2)}, u32[]{:S(2)}) collective-permute-start(f32[2,512,512]{2,1,0:T(8,128)} %get-tuple-element.119), channel_id=1, source_target_pairs={{6,2},{28,24},{24,28},{2,6},{4,0},{30,26},{0,4},{26,30},{20,16},{1... | collective-permute-start | bytes 6291464 | tf_op jit(solution)/shard_map/ppermute | solution.py:565
  353.1 62.4 %collective-permute-start.27 = (f32[2,512,512]{2,1,0:T(8,128)}, f32[2,512,512]{2,1,0:T(8,128)}, u32[]{:S(2)}, u32[]{:S(2)}) collective-permute-start(f32[2,512,512]{2,1,0:T(8,128)} %get-tuple-element.120), channel_id=1, source_target_pairs={{30,28},{0,2},{4,6},{26,24},{2,0},{6,4},{28,30},{24,26},{8,10},{31... | collective-permute-start | bytes 6291464 | tf_op jit(solution)/shard_map/ppermute | solution.py:565
  377.9 46.3 %collective-permute-start.28 = (f32[2,512,512]{2,1,0:T(8,128)S(1)}, f32[2,512,512]{2,1,0:T(8,128)S(1)}, u32[]{:S(2)}, u32[]{:S(2)}) collective-permute-start(f32[2,512,512]{2,1,0:T(8,128)S(1)} %get-tuple-element.124), channel_id=1, source_target_pairs={{16,24},{20,28},{17,25},{21,29}} | collective-permute-start | bytes 6291464 | tf_op jit(solution)/shard_map/ppermute | solution.py:565
  378.7 31.7 %copy-start.2 = (f32[2,512,512]{2,1,0:T(8,128)}, f32[2,512,512]{2,1,0:T(8,128)S(1)}, u32[]{:S(2)}) copy-start(f32[2,512,512]{2,1,0:T(8,128)S(1)} %collective-permute-done.24.refs_3_) | copy-start | bytes 6291460
  378.7 46.8 %collective-permute-start.29 = (f32[2,512,512]{2,1,0:T(8,128)}, f32[2,512,512]{2,1,0:T(8,128)S(1)}, u32[]{:S(2)}, u32[]{:S(2)}) collective-permute-start(f32[2,512,512]{2,1,0:T(8,128)} %get-tuple-element.125), channel_id=1, source_target_pairs={{14,6},{10,2},{8,0},{15,7},{11,3},{9,1}} | collective-permute-start | bytes 6291464 | tf_op jit(solution)/shard_map/ppermute | solution.py:565
  380.0 30.4 %copy-start.6 = (f32[2,512,512]{2,1,0:T(8,128)}, f32[2,512,512]{2,1,0:T(8,128)S(1)}, u32[]{:S(2)}) copy-start(f32[2,512,512]{2,1,0:T(8,128)S(1)} %collective-permute-done.25.refs_4_) | copy-start | bytes 6291460
  380.0 49.7 %collective-permute-start.30 = (f32[2,512,512]{2,1,0:T(8,128)}, f32[2,512,512]{2,1,0:T(8,128)}, u32[]{:S(2)}, u32[]{:S(2)}) collective-permute-start(f32[2,512,512]{2,1,0:T(8,128)} %get-tuple-element.126), channel_id=1, source_target_pairs={{28,24},{24,28},{6,2},{2,6},{0,4},{20,16},{29,25},{25,29},{7,3},{3... | collective-permute-start | bytes 6291464 | tf_op jit(solution)/shard_map/ppermute | solution.py:565
  383.2 77.3 %collective-permute-start.31 = (f32[2,512,512]{2,1,0:T(8,128)}, f32[2,512,512]{2,1,0:T(8,128)}, u32[]{:S(2)}, u32[]{:S(2)}) collective-permute-start(f32[2,512,512]{2,1,0:T(8,128)} %get-tuple-element.127), channel_id=1, source_target_pairs={{0,2},{30,28},{26,24},{4,6},{28,30},{24,26},{1,3},{31,29},{27,25},... | collective-permute-start | bytes 6291464 | tf_op jit(solution)/shard_map/ppermute | solution.py:565
  423.4 71.2 %collective-permute-start.32 = (f32[2,512,512]{2,1,0:T(8,128)S(1)}, f32[2,512,512]{2,1,0:T(8,128)S(1)}, u32[]{:S(2)}, u32[]{:S(2)}) collective-permute-start(f32[2,512,512]{2,1,0:T(8,128)S(1)} %get-tuple-element.131), channel_id=1, source_target_pairs={{16,24},{20,28},{17,25},{21,29}} | collective-permute-start | bytes 6291464 | tf_op jit(solution)/shard_map/ppermute | solution.py:565
  424.3 70.4 %collective-permute-start.33 = (f32[2,512,512]{2,1,0:T(8,128)}, f32[2,512,512]{2,1,0:T(8,128)S(1)}, u32[]{:S(2)}, u32[]{:S(2)}) collective-permute-start(f32[2,512,512]{2,1,0:T(8,128)} %get-tuple-element.132), channel_id=1, source_target_pairs={{10,2},{14,6},{11,3},{15,7}} | collective-permute-start | bytes 6291464 | tf_op jit(solution)/shard_map/ppermute | solution.py:565
  425.6 23.5 %copy-start.8 = (f32[2,512,512]{2,1,0:T(8,128)}, f32[2,512,512]{2,1,0:T(8,128)S(1)}, u32[]{:S(2)}) copy-start(f32[2,512,512]{2,1,0:T(8,128)S(1)} %collective-permute-done.29.refs_4_) | copy-start | bytes 6291460
  425.6 69.1 %collective-permute-start.34 = (f32[2,512,512]{2,1,0:T(8,128)}, f32[2,512,512]{2,1,0:T(8,128)S(1)}, u32[]{:S(2)}, u32[]{:S(2)}) collective-permute-start(f32[2,512,512]{2,1,0:T(8,128)} %get-tuple-element.133), channel_id=1, source_target_pairs={{6,2},{28,24},{7,3},{29,25}} | collective-permute-start | bytes 6291464 | tf_op jit(solution)/shard_map/ppermute | solution.py:565
  429.8 65.0 %collective-permute-start.35 = (f32[2,512,512]{2,1,0:T(8,128)}, f32[2,512,512]{2,1,0:T(8,128)}, u32[]{:S(2)}, u32[]{:S(2)}) collective-permute-start(f32[2,512,512]{2,1,0:T(8,128)} %get-tuple-element.134), channel_id=1, source_target_pairs={{4,6},{30,28},{5,7},{31,29}} | collective-permute-start | bytes 6291464 | tf_op jit(solution)/shard_map/ppermute | solution.py:565
  494.6 1.3 copy-start.10
  494.6 2.0 copy-start.11

commit v3 on v2

--- a/solution.py
+++ b/solution.py
@@ -322,6 +322,34 @@
         pl.when(tab[i] >= 0)(lambda: again(i).wait())
 
 
+def send_kernel(start, ways, sent, tab, own, *refs):
+    outs, (hold, sem_get, sem_put) = refs[: len(sent)], refs[len(sent) :]
+    tile = hold.shape[-1]
+    of = [tab[start + ways + way] for way in sent]
+
+    def load(i):
+        for c in range(2):
+            at = pl.ds(pl.multiple_of(of[i] * tile, tile), tile)
+            yield pltpu.make_async_copy(own.at[0, c, :, at], hold.at[i, c], sem_get.at[i, c])
+
+    def store(i):
+        return pltpu.make_async_copy(hold.at[i], outs[i], sem_put.at[i])
+
+    for i in range(len(sent)):
+        @pl.when(of[i] >= 0)
+        def _():
+            for copy in load(i):
+                copy.start()
+    for i in range(len(sent)):
+        @pl.when(of[i] >= 0)
+        def _():
+            for copy in load(i):
+                copy.wait()
+            store(i).start()
+    for i in range(len(sent)):
+        pl.when(of[i] >= 0)(lambda: store(i).wait())
+
+
 def route_kernel(start, ways, taken, sent, slots, tab, *refs):
     got = refs[3 : 3 + len(taken)]
     buf, cuts = refs[3 + len(taken) : 5 + len(taken)]
@@ -517,9 +545,29 @@
         )(tab, *ins)
 
     size = tile * tile * 8
+    acc = None
+    flight = {}
+    own = recorded
+    for step in range(min(2, steps)):
+        sent = [way for way in range(ways) if perms[step][way]]
+        out = call(
+            functools.partial(send_kernel, starts["route", step], ways, sent),
+            [own],
+            [chunk] * len(sent),
+            [
+                pltpu.VMEM((len(sent), 2, tile, tile), jnp.float32),
+                pltpu.SemaphoreType.DMA((len(sent), 2)),
+                pltpu.SemaphoreType.DMA((len(sent),)),
+            ],
+            {},
+            (0, 2 * len(sent) * size),
+            32 << 20,
+        )
+        out, own = lax.optimization_barrier((out, own))
+        flight[step] = {way: lax.ppermute(value, AXES, perms[step][way]) for way, value in zip(sent, out)}
     buf, cuts = call(
         first_kernel,
-        [recorded],
+        [own],
         [buf_shape, cut_shape],
         [
             pltpu.VMEM((width, 2, tile, tile), jnp.float32),
@@ -531,9 +579,7 @@
         (0, 3 * width * size),
         48 << 20,
     )
-    acc = None
-    flight = {}
-    for step in range(steps + 2):
+    for step in range(2, steps + 2):
         got = flight.pop(step - 2, {})
         taken = sorted(got)
         sent = [way for way in range(ways) if step < steps and perms[step][way]]
@@ -561,9 +607,7 @@
         buf, cuts = done[:2]
         if m == 3:
             acc = done[2]
-        flight[step] = {
-            way: lax.ppermute(value, AXES, perms[step][way]) for way, value in zip(sent, done[m:])
-        }
+        out = done[m:]
         if step in calls and longest[calls.index(step)]:
             ops = longest[calls.index(step)]
             first = acc is None
@@ -584,6 +628,9 @@
                 (ops * 24 * tile**3, ops * 3 * size),
                 32 << 20,
             )
+            if sent:
+                out, acc = lax.optimization_barrier((out, acc))
+        flight[step] = {way: lax.ppermute(value, AXES, perms[step][way]) for way, value in zip(sent, out)}
     return acc
 
 

time: 523 us -> 460 us (0.88)
  waiting for transfers between devices: 141 us -> 79 us
  Pallas kernels: 274 us -> 267 us
    ppermute x36, waiting for transfers between devices: 141 us -> 79 us  [local(): lax.ppermute(value, AXES, perms[step][way])]
    pallas_call x20, Pallas kernels: 274 us -> 267 us  [call(): pl.pallas_call(kernel, out_shape=outs, grid_spec=pltpu.PrefetchScalarGrid...]
  transfers between devices with their start and end apart: 36 -> 36, of which waited for: 14 -> 11; matrix products, arithmetic and copies ran while one was open for 0% -> 0% of each run, Pallas kernels for 45% -> 52%
where the time goes in v3:
time: 460 us; the launch traced here: 459 us
  Pallas kernels  267 us (58%)
  starting transfers between devices  105 us (23%)
  waiting for transfers between devices  79 us (17%)
  local copies, waits for them, and re-layouts  6.72 us (1%)
    pallas_call x20, Pallas kernels, call(): pl.pallas_call(kernel, out_shape=outs, grid_spec=pltpu.PrefetchScalarGrid...  267 us
    ppermute x36, starting transfers between devices, local(): lax.ppermute(value, AXES, perms[step][way])  105 us
    ppermute x36, waiting for transfers between devices, local(): lax.ppermute(value, AXES, perms[step][way])  79 us
  transfers between devices with their start and end apart: 36, of which 11 were waited for; matrix products, arithmetic and copies ran while one was open for 0% of the time, Pallas kernels for 52%

profile of v3, /device:TPU:6, one launch (start us, length us, event | category | flops | bytes accessed | tf_op | source)
XLA Modules:
  0.0 459.0 jit_solution(8739590904493410934)
XLA Ops:
  0.0 0.7 dynamic-slice_reduce_fusion.tab
  0.8 3.4 copy-done
  4.1 2.0 shard_map.28
  6.1 4.0 collective-permute-start
  10.1 1.3 collective-permute-start.1
  11.4 0.6 collective-permute-start.2
  12.0 0.5 collective-permute-start.3
  12.5 2.0 shard_map.29
  14.5 6.3 %collective-permute-start.4 = (f32[2,512,512]{2,1,0:T(8,128)S(1)}, f32[2,512,512]{2,1,0:T(8,128)}, u32[]{:S(2)}, u32[]{:S(2)}) collective-permute-start(f32[2,512,512]{2,1,0:T(8,128)S(1)} %get-tuple-element.125), channel_id=1, source_target_pairs={{20,28},{16,24},{18,26},{22,30},{2,10},{12,20},{6,14},{8,16},{14,2... | collective-permute-start | bytes 6291464 | tf_op jit(solution)/shard_map/ppermute | solution.py:567
  20.8 35.2 %collective-permute-done.refs_2_ = f32[2,512,512]{2,1,0:T(8,128)S(1)} collective-permute-done((f32[2,512,512]{2,1,0:T(8,128)S(1)}, f32[2,512,512]{2,1,0:T(8,128)S(1)}, u32[]{:S(2)}, u32[]{:S(2)}) %collective-permute-start) | collective-permute-done | bytes 2097184 | tf_op jit(solution)/shard_map/ppermute | solution.py:567
  56.0 1.3 collective-permute-start.5
  57.3 1.8 collective-permute-done.1.refs_3_
  59.6 0.8 copy-done.14
  61.0 10.4 %shard_map.30 = (f32[13,2,512,512]{3,2,1,0:T(8,128)}, bf16[36,2,2,512,512]{4,3,2,1,0:T(8,128)(2,1)}) custom-call(s32[536]{0:T(1024)S(1)} %dynamic-slice_reduce_fusion.tab, f32[1,2,512,2048]{3,2,1,0:T(8,128)} %own.3), custom_call_target="tpu_custom_call" | custom-call | bytes 25165824 | tf_op jit(solution)/shard_map/pallas_call | solution.py:532
  71.4 10.6 %shard_map.31 = (f32[13,2,512,512]{3,2,1,0:T(8,128)}, bf16[36,2,2,512,512]{4,3,2,1,0:T(8,128)(2,1)}, f32[2,512,512]{2,1,0:T(8,128)S(1)}, f32[2,512,512]{2,1,0:T(...) custom-call(s32[536]{0:T(1024)S(1)} %dynamic-slice_reduce_fusion.tab, ...), custom_call_target="tpu_custom_call", output_to_operand_aliasing={{0}: (1, {}), {1}: (2, {})} | custom-call | bytes 41943040 | tf_op jit(solution)/shard_map/pallas_call | solution.py:532
  82.0 5.4 %collective-permute-start.8 = (f32[2,512,512]{2,1,0:T(8,128)S(1)}, f32[2,512,512]{2,1,0:T(8,128)S(1)}, u32[]{:S(2)}, u32[]{:S(2)}) collective-permute-start(f32[2,512,512]{2,1,0:T(8,128)S(1)} %get-tuple-element.136), channel_id=1, source_target_pairs={{16,24},{20,28},{18,26},{22,30},{2,10},{12,20},{8,16},{6,14},{10,1... | collective-permute-start | bytes 6291464 | tf_op jit(solution)/shard_map/ppermute | solution.py:633
  87.3 13.6 %collective-permute-done.4.refs_2_ = f32[2,512,512]{2,1,0:T(8,128)} collective-permute-done((f32[2,512,512]{2,1,0:T(8,128)S(1)}, f32[2,512,512]{2,1,0:T(8,128)}, u32[]{:S(2)}, u32[]{:S(2)}) %collective-permute-start.4) | collective-permute-done | bytes 2097184 | tf_op jit(solution)/shard_map/ppermute | solution.py:567
  101.0 1.3 collective-permute-start.9
  102.3 2.0 collective-permute-done.5.refs_3_
  104.7 1.8 collective-permute-done.6.refs_4_
  107.4 8.8 %shard_map.32 = (f32[13,2,512,512]{3,2,1,0:T(8,128)}, bf16[36,2,2,512,512]{4,3,2,1,0:T(8,128)(2,1)}, f32[2,512,512]{2,1,0:T(8,128)S(1)}, f32[2,512,512]{2,1,0:T(...) custom-call(s32[536]{0:T(1024)S(1)} %dynamic-slice_reduce_fusion.tab, ...), custom_call_target="tpu_custom_call", output_to_operand_aliasing={{0}: (1, {}), {1}: (2, {})} | custom-call | bytes 41943040 | tf_op jit(solution)/shard_map/pallas_call | solution.py:532
  116.2 29.5 %shard_map.33.refs_2_ = f32[1,2,512,2048]{3,2,1,0:T(8,128)} custom-call(s32[536]{0:T(1024)S(1)} %dynamic-slice_reduce_fusion.tab, bf16[36,2,2,512,512]{4,3,2,1,0:T(8,128)(2,1)} %get-tuple-element.130.cuts.refs_1_), custom_call_target="tpu_custom_call" | custom-call | flops 19327352832 | bytes 37748736 | tf_op jit(solution)/shard_map/pallas_call | solution.py:532
  145.7 3.9 collective-permute-start.12
  149.7 1.3 collective-permute-start.13
  151.0 2.4 collective-permute-start.14
  153.4 1.8 collective-permute-start.15
  155.2 9.4 %shard_map.34 = (f32[13,2,512,512]{3,2,1,0:T(8,128)}, bf16[36,2,2,512,512]{4,3,2,1,0:T(8,128)(2,1)}, f32[1,2,512,2048]{3,2,1,0:T(8,128)}, f32[2,512,512]{2,1,0:T...) custom-call(s32[536]{0:T(1024)S(1)} %dynamic-slice_reduce_fusion.tab, ...), custom_call_target="tpu_custom_call", output_to_operand_aliasing={{0}: (1, {}), {1}: (2, {}), {2}: (3, {})} | custom-call | bytes 41943040 | tf_op jit(solution)/shard_map/pallas_call | solution.py:532
  164.6 16.7 %shard_map.35.refs_2_ = f32[1,2,512,2048]{3,2,1,0:T(8,128)} custom-call(s32[536]{0:T(1024)S(1)} %dynamic-slice_reduce_fusion.tab, bf16[36,2,2,512,512]{4,3,2,1,0:T(8,128)(2,1)} %get-tuple-element.141.cuts.refs_1_, f32[1,2,512,2048]{3,2,1,0:T(8,128)} %get-tuple-element.146.refs_0_), custom_call_target="tpu_custom_call", output_to_operand_aliasing={{}: (2, {})} | custom-call | flops 19327352832 | bytes 37748736 | tf_op jit(solution)/shard_map/pallas_call | solution.py:532
  181.4 17.4 %collective-permute-start.16 = (f32[2,512,512]{2,1,0:T(8,128)S(1)}, f32[2,512,512]{2,1,0:T(8,128)S(1)}, u32[]{:S(2)}, u32[]{:S(2)}) collective-permute-start(f32[2,512,512]{2,1,0:T(8,128)S(1)} %get-tuple-element.160), channel_id=1, source_target_pairs={{20,28},{16,24},{18,26},{22,30},{6,14},{2,10},{8,16},{12,20},{4,12... | collective-permute-start | bytes 6291464 | tf_op jit(solution)/shard_map/ppermute | solution.py:633
  198.8 1.3 collective-permute-start.17
  200.2 3.4 collective-permute-start.19
  203.6 9.3 %shard_map.36 = (f32[13,2,512,512]{3,2,1,0:T(8,128)}, bf16[36,2,2,512,512]{4,3,2,1,0:T(8,128)(2,1)}, f32[1,2,512,2048]{3,2,1,0:T(8,128)}, f32[2,512,512]{2,1,0:T...) custom-call(s32[536]{0:T(1024)S(1)} %dynamic-slice_reduce_fusion.tab, ...), custom_call_target="tpu_custom_call", output_to_operand_aliasing={{0}: (1, {}), {1}: (2, {}), {2}: (3, {})} | custom-call | bytes 41943040 | tf_op jit(solution)/shard_map/pallas_call | solution.py:532
  212.9 23.2 %shard_map.37.refs_2_ = f32[1,2,512,2048]{3,2,1,0:T(8,128)} custom-call(s32[536]{0:T(1024)S(1)} %dynamic-slice_reduce_fusion.tab, bf16[36,2,2,512,512]{4,3,2,1,0:T(8,128)(2,1)} %get-tuple-element.153.cuts.refs_1_, f32[1,2,512,2048]{3,2,1,0:T(8,128)} %get-tuple-element.158.refs_0_), custom_call_target="tpu_custom_call", output_to_operand_aliasing={{}: (2, {})} | custom-call | flops 19327352832 | bytes 37748736 | tf_op jit(solution)/shard_map/pallas_call | solution.py:532
  236.1 12.0 %collective-permute-start.20 = (f32[2,512,512]{2,1,0:T(8,128)S(1)}, f32[2,512,512]{2,1,0:T(8,128)S(1)}, u32[]{:S(2)}, u32[]{:S(2)}) collective-permute-start(f32[2,512,512]{2,1,0:T(8,128)S(1)} %get-tuple-element.172), channel_id=1, source_target_pairs={{16,24},{20,28},{18,26},{22,30},{2,10},{6,14},{8,16},{12,20},{0,8}... | collective-permute-start | bytes 6291464 | tf_op jit(solution)/shard_map/ppermute | solution.py:633
  248.2 1.3 collective-permute-start.21
  249.5 3.0 collective-permute-start.22
  252.5 3.7 collective-permute-start.23
  256.2 8.7 %shard_map.38 = (f32[13,2,512,512]{3,2,1,0:T(8,128)}, bf16[36,2,2,512,512]{4,3,2,1,0:T(8,128)(2,1)}, f32[1,2,512,2048]{3,2,1,0:T(8,128)}, f32[2,512,512]{2,1,0:T...) custom-call(s32[536]{0:T(1024)S(1)} %dynamic-slice_reduce_fusion.tab, ...), custom_call_target="tpu_custom_call", output_to_operand_aliasing={{0}: (1, {}), {1}: (2, {}), {2}: (3, {})} | custom-call | bytes 41943040 | tf_op jit(solution)/shard_map/pallas_call | solution.py:532
  265.0 16.7 %shard_map.39.refs_2_ = f32[1,2,512,2048]{3,2,1,0:T(8,128)} custom-call(s32[536]{0:T(1024)S(1)} %dynamic-slice_reduce_fusion.tab, bf16[36,2,2,512,512]{4,3,2,1,0:T(8,128)(2,1)} %get-tuple-element.165.cuts.refs_1_, f32[1,2,512,2048]{3,2,1,0:T(8,128)} %get-tuple-element.170.refs_0_), custom_call_target="tpu_custom_call", output_to_operand_aliasing={{}: (2, {})} | custom-call | flops 19327352832 | bytes 37748736 | tf_op jit(solution)/shard_map/pallas_call | solution.py:532
  281.7 0.8 collective-permute-start.24
  282.5 4.9 %collective-permute-done.20.refs_3_ = f32[2,512,512]{2,1,0:T(8,128)S(1)} collective-permute-done((f32[2,512,512]{2,1,0:T(8,128)S(1)}, f32[2,512,512]{2,1,0:T(8,128)S(1)}, u32[]{:S(2)}, u32[]{:S(2)}) %collective-permute-start.20) | collective-permute-done | bytes 2097184 | tf_op jit(solution)/shard_map/ppermute | solution.py:633
  287.4 1.3 collective-permute-start.25
  288.7 4.0 collective-permute-done.21.refs_4_
  292.7 3.0 collective-permute-start.26
  295.9 5.2 %collective-permute-start.27 = (f32[2,512,512]{2,1,0:T(8,128)}, f32[2,512,512]{2,1,0:T(8,128)}, u32[]{:S(2)}, u32[]{:S(2)}) collective-permute-start(f32[2,512,512]{2,1,0:T(8,128)} %get-tuple-element.187), channel_id=1, source_target_pairs={{30,28},{0,2},{4,6},{26,24},{2,0},{6,4},{28,30},{24,26},{8,10},{31... | collective-permute-start | bytes 6291464 | tf_op jit(solution)/shard_map/ppermute | solution.py:633
  301.1 9.2 %shard_map.40 = (f32[13,2,512,512]{3,2,1,0:T(8,128)}, bf16[36,2,2,512,512]{4,3,2,1,0:T(8,128)(2,1)}, f32[1,2,512,2048]{3,2,1,0:T(8,128)}, f32[2,512,512]{2,1,0:T...) custom-call(s32[536]{0:T(1024)S(1)} %dynamic-slice_reduce_fusion.tab, ...), custom_call_target="tpu_custom_call", output_to_operand_aliasing={{0}: (1, {}), {1}: (2, {}), {2}: (3, {})} | custom-call | bytes 41943040 | tf_op jit(solution)/shard_map/pallas_call | solution.py:532
  310.3 26.0 %shard_map.41.refs_2_ = f32[1,2,512,2048]{3,2,1,0:T(8,128)} custom-call(s32[536]{0:T(1024)S(1)} %dynamic-slice_reduce_fusion.tab, bf16[36,2,2,512,512]{4,3,2,1,0:T(8,128)(2,1)} %get-tuple-element.177.cuts.refs_1_, f32[1,2,512,2048]{3,2,1,0:T(8,128)} %get-tuple-element.182.refs_0_), custom_call_target="tpu_custom_call", output_to_operand_aliasing={{}: (2, {})} | custom-call | flops 19327352832 | bytes 37748736 | tf_op jit(solution)/shard_map/pallas_call | solution.py:532
  336.3 0.8 collective-permute-start.28
  337.1 1.3 collective-permute-start.29
  338.4 5.2 %collective-permute-start.30 = (f32[2,512,512]{2,1,0:T(8,128)}, f32[2,512,512]{2,1,0:T(8,128)}, u32[]{:S(2)}, u32[]{:S(2)}) collective-permute-start(f32[2,512,512]{2,1,0:T(8,128)} %get-tuple-element.198), channel_id=1, source_target_pairs={{28,24},{24,28},{6,2},{2,6},{0,4},{20,16},{29,25},{25,29},{7,3},{3... | collective-permute-start | bytes 6291464 | tf_op jit(solution)/shard_map/ppermute | solution.py:633
  343.6 1.3 collective-permute-start.31
  345.0 7.9 %shard_map.42 = (f32[13,2,512,512]{3,2,1,0:T(8,128)}, bf16[36,2,2,512,512]{4,3,2,1,0:T(8,128)(2,1)}, f32[1,2,512,2048]{3,2,1,0:T(8,128)}, f32[2,512,512]{2,1,0:T...) custom-call(s32[536]{0:T(1024)S(1)} %dynamic-slice_reduce_fusion.tab, ...), custom_call_target="tpu_custom_call", output_to_operand_aliasing={{0}: (1, {}), {1}: (2, {}), {2}: (3, {})} | custom-call | bytes 41943040 | tf_op jit(solution)/shard_map/pallas_call | solution.py:532
  352.9 18.0 %shard_map.43.refs_2_ = f32[1,2,512,2048]{3,2,1,0:T(8,128)} custom-call(s32[536]{0:T(1024)S(1)} %dynamic-slice_reduce_fusion.tab, bf16[36,2,2,512,512]{4,3,2,1,0:T(8,128)(2,1)} %get-tuple-element.189.cuts.refs_1_, f32[1,2,512,2048]{3,2,1,0:T(8,128)} %get-tuple-element.194.refs_0_), custom_call_target="tpu_custom_call", output_to_operand_aliasing={{}: (2, {})} | custom-call | flops 12884901888 | bytes 25165824 | tf_op jit(solution)/shard_map/pallas_call | solution.py:532
  370.8 0.8 collective-permute-start.32
  371.7 1.3 collective-permute-start.33
  373.0 14.8 %collective-permute-done.29.refs_4_ = f32[2,512,512]{2,1,0:T(8,128)S(1)} collective-permute-done((f32[2,512,512]{2,1,0:T(8,128)}, f32[2,512,512]{2,1,0:T(8,128)S(1)}, u32[]{:S(2)}, u32[]{:S(2)}) %collective-permute-start.29) | collective-permute-done | bytes 2097184 | tf_op jit(solution)/shard_map/ppermute | solution.py:633
  387.8 8.8 %collective-permute-start.34 = (f32[2,512,512]{2,1,0:T(8,128)}, f32[2,512,512]{2,1,0:T(8,128)S(1)}, u32[]{:S(2)}, u32[]{:S(2)}) collective-permute-start(f32[2,512,512]{2,1,0:T(8,128)} %get-tuple-element.205), channel_id=1, source_target_pairs={{6,2},{28,24},{7,3},{29,25}} | collective-permute-start | bytes 6291464 | tf_op jit(solution)/shard_map/ppermute | solution.py:633
  396.6 1.3 collective-permute-start.35
  397.9 9.2 %shard_map.44 = (f32[13,2,512,512]{3,2,1,0:T(8,128)}, bf16[36,2,2,512,512]{4,3,2,1,0:T(8,128)(2,1)}, f32[1,2,512,2048]{3,2,1,0:T(8,128)}) custom-call(s32[536]{0:T(1024)S(1)} %dynamic-slice_reduce_fusion.tab, f32[13,2,512,512]{3,2,1,0:T(8,128)} %get-tuple-element.188.refs_0_, ...), custom_call_target="tpu_custom_call", output_to_operand_aliasing={{0}: (1, {}), {1}: (2, {}), {2}: (3, {})} | custom-call | bytes 25165824 | tf_op jit(solution)/shard_map/pallas_call | solution.py:532
  407.1 24.7 %shard_map.45.refs_2_ = f32[1,2,512,2048]{3,2,1,0:T(8,128)} custom-call(s32[536]{0:T(1024)S(1)} %dynamic-slice_reduce_fusion.tab, bf16[36,2,2,512,512]{4,3,2,1,0:T(8,128)(2,1)} %get-tuple-element.201.cuts.refs_1_, f32[1,2,512,2048]{3,2,1,0:T(8,128)} %get-tuple-element.202.refs_0_), custom_call_target="tpu_custom_call", output_to_operand_aliasing={{}: (2, {})} | custom-call | flops 16106127360 | bytes 31457280 | tf_op jit(solution)/shard_map/pallas_call | solution.py:532
  432.2 1.0 copy-done.11
  433.2 0.7 copy-done.12
  433.9 7.0 %shard_map.46 = (f32[13,2,512,512]{3,2,1,0:T(8,128)}, bf16[36,2,2,512,512]{4,3,2,1,0:T(8,128)(2,1)}, f32[1,2,512,2048]{3,2,1,0:T(8,128)}) custom-call(s32[536]{0:T(1024)S(1)} %dynamic-slice_reduce_fusion.tab, f32[13,2,512,512]{3,2,1,0:T(8,128)} %get-tuple-element.200.refs_0_, ...), custom_call_target="tpu_custom_call", output_to_operand_aliasing={{0}: (1, {}), {1}: (2, {}), {2}: (3, {})} | custom-call | bytes 25165824 | tf_op jit(solution)/shard_map/pallas_call | solution.py:532
  440.9 18.0 %shard_map.47 = f32[1,2,512,2048]{3,2,1,0:T(8,128)} custom-call(s32[536]{0:T(1024)S(1)} %dynamic-slice_reduce_fusion.tab, bf16[36,2,2,512,512]{4,3,2,1,0:T(8,128)(2,1)} %get-tuple-element.207.cuts, f32[1,2,512,2048]{3,2,1,0:T(8,128)} %get-tuple-element.208.refs_0_), custom_call_target="tpu_custom_call", output_to_operand_aliasing={{}: (2, {})} | custom-call | flops 9663676416 | bytes 18874368 | tf_op jit(solution)/shard_map/pallas_call | solution.py:532
  (59 shorter events, 3.0 us)
Async XLA Ops:
  0.7 3.4 copy-start
  6.1 49.9 %collective-permute-start = (f32[2,512,512]{2,1,0:T(8,128)S(1)}, f32[2,512,512]{2,1,0:T(8,128)S(1)}, u32[]{:S(2)}, u32[]{:S(2)}) collective-permute-start(f32[2,512,512]{2,1,0:T(8,128)S(1)} %get-tuple-element.119), channel_id=1, source_target_pairs={{20,28},{16,24},{18,26},{22,30},{2,10},{12,20},{8,16},{6,14},{14,2... | collective-permute-start | bytes 6291464 | tf_op jit(solution)/shard_map/ppermute | solution.py:567
  10.1 49.0 %collective-permute-start.1 = (f32[2,512,512]{2,1,0:T(8,128)S(1)}, f32[2,512,512]{2,1,0:T(8,128)S(1)}, u32[]{:S(2)}, u32[]{:S(2)}) collective-permute-start(f32[2,512,512]{2,1,0:T(8,128)S(1)} %get-tuple-element.120), channel_id=1, source_target_pairs={{10,2},{14,6},{12,4},{8,0},{24,16},{18,10},{22,14},{28,20},{16,8},... | collective-permute-start | bytes 6291464 | tf_op jit(solution)/shard_map/ppermute | solution.py:567
  11.4 48.2 %collective-permute-start.2 = (f32[2,512,512]{2,1,0:T(8,128)S(1)}, f32[2,512,512]{2,1,0:T(8,128)}, u32[]{:S(2)}, u32[]{:S(2)}) collective-permute-start(f32[2,512,512]{2,1,0:T(8,128)S(1)} %get-tuple-element.121), channel_id=1, source_target_pairs={{6,2},{28,24},{2,6},{24,28},{30,26},{0,4},{26,30},{4,0},{16,20},{2... | collective-permute-start | bytes 6291464 | tf_op jit(solution)/shard_map/ppermute | solution.py:567
  12.0 59.4 %collective-permute-start.3 = (f32[2,512,512]{2,1,0:T(8,128)S(1)}, f32[2,512,512]{2,1,0:T(8,128)}, u32[]{:S(2)}, u32[]{:S(2)}) collective-permute-start(f32[2,512,512]{2,1,0:T(8,128)S(1)} %get-tuple-element.122), channel_id=1, source_target_pairs={{0,2},{4,6},{30,28},{26,24},{28,30},{2,0},{24,26},{6,4},{8,10},{18... | collective-permute-start | bytes 6291464 | tf_op jit(solution)/shard_map/ppermute | solution.py:567
  14.5 86.4 %collective-permute-start.4 = (f32[2,512,512]{2,1,0:T(8,128)S(1)}, f32[2,512,512]{2,1,0:T(8,128)}, u32[]{:S(2)}, u32[]{:S(2)}) collective-permute-start(f32[2,512,512]{2,1,0:T(8,128)S(1)} %get-tuple-element.125), channel_id=1, source_target_pairs={{20,28},{16,24},{18,26},{22,30},{2,10},{12,20},{6,14},{8,16},{14,2... | collective-permute-start | bytes 6291464 | tf_op jit(solution)/shard_map/ppermute | solution.py:567
  56.0 15.4 %copy-start.13 = (f32[2,512,512]{2,1,0:T(8,128)}, f32[2,512,512]{2,1,0:T(8,128)S(1)}, u32[]{:S(2)}) copy-start(f32[2,512,512]{2,1,0:T(8,128)S(1)} %collective-permute-done.refs_2_) | copy-start | bytes 6291460
  56.0 48.2 %collective-permute-start.5 = (f32[2,512,512]{2,1,0:T(8,128)S(1)}, f32[2,512,512]{2,1,0:T(8,128)}, u32[]{:S(2)}, u32[]{:S(2)}) collective-permute-start(f32[2,512,512]{2,1,0:T(8,128)S(1)} %get-tuple-element.126), channel_id=1, source_target_pairs={{14,6},{10,2},{8,0},{12,4},{28,20},{24,16},{22,14},{18,10},{16,8},... | collective-permute-start | bytes 6291464 | tf_op jit(solution)/shard_map/ppermute | solution.py:567
  59.1 1.3 copy-start.14
  59.1 47.4 %collective-permute-start.6 = (f32[2,512,512]{2,1,0:T(8,128)S(1)}, f32[2,512,512]{2,1,0:T(8,128)}, u32[]{:S(2)}, u32[]{:S(2)}) collective-permute-start(f32[2,512,512]{2,1,0:T(8,128)S(1)} %get-tuple-element.127), channel_id=1, source_target_pairs={{24,28},{2,6},{28,24},{6,2},{26,30},{0,4},{30,26},{4,0},{10,14},{1... | collective-permute-start | bytes 6291464 | tf_op jit(solution)/shard_map/ppermute | solution.py:567
  60.5 46.9 %collective-permute-start.7 = (f32[2,512,512]{2,1,0:T(8,128)S(1)}, f32[2,512,512]{2,1,0:T(8,128)}, u32[]{:S(2)}, u32[]{:S(2)}) collective-permute-start(f32[2,512,512]{2,1,0:T(8,128)S(1)} %get-tuple-element.128), channel_id=1, source_target_pairs={{26,24},{30,28},{4,6},{0,2},{24,26},{2,0},{28,30},{6,4},{12,14},{8... | collective-permute-start | bytes 6291464 | tf_op jit(solution)/shard_map/ppermute | solution.py:567
  82.0 67.7 %collective-permute-start.8 = (f32[2,512,512]{2,1,0:T(8,128)S(1)}, f32[2,512,512]{2,1,0:T(8,128)S(1)}, u32[]{:S(2)}, u32[]{:S(2)}) collective-permute-start(f32[2,512,512]{2,1,0:T(8,128)S(1)} %get-tuple-element.136), channel_id=1, source_target_pairs={{16,24},{20,28},{18,26},{22,30},{2,10},{12,20},{8,16},{6,14},{10,1... | collective-permute-start | bytes 6291464 | tf_op jit(solution)/shard_map/ppermute | solution.py:633
  101.0 50.0 %collective-permute-start.9 = (f32[2,512,512]{2,1,0:T(8,128)}, f32[2,512,512]{2,1,0:T(8,128)}, u32[]{:S(2)}, u32[]{:S(2)}) collective-permute-start(f32[2,512,512]{2,1,0:T(8,128)} %get-tuple-element.137), channel_id=1, source_target_pairs={{14,6},{10,2},{8,0},{12,4},{22,14},{28,20},{18,10},{24,16},{20,12}... | collective-permute-start | bytes 6291464 | tf_op jit(solution)/shard_map/ppermute | solution.py:633
  104.2 49.2 %collective-permute-start.10 = (f32[2,512,512]{2,1,0:T(8,128)}, f32[2,512,512]{2,1,0:T(8,128)}, u32[]{:S(2)}, u32[]{:S(2)}) collective-permute-start(f32[2,512,512]{2,1,0:T(8,128)} %get-tuple-element.138), channel_id=1, source_target_pairs={{6,2},{28,24},{2,6},{24,28},{26,30},{4,0},{30,26},{0,4},{10,14},{1... | collective-permute-start | bytes 6291464 | tf_op jit(solution)/shard_map/ppermute | solution.py:633
  106.6 48.7 %collective-permute-start.11 = (f32[2,512,512]{2,1,0:T(8,128)}, f32[2,512,512]{2,1,0:T(8,128)}, u32[]{:S(2)}, u32[]{:S(2)}) collective-permute-start(f32[2,512,512]{2,1,0:T(8,128)} %get-tuple-element.139), channel_id=1, source_target_pairs={{4,6},{26,24},{30,28},{0,2},{6,4},{2,0},{28,30},{24,26},{22,20},{1... | collective-permute-start | bytes 6291464 | tf_op jit(solution)/shard_map/ppermute | solution.py:633
  145.7 53.1 %collective-permute-start.12 = (f32[2,512,512]{2,1,0:T(8,128)S(1)}, f32[2,512,512]{2,1,0:T(8,128)S(1)}, u32[]{:S(2)}, u32[]{:S(2)}) collective-permute-start(f32[2,512,512]{2,1,0:T(8,128)S(1)} %get-tuple-element.148), channel_id=1, source_target_pairs={{16,24},{20,28},{18,26},{22,30},{12,20},{8,16},{6,14},{2,10},{4,12... | collective-permute-start | bytes 6291464 | tf_op jit(solution)/shard_map/ppermute | solution.py:633
  149.6 5.6 %copy-start.5 = (f32[2,512,512]{2,1,0:T(8,128)}, f32[2,512,512]{2,1,0:T(8,128)S(1)}, u32[]{:S(2)}) copy-start(f32[2,512,512]{2,1,0:T(8,128)S(1)} %collective-permute-done.8.refs_3_) | copy-start | bytes 6291460
  149.7 50.4 %collective-permute-start.13 = (f32[2,512,512]{2,1,0:T(8,128)}, f32[2,512,512]{2,1,0:T(8,128)S(1)}, u32[]{:S(2)}, u32[]{:S(2)}) collective-permute-start(f32[2,512,512]{2,1,0:T(8,128)} %get-tuple-element.149), channel_id=1, source_target_pairs={{10,2},{14,6},{12,4},{8,0},{18,10},{22,14},{24,16},{28,20},{16,8},... | collective-permute-start | bytes 6291464 | tf_op jit(solution)/shard_map/ppermute | solution.py:633
  151.0 49.2 %collective-permute-start.14 = (f32[2,512,512]{2,1,0:T(8,128)}, f32[2,512,512]{2,1,0:T(8,128)}, u32[]{:S(2)}, u32[]{:S(2)}) collective-permute-start(f32[2,512,512]{2,1,0:T(8,128)} %get-tuple-element.150), channel_id=1, source_target_pairs={{28,24},{2,6},{24,28},{6,2},{26,30},{4,0},{0,4},{30,26},{20,16},{1... | collective-permute-start | bytes 6291464 | tf_op jit(solution)/shard_map/ppermute | solution.py:633
  153.4 50.2 %collective-permute-start.15 = (f32[2,512,512]{2,1,0:T(8,128)}, f32[2,512,512]{2,1,0:T(8,128)}, u32[]{:S(2)}, u32[]{:S(2)}) collective-permute-start(f32[2,512,512]{2,1,0:T(8,128)} %get-tuple-element.151), channel_id=1, source_target_pairs={{4,6},{30,28},{0,2},{26,24},{6,4},{28,30},{2,0},{24,26},{22,20},{8... | collective-permute-start | bytes 6291464 | tf_op jit(solution)/shard_map/ppermute | solution.py:633
  181.4 66.8 %collective-permute-start.16 = (f32[2,512,512]{2,1,0:T(8,128)S(1)}, f32[2,512,512]{2,1,0:T(8,128)S(1)}, u32[]{:S(2)}, u32[]{:S(2)}) collective-permute-start(f32[2,512,512]{2,1,0:T(8,128)S(1)} %get-tuple-element.160), channel_id=1, source_target_pairs={{20,28},{16,24},{18,26},{22,30},{6,14},{2,10},{8,16},{12,20},{4,12... | collective-permute-start | bytes 6291464 | tf_op jit(solution)/shard_map/ppermute | solution.py:633
  198.8 4.8 %copy-start.1 = (f32[2,512,512]{2,1,0:T(8,128)}, f32[2,512,512]{2,1,0:T(8,128)S(1)}, u32[]{:S(2)}) copy-start(f32[2,512,512]{2,1,0:T(8,128)S(1)} %collective-permute-done.12.refs_3_) | copy-start | bytes 6291460
  198.8 50.7 %collective-permute-start.17 = (f32[2,512,512]{2,1,0:T(8,128)}, f32[2,512,512]{2,1,0:T(8,128)}, u32[]{:S(2)}, u32[]{:S(2)}) collective-permute-start(f32[2,512,512]{2,1,0:T(8,128)} %get-tuple-element.161), channel_id=1, source_target_pairs={{14,6},{10,2},{12,4},{8,0},{18,10},{24,16},{22,14},{28,20},{20,12}... | collective-permute-start | bytes 6291464 | tf_op jit(solution)/shard_map/ppermute | solution.py:633
  200.1 3.5 copy-start.6
  200.1 52.4 %collective-permute-start.18 = (f32[2,512,512]{2,1,0:T(8,128)}, f32[2,512,512]{2,1,0:T(8,128)}, u32[]{:S(2)}, u32[]{:S(2)}) collective-permute-start(f32[2,512,512]{2,1,0:T(8,128)} %get-tuple-element.162), channel_id=1, source_target_pairs={{28,24},{24,28},{6,2},{2,6},{0,4},{26,30},{30,26},{4,0},{16,20},{1... | collective-permute-start | bytes 6291464 | tf_op jit(solution)/shard_map/ppermute | solution.py:633
  200.2 56.0 %collective-permute-start.19 = (f32[2,512,512]{2,1,0:T(8,128)}, f32[2,512,512]{2,1,0:T(8,128)}, u32[]{:S(2)}, u32[]{:S(2)}) collective-permute-start(f32[2,512,512]{2,1,0:T(8,128)} %get-tuple-element.163), channel_id=1, source_target_pairs={{4,6},{0,2},{30,28},{26,24},{24,26},{28,30},{6,4},{2,0},{8,10},{12... | collective-permute-start | bytes 6291464 | tf_op jit(solution)/shard_map/ppermute | solution.py:633
  236.1 51.3 %collective-permute-start.20 = (f32[2,512,512]{2,1,0:T(8,128)S(1)}, f32[2,512,512]{2,1,0:T(8,128)S(1)}, u32[]{:S(2)}, u32[]{:S(2)}) collective-permute-start(f32[2,512,512]{2,1,0:T(8,128)S(1)} %get-tuple-element.172), channel_id=1, source_target_pairs={{16,24},{20,28},{18,26},{22,30},{2,10},{6,14},{8,16},{12,20},{0,8}... | collective-permute-start | bytes 6291464 | tf_op jit(solution)/shard_map/ppermute | solution.py:633
  248.2 8.1 %copy-start.2 = (f32[2,512,512]{2,1,0:T(8,128)}, f32[2,512,512]{2,1,0:T(8,128)S(1)}, u32[]{:S(2)}) copy-start(f32[2,512,512]{2,1,0:T(8,128)S(1)} %collective-permute-done.16.refs_3_) | copy-start | bytes 6291460
  248.2 44.5 %collective-permute-start.21 = (f32[2,512,512]{2,1,0:T(8,128)}, f32[2,512,512]{2,1,0:T(8,128)S(1)}, u32[]{:S(2)}, u32[]{:S(2)}) collective-permute-start(f32[2,512,512]{2,1,0:T(8,128)} %get-tuple-element.173), channel_id=1, source_target_pairs={{10,2},{14,6},{8,0},{12,4},{24,16},{18,10},{22,14},{28,20},{26,18}... | collective-permute-start | bytes 6291464 | tf_op jit(solution)/shard_map/ppermute | solution.py:633
  249.5 46.4 %collective-permute-start.22 = (f32[2,512,512]{2,1,0:T(8,128)}, f32[2,512,512]{2,1,0:T(8,128)S(1)}, u32[]{:S(2)}, u32[]{:S(2)}) collective-permute-start(f32[2,512,512]{2,1,0:T(8,128)} %get-tuple-element.174), channel_id=1, source_target_pairs={{28,24},{6,2},{24,28},{2,6},{4,0},{30,26},{26,30},{0,4},{16,20},{2... | collective-permute-start | bytes 6291464 | tf_op jit(solution)/shard_map/ppermute | solution.py:633
  252.5 48.5 %collective-permute-start.23 = (f32[2,512,512]{2,1,0:T(8,128)}, f32[2,512,512]{2,1,0:T(8,128)}, u32[]{:S(2)}, u32[]{:S(2)}) collective-permute-start(f32[2,512,512]{2,1,0:T(8,128)} %get-tuple-element.175), channel_id=1, source_target_pairs={{30,28},{4,6},{26,24},{0,2},{28,30},{24,26},{2,0},{6,4},{8,10},{22... | collective-permute-start | bytes 6291464 | tf_op jit(solution)/shard_map/ppermute | solution.py:633
  281.7 55.4 %collective-permute-start.24 = (f32[2,512,512]{2,1,0:T(8,128)S(1)}, f32[2,512,512]{2,1,0:T(8,128)S(1)}, u32[]{:S(2)}, u32[]{:S(2)}) collective-permute-start(f32[2,512,512]{2,1,0:T(8,128)S(1)} %get-tuple-element.184), channel_id=1, source_target_pairs={{20,28},{16,24},{22,30},{18,26},{8,16},{12,20},{21,29},{17,25},{23... | collective-permute-start | bytes 6291464 | tf_op jit(solution)/shard_map/ppermute | solution.py:633
  287.4 13.7 %copy-start.3 = (f32[2,512,512]{2,1,0:T(8,128)}, f32[2,512,512]{2,1,0:T(8,128)S(1)}, u32[]{:S(2)}) copy-start(f32[2,512,512]{2,1,0:T(8,128)S(1)} %collective-permute-done.20.refs_3_) | copy-start | bytes 6291460
  287.4 51.0 %collective-permute-start.25 = (f32[2,512,512]{2,1,0:T(8,128)}, f32[2,512,512]{2,1,0:T(8,128)S(1)}, u32[]{:S(2)}, u32[]{:S(2)}) collective-permute-start(f32[2,512,512]{2,1,0:T(8,128)} %get-tuple-element.185), channel_id=1, source_target_pairs={{14,6},{10,2},{12,4},{8,0},{18,10},{22,14},{15,7},{11,3},{13,5},{9... | collective-permute-start | bytes 6291464 | tf_op jit(solution)/shard_map/ppermute | solution.py:633
  292.7 8.4 %copy-start.7 = (f32[2,512,512]{2,1,0:T(8,128)}, f32[2,512,512]{2,1,0:T(8,128)S(1)}, u32[]{:S(2)}) copy-start(f32[2,512,512]{2,1,0:T(8,128)S(1)} %collective-permute-done.21.refs_4_) | copy-start | bytes 6291460
  292.7 50.9 %collective-permute-start.26 = (f32[2,512,512]{2,1,0:T(8,128)}, f32[2,512,512]{2,1,0:T(8,128)}, u32[]{:S(2)}, u32[]{:S(2)}) collective-permute-start(f32[2,512,512]{2,1,0:T(8,128)} %get-tuple-element.186), channel_id=1, source_target_pairs={{6,2},{28,24},{24,28},{2,6},{4,0},{30,26},{0,4},{26,30},{20,16},{1... | collective-permute-start | bytes 6291464 | tf_op jit(solution)/shard_map/ppermute | solution.py:633
  295.9 5.2 %copy-start.10 = (f32[2,512,512]{2,1,0:T(8,128)}, f32[2,512,512]{2,1,0:T(8,128)S(1)}, u32[]{:S(2)}) copy-start(f32[2,512,512]{2,1,0:T(8,128)S(1)} %collective-permute-done.22.refs_5_) | copy-start | bytes 6291460
  295.9 49.0 %collective-permute-start.27 = (f32[2,512,512]{2,1,0:T(8,128)}, f32[2,512,512]{2,1,0:T(8,128)}, u32[]{:S(2)}, u32[]{:S(2)}) collective-permute-start(f32[2,512,512]{2,1,0:T(8,128)} %get-tuple-element.187), channel_id=1, source_target_pairs={{30,28},{0,2},{4,6},{26,24},{2,0},{6,4},{28,30},{24,26},{8,10},{31... | collective-permute-start | bytes 6291464 | tf_op jit(solution)/shard_map/ppermute | solution.py:633
  336.3 35.4 %collective-permute-start.28 = (f32[2,512,512]{2,1,0:T(8,128)S(1)}, f32[2,512,512]{2,1,0:T(8,128)S(1)}, u32[]{:S(2)}, u32[]{:S(2)}) collective-permute-start(f32[2,512,512]{2,1,0:T(8,128)S(1)} %get-tuple-element.196), channel_id=1, source_target_pairs={{16,24},{20,28},{17,25},{21,29}} | collective-permute-start | bytes 6291464 | tf_op jit(solution)/shard_map/ppermute | solution.py:633
  337.1 7.8 %copy-start.4 = (f32[2,512,512]{2,1,0:T(8,128)}, f32[2,512,512]{2,1,0:T(8,128)S(1)}, u32[]{:S(2)}) copy-start(f32[2,512,512]{2,1,0:T(8,128)S(1)} %collective-permute-done.24.refs_3_) | copy-start | bytes 6291460
  337.1 50.7 %collective-permute-start.29 = (f32[2,512,512]{2,1,0:T(8,128)}, f32[2,512,512]{2,1,0:T(8,128)S(1)}, u32[]{:S(2)}, u32[]{:S(2)}) collective-permute-start(f32[2,512,512]{2,1,0:T(8,128)} %get-tuple-element.197), channel_id=1, source_target_pairs={{14,6},{10,2},{8,0},{15,7},{11,3},{9,1}} | collective-permute-start | bytes 6291464 | tf_op jit(solution)/shard_map/ppermute | solution.py:633
  338.4 6.5 %copy-start.8 = (f32[2,512,512]{2,1,0:T(8,128)}, f32[2,512,512]{2,1,0:T(8,128)S(1)}, u32[]{:S(2)}) copy-start(f32[2,512,512]{2,1,0:T(8,128)S(1)} %collective-permute-done.25.refs_4_) | copy-start | bytes 6291460
  338.4 58.2 %collective-permute-start.30 = (f32[2,512,512]{2,1,0:T(8,128)}, f32[2,512,512]{2,1,0:T(8,128)}, u32[]{:S(2)}, u32[]{:S(2)}) collective-permute-start(f32[2,512,512]{2,1,0:T(8,128)} %get-tuple-element.198), channel_id=1, source_target_pairs={{28,24},{24,28},{6,2},{2,6},{0,4},{20,16},{29,25},{25,29},{7,3},{3... | collective-permute-start | bytes 6291464 | tf_op jit(solution)/shard_map/ppermute | solution.py:633
  343.6 54.3 %collective-permute-start.31 = (f32[2,512,512]{2,1,0:T(8,128)}, f32[2,512,512]{2,1,0:T(8,128)}, u32[]{:S(2)}, u32[]{:S(2)}) collective-permute-start(f32[2,512,512]{2,1,0:T(8,128)} %get-tuple-element.199), channel_id=1, source_target_pairs={{0,2},{30,28},{26,24},{4,6},{28,30},{24,26},{1,3},{31,29},{27,25},... | collective-permute-start | bytes 6291464 | tf_op jit(solution)/shard_map/ppermute | solution.py:633
  370.8 61.0 %collective-permute-start.32 = (f32[2,512,512]{2,1,0:T(8,128)S(1)}, f32[2,512,512]{2,1,0:T(8,128)S(1)}, u32[]{:S(2)}, u32[]{:S(2)}) collective-permute-start(f32[2,512,512]{2,1,0:T(8,128)S(1)} %get-tuple-element.203), channel_id=1, source_target_pairs={{16,24},{20,28},{17,25},{21,29}} | collective-permute-start | bytes 6291464 | tf_op jit(solution)/shard_map/ppermute | solution.py:633
  371.7 60.2 %collective-permute-start.33 = (f32[2,512,512]{2,1,0:T(8,128)}, f32[2,512,512]{2,1,0:T(8,128)S(1)}, u32[]{:S(2)}, u32[]{:S(2)}) collective-permute-start(f32[2,512,512]{2,1,0:T(8,128)} %get-tuple-element.204), channel_id=1, source_target_pairs={{10,2},{14,6},{11,3},{15,7}} | collective-permute-start | bytes 6291464 | tf_op jit(solution)/shard_map/ppermute | solution.py:633
  387.8 10.1 %copy-start.9 = (f32[2,512,512]{2,1,0:T(8,128)}, f32[2,512,512]{2,1,0:T(8,128)S(1)}, u32[]{:S(2)}) copy-start(f32[2,512,512]{2,1,0:T(8,128)S(1)} %collective-permute-done.29.refs_4_) | copy-start | bytes 6291460
  387.8 44.1 %collective-permute-start.34 = (f32[2,512,512]{2,1,0:T(8,128)}, f32[2,512,512]{2,1,0:T(8,128)S(1)}, u32[]{:S(2)}, u32[]{:S(2)}) collective-permute-start(f32[2,512,512]{2,1,0:T(8,128)} %get-tuple-element.205), channel_id=1, source_target_pairs={{6,2},{28,24},{7,3},{29,25}} | collective-permute-start | bytes 6291464 | tf_op jit(solution)/shard_map/ppermute | solution.py:633
  396.6 35.6 %collective-permute-start.35 = (f32[2,512,512]{2,1,0:T(8,128)}, f32[2,512,512]{2,1,0:T(8,128)}, u32[]{:S(2)}, u32[]{:S(2)}) collective-permute-start(f32[2,512,512]{2,1,0:T(8,128)} %get-tuple-element.206), channel_id=1, source_target_pairs={{4,6},{30,28},{5,7},{31,29}} | collective-permute-start | bytes 6291464 | tf_op jit(solution)/shard_map/ppermute | solution.py:633
  431.9 1.3 copy-start.11
  431.9 2.0 copy-start.12

commit v4 on v3

--- a/solution.py
+++ b/solution.py
@@ -11,7 +11,7 @@
 
 AXES = ("src", "rcv")
 FIELDS = 6
-CAP = 6
+CAP = 5
 
 
 def split_axis(n):

time: 460 us -> 449 us (0.976)
  starting transfers between devices: 105 us -> 71.7 us
  waiting for transfers between devices: 79 us -> 104 us
    ppermute x36, starting transfers between devices: 105 us -> 71.7 us  [local(): lax.ppermute(value, AXES, perms[step][way])]
    ppermute x36, waiting for transfers between devices: 79 us -> 104 us  [local(): lax.ppermute(value, AXES, perms[step][way])]
  transfers between devices with their start and end apart: 36 -> 36, of which waited for: 11 -> 22; matrix products, arithmetic and copies ran while one was open for 0% -> 0% of each run, Pallas kernels for 52% -> 54%
where the time goes in v4:
time: 449 us; the launch traced here: 448 us
  Pallas kernels  267 us (59%)
  waiting for transfers between devices  104 us (23%)
  starting transfers between devices  71.7 us (16%)
  local copies, waits for them, and re-layouts  4.97 us (1%)
    pallas_call x20, Pallas kernels, call(): pl.pallas_call(kernel, out_shape=outs, grid_spec=pltpu.PrefetchScalarGrid...  267 us
    ppermute x36, waiting for transfers between devices, local(): lax.ppermute(value, AXES, perms[step][way])  104 us
    ppermute x36, starting transfers between devices, local(): lax.ppermute(value, AXES, perms[step][way])  71.7 us
  transfers between devices with their start and end apart: 36, of which 22 were waited for; matrix products, arithmetic and copies ran while one was open for 0% of the time, Pallas kernels for 54%

profile of v4, /device:TPU:6, one launch (start us, length us, event | category | flops | bytes accessed | tf_op | source)
XLA Modules:
  0.0 448.4 jit_solution(17123395972677513599)
XLA Ops:
  0.7 3.4 copy-done
  4.1 2.0 shard_map.28
  6.1 4.0 collective-permute-start
  10.1 1.3 collective-permute-start.1
  12.5 2.0 shard_map.29
  14.5 6.3 %collective-permute-start.4 = (f32[2,512,512]{2,1,0:T(8,128)S(1)}, f32[2,512,512]{2,1,0:T(8,128)}, u32[]{:S(2)}, u32[]{:S(2)}) collective-permute-start(f32[2,512,512]{2,1,0:T(8,128)S(1)} %get-tuple-element.125), channel_id=1, source_target_pairs={{20,28},{16,24},{18,26},{22,30},{2,10},{12,20},{6,14},{8,16},{14,2... | collective-permute-start | bytes 6291464 | tf_op jit(solution)/shard_map/ppermute | solution.py:567
  20.8 35.2 %collective-permute-done.refs_2_ = f32[2,512,512]{2,1,0:T(8,128)S(1)} collective-permute-done((f32[2,512,512]{2,1,0:T(8,128)S(1)}, f32[2,512,512]{2,1,0:T(8,128)S(1)}, u32[]{:S(2)}, u32[]{:S(2)}) %collective-permute-start) | collective-permute-done | bytes 2097184 | tf_op jit(solution)/shard_map/ppermute | solution.py:567
  56.0 1.3 collective-permute-start.5
  57.3 1.8 collective-permute-done.1.refs_3_
  59.6 0.8 copy-done.14
  61.0 10.3 %shard_map.30 = (f32[13,2,512,512]{3,2,1,0:T(8,128)}, bf16[36,2,2,512,512]{4,3,2,1,0:T(8,128)(2,1)}) custom-call(s32[512]{0:T(512)S(1)} %bitcast.3, f32[1,2,512,2048]{3,2,1,0:T(8,128)} %own.3), custom_call_target="tpu_custom_call" | custom-call | bytes 25165824 | tf_op jit(solution)/shard_map/pallas_call | solution.py:532
  71.3 10.7 %shard_map.31 = (f32[13,2,512,512]{3,2,1,0:T(8,128)}, bf16[36,2,2,512,512]{4,3,2,1,0:T(8,128)(2,1)}, f32[2,512,512]{2,1,0:T(8,128)S(1)}, f32[2,512,512]{2,1,0:T(...) custom-call(s32[512]{0:T(512)S(1)} %bitcast.4, ...), custom_call_target="tpu_custom_call", output_to_operand_aliasing={{0}: (1, {}), {1}: (2, {})} | custom-call | bytes 41943040 | tf_op jit(solution)/shard_map/pallas_call | solution.py:532
  82.0 5.2 %collective-permute-start.8 = (f32[2,512,512]{2,1,0:T(8,128)S(1)}, f32[2,512,512]{2,1,0:T(8,128)S(1)}, u32[]{:S(2)}, u32[]{:S(2)}) collective-permute-start(f32[2,512,512]{2,1,0:T(8,128)S(1)} %get-tuple-element.136), channel_id=1, source_target_pairs={{16,24},{20,28},{18,26},{22,30},{2,10},{12,20},{8,16},{6,14},{10,1... | collective-permute-start | bytes 6291464 | tf_op jit(solution)/shard_map/ppermute | solution.py:633
  87.2 13.7 %collective-permute-done.4.refs_2_ = f32[2,512,512]{2,1,0:T(8,128)} collective-permute-done((f32[2,512,512]{2,1,0:T(8,128)S(1)}, f32[2,512,512]{2,1,0:T(8,128)}, u32[]{:S(2)}, u32[]{:S(2)}) %collective-permute-start.4) | collective-permute-done | bytes 2097184 | tf_op jit(solution)/shard_map/ppermute | solution.py:567
  100.9 1.3 collective-permute-start.9
  102.2 2.0 collective-permute-done.5.refs_3_
  104.7 1.8 collective-permute-done.6.refs_4_
  107.3 8.8 %shard_map.32 = (f32[13,2,512,512]{3,2,1,0:T(8,128)}, bf16[36,2,2,512,512]{4,3,2,1,0:T(8,128)(2,1)}, f32[2,512,512]{2,1,0:T(8,128)S(1)}, f32[2,512,512]{2,1,0:T(...) custom-call(s32[512]{0:T(512)S(1)} %bitcast.5, ...), custom_call_target="tpu_custom_call", output_to_operand_aliasing={{0}: (1, {}), {1}: (2, {})} | custom-call | bytes 41943040 | tf_op jit(solution)/shard_map/pallas_call | solution.py:532
  116.1 25.4 %shard_map.33.refs_2_ = f32[1,2,512,2048]{3,2,1,0:T(8,128)} custom-call(s32[512]{0:T(512)S(1)} %bitcast.6, bf16[36,2,2,512,512]{4,3,2,1,0:T(8,128)(2,1)} %get-tuple-element.130.cuts.refs_1_), custom_call_target="tpu_custom_call" | custom-call | flops 16106127360 | bytes 31457280 | tf_op jit(solution)/shard_map/pallas_call | solution.py:532
  141.5 3.9 collective-permute-start.12
  145.9 1.3 collective-permute-start.13
  147.2 2.2 collective-permute-done.9.refs_4_
  149.8 1.5 collective-permute-done.10.refs_5_
  152.6 9.4 %shard_map.34 = (f32[13,2,512,512]{3,2,1,0:T(8,128)}, bf16[36,2,2,512,512]{4,3,2,1,0:T(8,128)(2,1)}, f32[1,2,512,2048]{3,2,1,0:T(8,128)}, f32[2,512,512]{2,1,0:T...) custom-call(s32[512]{0:T(512)S(1)} %bitcast.7, ...), custom_call_target="tpu_custom_call", output_to_operand_aliasing={{0}: (1, {}), {1}: (2, {}), {2}: (3, {})} | custom-call | bytes 41943040 | tf_op jit(solution)/shard_map/pallas_call | solution.py:532
  162.0 20.8 %shard_map.35.refs_2_ = f32[1,2,512,2048]{3,2,1,0:T(8,128)} custom-call(s32[512]{0:T(512)S(1)} %bitcast.8, bf16[36,2,2,512,512]{4,3,2,1,0:T(8,128)(2,1)} %get-tuple-element.141.cuts.refs_1_, f32[1,2,512,2048]{3,2,1,0:T(8,128)} %get-tuple-element.146.refs_0_), custom_call_target="tpu_custom_call", output_to_operand_aliasing={{}: (2, {})} | custom-call | flops 16106127360 | bytes 31457280 | tf_op jit(solution)/shard_map/pallas_call | solution.py:532
  182.9 7.6 %collective-permute-start.16 = (f32[2,512,512]{2,1,0:T(8,128)S(1)}, f32[2,512,512]{2,1,0:T(8,128)S(1)}, u32[]{:S(2)}, u32[]{:S(2)}) collective-permute-start(f32[2,512,512]{2,1,0:T(8,128)S(1)} %get-tuple-element.160), channel_id=1, source_target_pairs={{20,28},{16,24},{18,26},{22,30},{6,14},{2,10},{8,16},{12,20},{4,12... | collective-permute-start | bytes 6291464 | tf_op jit(solution)/shard_map/ppermute | solution.py:633
  190.5 0.9 collective-permute-done.12.refs_3_
  191.4 1.3 collective-permute-start.17
  192.7 2.0 collective-permute-done.13.refs_4_
  194.8 2.5 collective-permute-done.14.refs_5_
  197.8 9.3 %shard_map.36 = (f32[13,2,512,512]{3,2,1,0:T(8,128)}, bf16[36,2,2,512,512]{4,3,2,1,0:T(8,128)(2,1)}, f32[1,2,512,2048]{3,2,1,0:T(8,128)}, f32[2,512,512]{2,1,0:T...) custom-call(s32[512]{0:T(512)S(1)} %bitcast.9, ...), custom_call_target="tpu_custom_call", output_to_operand_aliasing={{0}: (1, {}), {1}: (2, {}), {2}: (3, {})} | custom-call | bytes 41943040 | tf_op jit(solution)/shard_map/pallas_call | solution.py:532
  207.1 23.2 %shard_map.37.refs_2_ = f32[1,2,512,2048]{3,2,1,0:T(8,128)} custom-call(s32[512]{0:T(512)S(1)} %bitcast.10, bf16[36,2,2,512,512]{4,3,2,1,0:T(8,128)(2,1)} %get-tuple-element.153.cuts.refs_1_, f32[1,2,512,2048]{3,2,1,0:T(8,128)} %get-tuple-element.158.refs_0_), custom_call_target="tpu_custom_call", output_to_operand_aliasing={{}: (2, {})} | custom-call | flops 16106127360 | bytes 31457280 | tf_op jit(solution)/shard_map/pallas_call | solution.py:532
  230.3 7.1 %collective-permute-start.20 = (f32[2,512,512]{2,1,0:T(8,128)S(1)}, f32[2,512,512]{2,1,0:T(8,128)S(1)}, u32[]{:S(2)}, u32[]{:S(2)}) collective-permute-start(f32[2,512,512]{2,1,0:T(8,128)S(1)} %get-tuple-element.172), channel_id=1, source_target_pairs={{16,24},{20,28},{18,26},{22,30},{2,10},{6,14},{8,16},{12,20},{0,8}... | collective-permute-start | bytes 6291464 | tf_op jit(solution)/shard_map/ppermute | solution.py:633
  237.5 1.3 collective-permute-start.21
  238.8 1.1 collective-permute-done.17.refs_4_
  239.8 3.8 collective-permute-start.22
  243.6 3.1 collective-permute-start.23
  246.8 8.7 %shard_map.38 = (f32[13,2,512,512]{3,2,1,0:T(8,128)}, bf16[36,2,2,512,512]{4,3,2,1,0:T(8,128)(2,1)}, f32[1,2,512,2048]{3,2,1,0:T(8,128)}, f32[2,512,512]{2,1,0:T...) custom-call(s32[512]{0:T(512)S(1)} %bitcast.11, ...), custom_call_target="tpu_custom_call", output_to_operand_aliasing={{0}: (1, {}), {1}: (2, {}), {2}: (3, {})} | custom-call | bytes 41943040 | tf_op jit(solution)/shard_map/pallas_call | solution.py:532
  255.5 16.7 %shard_map.39.refs_2_ = f32[1,2,512,2048]{3,2,1,0:T(8,128)} custom-call(s32[512]{0:T(512)S(1)} %bitcast.12, bf16[36,2,2,512,512]{4,3,2,1,0:T(8,128)(2,1)} %get-tuple-element.165.cuts.refs_1_, f32[1,2,512,2048]{3,2,1,0:T(8,128)} %get-tuple-element.170.refs_0_), custom_call_target="tpu_custom_call", output_to_operand_aliasing={{}: (2, {})} | custom-call | flops 16106127360 | bytes 31457280 | tf_op jit(solution)/shard_map/pallas_call | solution.py:532
  272.3 0.8 collective-permute-start.24
  273.1 6.5 %collective-permute-done.20.refs_3_ = f32[2,512,512]{2,1,0:T(8,128)S(1)} collective-permute-done((f32[2,512,512]{2,1,0:T(8,128)S(1)}, f32[2,512,512]{2,1,0:T(8,128)S(1)}, u32[]{:S(2)}, u32[]{:S(2)}) %collective-permute-start.20) | collective-permute-done | bytes 2097184 | tf_op jit(solution)/shard_map/ppermute | solution.py:633
  279.6 1.3 collective-permute-start.25
  280.8 5.8 %collective-permute-done.21.refs_4_ = f32[2,512,512]{2,1,0:T(8,128)S(1)} collective-permute-done((f32[2,512,512]{2,1,0:T(8,128)}, f32[2,512,512]{2,1,0:T(8,128)S(1)}, u32[]{:S(2)}, u32[]{:S(2)}) %collective-permute-start.21) | collective-permute-done | bytes 2097184 | tf_op jit(solution)/shard_map/ppermute | solution.py:633
  286.7 1.9 collective-permute-start.26
  288.6 2.5 collective-permute-start.27
  291.1 9.2 %shard_map.40 = (f32[13,2,512,512]{3,2,1,0:T(8,128)}, bf16[36,2,2,512,512]{4,3,2,1,0:T(8,128)(2,1)}, f32[1,2,512,2048]{3,2,1,0:T(8,128)}, f32[2,512,512]{2,1,0:T...) custom-call(s32[512]{0:T(512)S(1)} %bitcast.13, ...), custom_call_target="tpu_custom_call", output_to_operand_aliasing={{0}: (1, {}), {1}: (2, {}), {2}: (3, {})} | custom-call | bytes 41943040 | tf_op jit(solution)/shard_map/pallas_call | solution.py:532
  300.3 25.9 %shard_map.41.refs_2_ = f32[1,2,512,2048]{3,2,1,0:T(8,128)} custom-call(s32[512]{0:T(512)S(1)} %bitcast.14, bf16[36,2,2,512,512]{4,3,2,1,0:T(8,128)(2,1)} %get-tuple-element.177.cuts.refs_1_, f32[1,2,512,2048]{3,2,1,0:T(8,128)} %get-tuple-element.182.refs_0_), custom_call_target="tpu_custom_call", output_to_operand_aliasing={{}: (2, {})} | custom-call | flops 16106127360 | bytes 31457280 | tf_op jit(solution)/shard_map/pallas_call | solution.py:532
  326.3 0.8 collective-permute-start.28
  327.1 1.3 collective-permute-start.29
  328.4 3.2 collective-permute-done.25.refs_4_
  331.6 1.9 collective-permute-start.30
  333.5 1.3 collective-permute-start.31
  334.9 7.9 %shard_map.42 = (f32[13,2,512,512]{3,2,1,0:T(8,128)}, bf16[36,2,2,512,512]{4,3,2,1,0:T(8,128)(2,1)}, f32[1,2,512,2048]{3,2,1,0:T(8,128)}, f32[2,512,512]{2,1,0:T...) custom-call(s32[512]{0:T(512)S(1)} %bitcast.15, ...), custom_call_target="tpu_custom_call", output_to_operand_aliasing={{0}: (1, {}), {1}: (2, {}), {2}: (3, {})} | custom-call | bytes 41943040 | tf_op jit(solution)/shard_map/pallas_call | solution.py:532
  342.8 18.0 %shard_map.43.refs_2_ = f32[1,2,512,2048]{3,2,1,0:T(8,128)} custom-call(s32[512]{0:T(512)S(1)} %bitcast.16, bf16[36,2,2,512,512]{4,3,2,1,0:T(8,128)(2,1)} %get-tuple-element.189.cuts.refs_1_, f32[1,2,512,2048]{3,2,1,0:T(8,128)} %get-tuple-element.194.refs_0_), custom_call_target="tpu_custom_call", output_to_operand_aliasing={{}: (2, {})} | custom-call | flops 16106127360 | bytes 31457280 | tf_op jit(solution)/shard_map/pallas_call | solution.py:532
  361.5 1.3 collective-permute-start.33
  362.8 14.9 %collective-permute-done.29.refs_4_ = f32[2,512,512]{2,1,0:T(8,128)S(1)} collective-permute-done((f32[2,512,512]{2,1,0:T(8,128)}, f32[2,512,512]{2,1,0:T(8,128)S(1)}, u32[]{:S(2)}, u32[]{:S(2)}) %collective-permute-start.29) | collective-permute-done | bytes 2097184 | tf_op jit(solution)/shard_map/ppermute | solution.py:633
  377.8 3.2 collective-permute-start.34
  381.0 1.3 collective-permute-start.35
  382.3 9.2 %shard_map.44 = (f32[13,2,512,512]{3,2,1,0:T(8,128)}, bf16[36,2,2,512,512]{4,3,2,1,0:T(8,128)(2,1)}, f32[1,2,512,2048]{3,2,1,0:T(8,128)}) custom-call(s32[512]{0:T(512)S(1)} %bitcast.17, f32[13,2,512,512]{3,2,1,0:T(8,128)} %get-tuple-element.188.refs_0_, ...), custom_call_target="tpu_custom_call", output_to_operand_aliasing={{0}: (1, {}), {1}: (2, {}), {2}: (3, {})} | custom-call | bytes 25165824 | tf_op jit(solution)/shard_map/pallas_call | solution.py:532
  391.5 24.7 %shard_map.45.refs_2_ = f32[1,2,512,2048]{3,2,1,0:T(8,128)} custom-call(s32[512]{0:T(512)S(1)} %bitcast.18, bf16[36,2,2,512,512]{4,3,2,1,0:T(8,128)(2,1)} %get-tuple-element.201.cuts.refs_1_, f32[1,2,512,2048]{3,2,1,0:T(8,128)} %get-tuple-element.202.refs_0_), custom_call_target="tpu_custom_call", output_to_operand_aliasing={{}: (2, {})} | custom-call | flops 16106127360 | bytes 31457280 | tf_op jit(solution)/shard_map/pallas_call | solution.py:532
  416.2 2.7 collective-permute-done.33.refs_4_
  419.1 4.1 collective-permute-done.35.refs_6_
  423.2 7.0 %shard_map.46 = (f32[13,2,512,512]{3,2,1,0:T(8,128)}, bf16[36,2,2,512,512]{4,3,2,1,0:T(8,128)(2,1)}, f32[1,2,512,2048]{3,2,1,0:T(8,128)}) custom-call(s32[512]{0:T(512)S(1)} %bitcast.19, f32[13,2,512,512]{3,2,1,0:T(8,128)} %get-tuple-element.200.refs_0_, ...), custom_call_target="tpu_custom_call", output_to_operand_aliasing={{0}: (1, {}), {1}: (2, {}), {2}: (3, {})} | custom-call | bytes 25165824 | tf_op jit(solution)/shard_map/pallas_call | solution.py:532
  430.2 18.0 %shard_map.47 = f32[1,2,512,2048]{3,2,1,0:T(8,128)} custom-call(s32[512]{0:T(512)S(1)} %bitcast.20, bf16[36,2,2,512,512]{4,3,2,1,0:T(8,128)(2,1)} %get-tuple-element.207.cuts, f32[1,2,512,2048]{3,2,1,0:T(8,128)} %get-tuple-element.208.refs_0_), custom_call_target="tpu_custom_call", output_to_operand_aliasing={{}: (2, {})} | custom-call | flops 9663676416 | bytes 18874368 | tf_op jit(solution)/shard_map/pallas_call | solution.py:532
  (59 shorter events, 8.0 us)
Async XLA Ops:
  0.7 3.4 copy-start
  6.1 49.9 %collective-permute-start = (f32[2,512,512]{2,1,0:T(8,128)S(1)}, f32[2,512,512]{2,1,0:T(8,128)S(1)}, u32[]{:S(2)}, u32[]{:S(2)}) collective-permute-start(f32[2,512,512]{2,1,0:T(8,128)S(1)} %get-tuple-element.119), channel_id=1, source_target_pairs={{20,28},{16,24},{18,26},{22,30},{2,10},{12,20},{8,16},{6,14},{14,2... | collective-permute-start | bytes 6291464 | tf_op jit(solution)/shard_map/ppermute | solution.py:567
  10.1 49.0 %collective-permute-start.1 = (f32[2,512,512]{2,1,0:T(8,128)S(1)}, f32[2,512,512]{2,1,0:T(8,128)S(1)}, u32[]{:S(2)}, u32[]{:S(2)}) collective-permute-start(f32[2,512,512]{2,1,0:T(8,128)S(1)} %get-tuple-element.120), channel_id=1, source_target_pairs={{10,2},{14,6},{12,4},{8,0},{24,16},{18,10},{22,14},{28,20},{16,8},... | collective-permute-start | bytes 6291464 | tf_op jit(solution)/shard_map/ppermute | solution.py:567
  11.4 48.2 %collective-permute-start.2 = (f32[2,512,512]{2,1,0:T(8,128)S(1)}, f32[2,512,512]{2,1,0:T(8,128)}, u32[]{:S(2)}, u32[]{:S(2)}) collective-permute-start(f32[2,512,512]{2,1,0:T(8,128)S(1)} %get-tuple-element.121), channel_id=1, source_target_pairs={{6,2},{28,24},{2,6},{24,28},{30,26},{0,4},{26,30},{4,0},{16,20},{2... | collective-permute-start | bytes 6291464 | tf_op jit(solution)/shard_map/ppermute | solution.py:567
  12.0 59.3 %collective-permute-start.3 = (f32[2,512,512]{2,1,0:T(8,128)S(1)}, f32[2,512,512]{2,1,0:T(8,128)}, u32[]{:S(2)}, u32[]{:S(2)}) collective-permute-start(f32[2,512,512]{2,1,0:T(8,128)S(1)} %get-tuple-element.122), channel_id=1, source_target_pairs={{0,2},{4,6},{30,28},{26,24},{28,30},{2,0},{24,26},{6,4},{8,10},{18... | collective-permute-start | bytes 6291464 | tf_op jit(solution)/shard_map/ppermute | solution.py:567
  14.5 86.5 %collective-permute-start.4 = (f32[2,512,512]{2,1,0:T(8,128)S(1)}, f32[2,512,512]{2,1,0:T(8,128)}, u32[]{:S(2)}, u32[]{:S(2)}) collective-permute-start(f32[2,512,512]{2,1,0:T(8,128)S(1)} %get-tuple-element.125), channel_id=1, source_target_pairs={{20,28},{16,24},{18,26},{22,30},{2,10},{12,20},{6,14},{8,16},{14,2... | collective-permute-start | bytes 6291464 | tf_op jit(solution)/shard_map/ppermute | solution.py:567
  56.0 15.3 %copy-start.13 = (f32[2,512,512]{2,1,0:T(8,128)}, f32[2,512,512]{2,1,0:T(8,128)S(1)}, u32[]{:S(2)}) copy-start(f32[2,512,512]{2,1,0:T(8,128)S(1)} %collective-permute-done.refs_2_) | copy-start | bytes 6291460
  56.0 48.2 %collective-permute-start.5 = (f32[2,512,512]{2,1,0:T(8,128)S(1)}, f32[2,512,512]{2,1,0:T(8,128)}, u32[]{:S(2)}, u32[]{:S(2)}) collective-permute-start(f32[2,512,512]{2,1,0:T(8,128)S(1)} %get-tuple-element.126), channel_id=1, source_target_pairs={{14,6},{10,2},{8,0},{12,4},{28,20},{24,16},{22,14},{18,10},{16,8},... | collective-permute-start | bytes 6291464 | tf_op jit(solution)/shard_map/ppermute | solution.py:567
  59.1 1.3 copy-start.14
  59.1 47.4 %collective-permute-start.6 = (f32[2,512,512]{2,1,0:T(8,128)S(1)}, f32[2,512,512]{2,1,0:T(8,128)}, u32[]{:S(2)}, u32[]{:S(2)}) collective-permute-start(f32[2,512,512]{2,1,0:T(8,128)S(1)} %get-tuple-element.127), channel_id=1, source_target_pairs={{24,28},{2,6},{28,24},{6,2},{26,30},{0,4},{30,26},{4,0},{10,14},{1... | collective-permute-start | bytes 6291464 | tf_op jit(solution)/shard_map/ppermute | solution.py:567
  60.4 46.9 %collective-permute-start.7 = (f32[2,512,512]{2,1,0:T(8,128)S(1)}, f32[2,512,512]{2,1,0:T(8,128)}, u32[]{:S(2)}, u32[]{:S(2)}) collective-permute-start(f32[2,512,512]{2,1,0:T(8,128)S(1)} %get-tuple-element.128), channel_id=1, source_target_pairs={{26,24},{30,28},{4,6},{0,2},{24,26},{2,0},{28,30},{6,4},{12,14},{8... | collective-permute-start | bytes 6291464 | tf_op jit(solution)/shard_map/ppermute | solution.py:567
  82.0 63.9 %collective-permute-start.8 = (f32[2,512,512]{2,1,0:T(8,128)S(1)}, f32[2,512,512]{2,1,0:T(8,128)S(1)}, u32[]{:S(2)}, u32[]{:S(2)}) collective-permute-start(f32[2,512,512]{2,1,0:T(8,128)S(1)} %get-tuple-element.136), channel_id=1, source_target_pairs={{16,24},{20,28},{18,26},{22,30},{2,10},{12,20},{8,16},{6,14},{10,1... | collective-permute-start | bytes 6291464 | tf_op jit(solution)/shard_map/ppermute | solution.py:633
  100.9 48.4 %collective-permute-start.9 = (f32[2,512,512]{2,1,0:T(8,128)}, f32[2,512,512]{2,1,0:T(8,128)}, u32[]{:S(2)}, u32[]{:S(2)}) collective-permute-start(f32[2,512,512]{2,1,0:T(8,128)} %get-tuple-element.137), channel_id=1, source_target_pairs={{14,6},{10,2},{8,0},{12,4},{22,14},{28,20},{18,10},{24,16},{20,12}... | collective-permute-start | bytes 6291464 | tf_op jit(solution)/shard_map/ppermute | solution.py:633
  104.2 47.2 %collective-permute-start.10 = (f32[2,512,512]{2,1,0:T(8,128)}, f32[2,512,512]{2,1,0:T(8,128)}, u32[]{:S(2)}, u32[]{:S(2)}) collective-permute-start(f32[2,512,512]{2,1,0:T(8,128)} %get-tuple-element.138), channel_id=1, source_target_pairs={{6,2},{28,24},{2,6},{24,28},{26,30},{4,0},{30,26},{0,4},{10,14},{1... | collective-permute-start | bytes 6291464 | tf_op jit(solution)/shard_map/ppermute | solution.py:633
  106.5 46.1 %collective-permute-start.11 = (f32[2,512,512]{2,1,0:T(8,128)}, f32[2,512,512]{2,1,0:T(8,128)}, u32[]{:S(2)}, u32[]{:S(2)}) collective-permute-start(f32[2,512,512]{2,1,0:T(8,128)} %get-tuple-element.139), channel_id=1, source_target_pairs={{4,6},{26,24},{30,28},{0,2},{6,4},{2,0},{28,30},{24,26},{22,20},{1... | collective-permute-start | bytes 6291464 | tf_op jit(solution)/shard_map/ppermute | solution.py:633
  141.5 49.9 %collective-permute-start.12 = (f32[2,512,512]{2,1,0:T(8,128)S(1)}, f32[2,512,512]{2,1,0:T(8,128)S(1)}, u32[]{:S(2)}, u32[]{:S(2)}) collective-permute-start(f32[2,512,512]{2,1,0:T(8,128)S(1)} %get-tuple-element.148), channel_id=1, source_target_pairs={{16,24},{20,28},{18,26},{22,30},{12,20},{8,16},{6,14},{2,10},{4,12... | collective-permute-start | bytes 6291464 | tf_op jit(solution)/shard_map/ppermute | solution.py:633
  145.9 6.8 %copy-start.5 = (f32[2,512,512]{2,1,0:T(8,128)}, f32[2,512,512]{2,1,0:T(8,128)S(1)}, u32[]{:S(2)}) copy-start(f32[2,512,512]{2,1,0:T(8,128)S(1)} %collective-permute-done.8.refs_3_) | copy-start | bytes 6291460
  145.9 48.8 %collective-permute-start.13 = (f32[2,512,512]{2,1,0:T(8,128)}, f32[2,512,512]{2,1,0:T(8,128)S(1)}, u32[]{:S(2)}, u32[]{:S(2)}) collective-permute-start(f32[2,512,512]{2,1,0:T(8,128)} %get-tuple-element.149), channel_id=1, source_target_pairs={{10,2},{14,6},{12,4},{8,0},{18,10},{22,14},{24,16},{28,20},{16,8},... | collective-permute-start | bytes 6291464 | tf_op jit(solution)/shard_map/ppermute | solution.py:633
  149.3 48.0 %collective-permute-start.14 = (f32[2,512,512]{2,1,0:T(8,128)}, f32[2,512,512]{2,1,0:T(8,128)}, u32[]{:S(2)}, u32[]{:S(2)}) collective-permute-start(f32[2,512,512]{2,1,0:T(8,128)} %get-tuple-element.150), channel_id=1, source_target_pairs={{28,24},{2,6},{24,28},{6,2},{26,30},{4,0},{0,4},{30,26},{20,16},{1... | collective-permute-start | bytes 6291464 | tf_op jit(solution)/shard_map/ppermute | solution.py:633
  151.4 46.4 %collective-permute-start.15 = (f32[2,512,512]{2,1,0:T(8,128)}, f32[2,512,512]{2,1,0:T(8,128)}, u32[]{:S(2)}, u32[]{:S(2)}) collective-permute-start(f32[2,512,512]{2,1,0:T(8,128)} %get-tuple-element.151), channel_id=1, source_target_pairs={{4,6},{30,28},{0,2},{26,24},{6,4},{28,30},{2,0},{24,26},{22,20},{8... | collective-permute-start | bytes 6291464 | tf_op jit(solution)/shard_map/ppermute | solution.py:633
  182.9 54.6 %collective-permute-start.16 = (f32[2,512,512]{2,1,0:T(8,128)S(1)}, f32[2,512,512]{2,1,0:T(8,128)S(1)}, u32[]{:S(2)}, u32[]{:S(2)}) collective-permute-start(f32[2,512,512]{2,1,0:T(8,128)S(1)} %get-tuple-element.160), channel_id=1, source_target_pairs={{20,28},{16,24},{18,26},{22,30},{6,14},{2,10},{8,16},{12,20},{4,12... | collective-permute-start | bytes 6291464 | tf_op jit(solution)/shard_map/ppermute | solution.py:633
  191.4 6.4 %copy-start.1 = (f32[2,512,512]{2,1,0:T(8,128)}, f32[2,512,512]{2,1,0:T(8,128)S(1)}, u32[]{:S(2)}) copy-start(f32[2,512,512]{2,1,0:T(8,128)S(1)} %collective-permute-done.12.refs_3_) | copy-start | bytes 6291460
  191.4 48.4 %collective-permute-start.17 = (f32[2,512,512]{2,1,0:T(8,128)}, f32[2,512,512]{2,1,0:T(8,128)}, u32[]{:S(2)}, u32[]{:S(2)}) collective-permute-start(f32[2,512,512]{2,1,0:T(8,128)} %get-tuple-element.161), channel_id=1, source_target_pairs={{14,6},{10,2},{12,4},{8,0},{18,10},{24,16},{22,14},{28,20},{20,12}... | collective-permute-start | bytes 6291464 | tf_op jit(solution)/shard_map/ppermute | solution.py:633
  194.7 3.1 copy-start.6
  194.7 49.0 %collective-permute-start.18 = (f32[2,512,512]{2,1,0:T(8,128)}, f32[2,512,512]{2,1,0:T(8,128)}, u32[]{:S(2)}, u32[]{:S(2)}) collective-permute-start(f32[2,512,512]{2,1,0:T(8,128)} %get-tuple-element.162), channel_id=1, source_target_pairs={{28,24},{24,28},{6,2},{2,6},{0,4},{26,30},{30,26},{4,0},{16,20},{1... | collective-permute-start | bytes 6291464 | tf_op jit(solution)/shard_map/ppermute | solution.py:633
  197.3 49.4 %collective-permute-start.19 = (f32[2,512,512]{2,1,0:T(8,128)}, f32[2,512,512]{2,1,0:T(8,128)}, u32[]{:S(2)}, u32[]{:S(2)}) collective-permute-start(f32[2,512,512]{2,1,0:T(8,128)} %get-tuple-element.163), channel_id=1, source_target_pairs={{4,6},{0,2},{30,28},{26,24},{24,26},{28,30},{6,4},{2,0},{8,10},{12... | collective-permute-start | bytes 6291464 | tf_op jit(solution)/shard_map/ppermute | solution.py:633
  230.3 49.2 %collective-permute-start.20 = (f32[2,512,512]{2,1,0:T(8,128)S(1)}, f32[2,512,512]{2,1,0:T(8,128)S(1)}, u32[]{:S(2)}, u32[]{:S(2)}) collective-permute-start(f32[2,512,512]{2,1,0:T(8,128)S(1)} %get-tuple-element.172), channel_id=1, source_target_pairs={{16,24},{20,28},{18,26},{22,30},{2,10},{6,14},{8,16},{12,20},{0,8}... | collective-permute-start | bytes 6291464 | tf_op jit(solution)/shard_map/ppermute | solution.py:633
  237.4 9.3 %copy-start.2 = (f32[2,512,512]{2,1,0:T(8,128)}, f32[2,512,512]{2,1,0:T(8,128)S(1)}, u32[]{:S(2)}) copy-start(f32[2,512,512]{2,1,0:T(8,128)S(1)} %collective-permute-done.16.refs_3_) | copy-start | bytes 6291460
  237.5 49.2 %collective-permute-start.21 = (f32[2,512,512]{2,1,0:T(8,128)}, f32[2,512,512]{2,1,0:T(8,128)S(1)}, u32[]{:S(2)}, u32[]{:S(2)}) collective-permute-start(f32[2,512,512]{2,1,0:T(8,128)} %get-tuple-element.173), channel_id=1, source_target_pairs={{10,2},{14,6},{8,0},{12,4},{24,16},{18,10},{22,14},{28,20},{26,18}... | collective-permute-start | bytes 6291464 | tf_op jit(solution)/shard_map/ppermute | solution.py:633
  239.8 48.8 %collective-permute-start.22 = (f32[2,512,512]{2,1,0:T(8,128)}, f32[2,512,512]{2,1,0:T(8,128)S(1)}, u32[]{:S(2)}, u32[]{:S(2)}) collective-permute-start(f32[2,512,512]{2,1,0:T(8,128)} %get-tuple-element.174), channel_id=1, source_target_pairs={{28,24},{6,2},{24,28},{2,6},{4,0},{30,26},{26,30},{0,4},{16,20},{2... | collective-permute-start | bytes 6291464 | tf_op jit(solution)/shard_map/ppermute | solution.py:633
  243.6 47.5 %collective-permute-start.23 = (f32[2,512,512]{2,1,0:T(8,128)}, f32[2,512,512]{2,1,0:T(8,128)}, u32[]{:S(2)}, u32[]{:S(2)}) collective-permute-start(f32[2,512,512]{2,1,0:T(8,128)} %get-tuple-element.175), channel_id=1, source_target_pairs={{30,28},{4,6},{26,24},{0,2},{28,30},{24,26},{2,0},{6,4},{8,10},{22... | collective-permute-start | bytes 6291464 | tf_op jit(solution)/shard_map/ppermute | solution.py:633
  272.3 54.8 %collective-permute-start.24 = (f32[2,512,512]{2,1,0:T(8,128)S(1)}, f32[2,512,512]{2,1,0:T(8,128)S(1)}, u32[]{:S(2)}, u32[]{:S(2)}) collective-permute-start(f32[2,512,512]{2,1,0:T(8,128)S(1)} %get-tuple-element.184), channel_id=1, source_target_pairs={{20,28},{16,24},{22,30},{18,26},{8,16},{12,20},{21,29},{17,25},{23... | collective-permute-start | bytes 6291464 | tf_op jit(solution)/shard_map/ppermute | solution.py:633
  279.6 11.6 %copy-start.3 = (f32[2,512,512]{2,1,0:T(8,128)}, f32[2,512,512]{2,1,0:T(8,128)S(1)}, u32[]{:S(2)}) copy-start(f32[2,512,512]{2,1,0:T(8,128)S(1)} %collective-permute-done.20.refs_3_) | copy-start | bytes 6291460
  279.6 52.0 %collective-permute-start.25 = (f32[2,512,512]{2,1,0:T(8,128)}, f32[2,512,512]{2,1,0:T(8,128)S(1)}, u32[]{:S(2)}, u32[]{:S(2)}) collective-permute-start(f32[2,512,512]{2,1,0:T(8,128)} %get-tuple-element.185), channel_id=1, source_target_pairs={{14,6},{10,2},{12,4},{8,0},{18,10},{22,14},{15,7},{11,3},{13,5},{9... | collective-permute-start | bytes 6291464 | tf_op jit(solution)/shard_map/ppermute | solution.py:633
  286.7 4.5 copy-start.7
  286.7 46.9 %collective-permute-start.26 = (f32[2,512,512]{2,1,0:T(8,128)}, f32[2,512,512]{2,1,0:T(8,128)}, u32[]{:S(2)}, u32[]{:S(2)}) collective-permute-start(f32[2,512,512]{2,1,0:T(8,128)} %get-tuple-element.186), channel_id=1, source_target_pairs={{6,2},{28,24},{24,28},{2,6},{4,0},{30,26},{0,4},{26,30},{20,16},{1... | collective-permute-start | bytes 6291464 | tf_op jit(solution)/shard_map/ppermute | solution.py:633
  288.6 2.5 copy-start.10
  288.6 46.2 %collective-permute-start.27 = (f32[2,512,512]{2,1,0:T(8,128)}, f32[2,512,512]{2,1,0:T(8,128)}, u32[]{:S(2)}, u32[]{:S(2)}) collective-permute-start(f32[2,512,512]{2,1,0:T(8,128)} %get-tuple-element.187), channel_id=1, source_target_pairs={{30,28},{0,2},{4,6},{26,24},{2,0},{6,4},{28,30},{24,26},{8,10},{31... | collective-permute-start | bytes 6291464 | tf_op jit(solution)/shard_map/ppermute | solution.py:633
  326.3 35.2 %collective-permute-start.28 = (f32[2,512,512]{2,1,0:T(8,128)S(1)}, f32[2,512,512]{2,1,0:T(8,128)S(1)}, u32[]{:S(2)}, u32[]{:S(2)}) collective-permute-start(f32[2,512,512]{2,1,0:T(8,128)S(1)} %get-tuple-element.196), channel_id=1, source_target_pairs={{16,24},{20,28},{17,25},{21,29}} | collective-permute-start | bytes 6291464 | tf_op jit(solution)/shard_map/ppermute | solution.py:633
  327.1 7.7 %copy-start.4 = (f32[2,512,512]{2,1,0:T(8,128)}, f32[2,512,512]{2,1,0:T(8,128)S(1)}, u32[]{:S(2)}) copy-start(f32[2,512,512]{2,1,0:T(8,128)S(1)} %collective-permute-done.24.refs_3_) | copy-start | bytes 6291460
  327.1 50.7 %collective-permute-start.29 = (f32[2,512,512]{2,1,0:T(8,128)}, f32[2,512,512]{2,1,0:T(8,128)S(1)}, u32[]{:S(2)}, u32[]{:S(2)}) collective-permute-start(f32[2,512,512]{2,1,0:T(8,128)} %get-tuple-element.197), channel_id=1, source_target_pairs={{14,6},{10,2},{8,0},{15,7},{11,3},{9,1}} | collective-permute-start | bytes 6291464 | tf_op jit(solution)/shard_map/ppermute | solution.py:633
  331.6 3.3 copy-start.8
  331.6 49.4 %collective-permute-start.30 = (f32[2,512,512]{2,1,0:T(8,128)}, f32[2,512,512]{2,1,0:T(8,128)}, u32[]{:S(2)}, u32[]{:S(2)}) collective-permute-start(f32[2,512,512]{2,1,0:T(8,128)} %get-tuple-element.198), channel_id=1, source_target_pairs={{28,24},{24,28},{6,2},{2,6},{0,4},{20,16},{29,25},{25,29},{7,3},{3... | collective-permute-start | bytes 6291464 | tf_op jit(solution)/shard_map/ppermute | solution.py:633
  333.5 48.8 %collective-permute-start.31 = (f32[2,512,512]{2,1,0:T(8,128)}, f32[2,512,512]{2,1,0:T(8,128)}, u32[]{:S(2)}, u32[]{:S(2)}) collective-permute-start(f32[2,512,512]{2,1,0:T(8,128)} %get-tuple-element.199), channel_id=1, source_target_pairs={{0,2},{30,28},{26,24},{4,6},{28,30},{24,26},{1,3},{31,29},{27,25},... | collective-permute-start | bytes 6291464 | tf_op jit(solution)/shard_map/ppermute | solution.py:633
  360.7 55.5 %collective-permute-start.32 = (f32[2,512,512]{2,1,0:T(8,128)S(1)}, f32[2,512,512]{2,1,0:T(8,128)S(1)}, u32[]{:S(2)}, u32[]{:S(2)}) collective-permute-start(f32[2,512,512]{2,1,0:T(8,128)S(1)} %get-tuple-element.203), channel_id=1, source_target_pairs={{16,24},{20,28},{17,25},{21,29}} | collective-permute-start | bytes 6291464 | tf_op jit(solution)/shard_map/ppermute | solution.py:633
  361.5 57.3 %collective-permute-start.33 = (f32[2,512,512]{2,1,0:T(8,128)}, f32[2,512,512]{2,1,0:T(8,128)S(1)}, u32[]{:S(2)}, u32[]{:S(2)}) collective-permute-start(f32[2,512,512]{2,1,0:T(8,128)} %get-tuple-element.204), channel_id=1, source_target_pairs={{10,2},{14,6},{11,3},{15,7}} | collective-permute-start | bytes 6291464 | tf_op jit(solution)/shard_map/ppermute | solution.py:633
  377.8 4.5 %copy-start.9 = (f32[2,512,512]{2,1,0:T(8,128)}, f32[2,512,512]{2,1,0:T(8,128)S(1)}, u32[]{:S(2)}) copy-start(f32[2,512,512]{2,1,0:T(8,128)S(1)} %collective-permute-done.29.refs_4_) | copy-start | bytes 6291460
  377.8 41.3 %collective-permute-start.34 = (f32[2,512,512]{2,1,0:T(8,128)}, f32[2,512,512]{2,1,0:T(8,128)S(1)}, u32[]{:S(2)}, u32[]{:S(2)}) collective-permute-start(f32[2,512,512]{2,1,0:T(8,128)} %get-tuple-element.205), channel_id=1, source_target_pairs={{6,2},{28,24},{7,3},{29,25}} | collective-permute-start | bytes 6291464 | tf_op jit(solution)/shard_map/ppermute | solution.py:633
  381.0 42.2 %collective-permute-start.35 = (f32[2,512,512]{2,1,0:T(8,128)}, f32[2,512,512]{2,1,0:T(8,128)}, u32[]{:S(2)}, u32[]{:S(2)}) collective-permute-start(f32[2,512,512]{2,1,0:T(8,128)} %get-tuple-element.206), channel_id=1, source_target_pairs={{4,6},{30,28},{5,7},{31,29}} | collective-permute-start | bytes 6291464 | tf_op jit(solution)/shard_map/ppermute | solution.py:633
  418.9 4.3 copy-start.11
  419.1 4.1 copy-start.12
